TPU v7x, 512 devices: a whole 4x8x8 slice. The times are simulated.
512 devices in a mesh: sample: 32 (over y, x), space: 16 (over z, core).
Axes of the slice: x: 4, y: 8, z: 8, core: 2. Of those that a mesh axis runs over, the one named last changes fastest.
Arguments:
- input_field: bfloat16 [32, 64, 64, 4, 128], P('sample', None, 'space'), may hold values from -6 to 6
- out_cotangent: bfloat16 [32, 256, 16, 1, 32], P('sample', None, 'space'), may hold values from -6 to 6
- first_weight: bfloat16 [27, 64, 128], replicated, may hold values from -0.15625 to 0.15625
- second_weight: bfloat16 [27, 128, 256], replicated, may hold values from -0.109375 to 0.109375
Outputs:
- input_grad: bfloat16 [32, 64, 64, 4, 128], P('sample', None, 'space')
- first_grad: bfloat16 [27, 64, 128], replicated
- second_grad: bfloat16 [27, 128, 256], P(None, None, 'space')
All inputs are finite; a program needn't handle non-finite values.
Results may differ from a plain program's by a relative error of at most 0.008.
Values may be sent and summed in bfloat16 or wider, within the bound.
No kernel may reach another device: no remote copies, remote signals or barrier semaphores. Data moves between devices by JAX's collectives and lax.ppermute only.
A program may use at most 64 MiB of HBM per device.

v0:
```python
import math

import jax
import jax.numpy as jnp
from jax import lax
from jax.sharding import PartitionSpec as P


def shifted(value, axis, steps):
    count = lax.axis_size(axis)
    initial, last = (max(0, -steps), min(count, count - steps))
    return lax.ppermute(value, axis, [(source, source + steps) for source in range(initial, last)])


def gradient_silu(values):
    logistic = jax.nn.sigmoid(values)
    return logistic * (1.0 + values * (1.0 - logistic))


def parity_split(padded, extents):
    planes_n, rows_n, cells_n = extents
    channels = padded.shape[0]
    grid = jnp.pad(padded, ((0, 0), (0, 1), (0, 1), (0, 1)))
    grid = grid.reshape(channels, planes_n + 1, 2, rows_n + 1, 2, cells_n + 1, 2)
    return grid.transpose(2, 4, 6, 0, 1, 3, 5)


def tap_block(split, extents, offset):
    planes_n, rows_n, cells_n = extents
    slices = []
    for row_tap in range(3):
        for cell_tap in range(3):
            piece = split[offset % 2, row_tap % 2, cell_tap % 2]
            slices.append(
                piece[
                    :,
                    offset // 2 : offset // 2 + planes_n,
                    row_tap // 2 : row_tap // 2 + rows_n,
                    cell_tap // 2 : cell_tap // 2 + cells_n,
                ]
            )
    stacked = jnp.stack(slices, 0)
    return stacked.reshape(-1, planes_n * rows_n * cells_n)


def make_blocks(padded, extents):
    split = parity_split(padded, extents)
    return [tap_block(split, extents, offset) for offset in range(3)]


def apply_filters(blocks, weight):
    channels = weight.shape[1]
    grouped = weight.reshape(3, 9 * channels, weight.shape[2])
    summed = lax.dot_general(
        grouped[0], blocks[0], (((0,), (0,)), ((), ())), preferred_element_type=jnp.float32
    )
    for offset in (1, 2):
        summed = summed + lax.dot_general(
            grouped[offset],
            blocks[offset],
            (((0,), (0,)), ((), ())),
            preferred_element_type=jnp.float32,
        )
    return summed


def filter_gradient(blocks, deltas):
    products = [
        lax.dot_general(
            tap_rows, deltas, (((1,), (1,)), ((), ())), preferred_element_type=jnp.float32
        )
        for tap_rows in blocks
    ]
    stacked = jnp.stack(products, 0)
    return stacked.reshape(27, -1, deltas.shape[0])


def alternate(taps, spatial):
    leading, central, trailing = (taps[0], taps[1], taps[2])
    planes_in = central.shape[spatial]
    widths = [(0, 0)] * leading.ndim
    upper_pad = list(widths)
    upper_pad[spatial] = (0, 1)
    lower_pad = list(widths)
    lower_pad[spatial] = (1, 0)
    even_part = jnp.pad(leading, upper_pad) + jnp.pad(trailing, lower_pad)
    paired = jnp.stack(
        [lax.slice_in_dim(even_part, 0, planes_in, axis=spatial), central], spatial + 1
    )
    target = list(central.shape)
    target[spatial] = 2 * planes_in
    merged = paired.reshape(target)
    return jnp.concatenate(
        [merged, lax.slice_in_dim(even_part, planes_in, planes_in + 1, axis=spatial)], spatial
    )


def spread_back(weight, deltas, extents):
    channels, filters = (weight.shape[1], weight.shape[2])
    flat_weight = weight.reshape(27 * channels, filters)
    patches = jnp.dot(flat_weight, deltas, preferred_element_type=jnp.float32)
    spread = patches.reshape((3, 3, 3, channels) + tuple(extents))
    spread = alternate(spread, 3)
    spread = alternate(spread, 3)
    spread = alternate(spread, 3)
    return spread


def shards(input_field, out_cotangent, first_weight, second_weight):
    volume = input_field[0]
    chan_in, planes, height, length = volume.shape
    chan_mid = first_weight.shape[2]
    chan_out = second_weight.shape[2]
    groups = lax.axis_size("space")
    samples_n = lax.axis_size("sample")
    first_ext = (planes // 2, height // 2, length // 2)
    second_ext = (planes // 4, height // 4, length // 4)
    lower_rim = shifted(volume[:, planes - 1 :], "space", 1)
    padded = jnp.pad(jnp.concatenate([lower_rim, volume], 1), ((0, 0), (0, 0), (1, 0), (1, 0)))
    first_blocks = make_blocks(padded, first_ext)
    first_pre = apply_filters(first_blocks, first_weight)
    hidden = jax.nn.silu(first_pre).astype(jnp.bfloat16).reshape((chan_mid,) + first_ext)
    cotangent = out_cotangent[0]
    gathered = lax.all_gather(hidden, "space", axis=1, tiled=True)
    gathered_pad = jnp.pad(gathered, ((0, 0), (1, 0), (1, 0), (1, 0)))
    gathered_ext = (gathered.shape[1] // 2, height // 4, length // 4)
    gathered_blocks = make_blocks(gathered_pad, gathered_ext)
    per_group = chan_out // groups
    own_weight = lax.dynamic_slice_in_dim(
        second_weight, lax.axis_index("space") * per_group, per_group, 2
    )
    own_pre = apply_filters(gathered_blocks, own_weight)
    own_cotangent = lax.all_to_all(
        cotangent, "space", split_axis=0, concat_axis=1, tiled=True
    ).reshape(per_group, -1)
    own_delta = (own_cotangent.astype(jnp.float32) * gradient_silu(own_pre)).astype(jnp.bfloat16)
    second_part = filter_gradient(gathered_blocks, own_delta)
    second_delta = lax.all_to_all(
        own_delta.reshape((per_group,) + gathered_ext),
        "space",
        split_axis=1,
        concat_axis=0,
        tiled=True,
    ).reshape(chan_out, -1)
    second_total = lax.psum(second_part, "sample")
    grad_pad = spread_back(second_weight, second_delta, second_ext)
    returned = shifted(grad_pad[:, :1, 1:, 1:], "space", -1)
    interior = grad_pad[:, 1:, 1:, 1:]
    hidden_grad = jnp.concatenate([interior[:, :-1], interior[:, -1:] + returned], 1)
    first_delta = (hidden_grad.reshape(chan_mid, -1) * gradient_silu(first_pre)).astype(
        jnp.bfloat16
    )
    first_part = filter_gradient(first_blocks, first_delta)
    first_total = lax.psum(first_part, ("sample", "space"))
    input_pad = spread_back(first_weight, first_delta, first_ext)
    input_back = shifted(input_pad[:, :1, 1:, 1:].astype(jnp.bfloat16), "space", -1).astype(
        jnp.float32
    )
    input_inner = input_pad[:, 1:, 1:, 1:]
    volume_grad = jnp.concatenate([input_inner[:, :-1], input_inner[:, -1:] + input_back], 1)
    first_scale = 1.0 / math.sqrt(samples_n * groups * first_ext[0] * first_ext[1] * first_ext[2])
    second_scale = 1.0 / math.sqrt(
        samples_n * groups * second_ext[0] * second_ext[1] * second_ext[2]
    )
    input_grad = volume_grad.astype(jnp.bfloat16)[None]
    return (
        input_grad,
        (first_total * first_scale).astype(jnp.bfloat16),
        (second_total * second_scale).astype(jnp.bfloat16),
    )


def solution(mesh):
    placed = (
        P("sample", None, "space", None, None),
        P("sample", None, "space", None, None),
        P(),
        P(),
    )
    return jax.shard_map(
        shards,
        mesh=mesh,
        in_specs=placed,
        out_specs=(P("sample", None, "space", None, None), P(), P(None, None, "space")),
        check_vma=False,
    )
```

profile of v0, /device:TPU:1, one launch (start us, length us, event | category | flops | bytes accessed | tf_op | source)
XLA Modules:
  0.0 558.1 jit_solution(18105045833384356062)
XLA Ops:
  7.2 0.9 slice.510
  8.1 5.4 collective-permute-start
  13.5 1.8 fusion.69
  15.3 1.7 collective-permute-done
  17.9 1.6 reshape.138
  19.6 2.4 fusion.67
  22.0 1.1 copy.637
  23.1 0.6 constant_dynamic-update-slice_fusion.26
  24.3 0.7 constant_dynamic-update-slice_fusion.25
  24.9 0.7 constant_dynamic-update-slice_fusion.24
  25.7 0.6 constant_dynamic-update-slice_fusion.23
  26.3 0.6 constant_dynamic-update-slice_fusion.22
  27.0 0.8 constant_dynamic-update-slice_fusion.21
  27.7 0.6 constant_dynamic-update-slice_fusion.20
  28.3 0.7 constant_dynamic-update-slice_fusion.19
  29.0 0.7 constant_dynamic-update-slice_fusion.18
  29.7 1.7 copy.641
  32.9 0.6 copy.646
  33.9 0.6 copy.647
  35.6 1.0 multiply_convert_fusion.2
  36.6 0.5 broadcast.46
  37.1 0.7 reduce
  37.9 0.7 reshape.162
  38.6 9.7 %all-to-all-start = ((bf16[16,2,256]{2,1,0:T(2,128)(2,1)}), bf16[16,2,256]{2,1,0:T(2,128)(2,1)S(1)}, u32[]{:S(2)}, u32[]{:S(2)}) async-start(bf16[16,2,256]{2,1,0:T(2,128)(2,1)} %reshape.162), calls=%async_computation | async-start | bytes 32768 | tf_op jit(solution)/shard_map/all_to_all | solution.py:133
  48.3 1.0 constant_dynamic-slice_fusion.1
  49.4 6.3 %all-to-all-done = bf16[16,2,256]{2,1,0:T(2,128)(2,1)S(1)} async-done(((bf16[16,2,256]{2,1,0:T(2,128)(2,1)}), bf16[16,2,256]{2,1,0:T(2,128)(2,1)S(1)}, u32[]{:S(2)}, u32[]{:S(2)}) %all-to-all-start) | async-done | bytes 16416 | tf_op jit(solution)/shard_map/all_to_all | solution.py:133
  56.0 26.5 %all-gather.2.cloned.1.call-done = bf16[128,32,2,64]{0,3,2,1:T(8,128)(2,1)} async-done(((bf16[128,2,2,64]{0,3,2,1:T(8,128)(2,1)}), bf16[128,32,2,64]{0,3,2,1:T(8,128)(2,1)}) %all-gather.2.cloned.1.call-update) | async-done | bytes 1048592 | tf_op jit(solution)/shard_map/all_gather | solution.py:124
  82.5 2.3 copy.719
  84.8 1.4 pad.117
  86.2 3.2 fusion.65
  89.8 0.6 fusion.71
  90.6 2.3 fusion.70
  92.9 0.5 fusion.72
  94.5 0.9 copy.654
  95.9 0.5 fusion.75
  96.4 0.9 fusion.74
  98.0 0.9 copy.658
  99.3 0.9 copy.659
  101.1 0.5 multiply_convert_fusion.3
  102.4 0.7 reshape.164
  103.1 4.5 all-to-all-start.1
  107.9 7.0 %all-to-all-done.1 = bf16[16,2,256]{2,1,0:T(2,128)(2,1)S(1)} async-done(((bf16[16,2,256]{2,1,0:T(2,128)(2,1)}), bf16[16,2,256]{2,1,0:T(2,128)(2,1)S(1)}, u32[]{:S(2)}, u32[]{:S(2)}) %all-to-all-start.1) | async-done | bytes 16416 | tf_op jit(solution)/shard_map/all_to_all | solution.py:138
  115.0 2.1 convolution_bitcast_fusion
  118.6 2.3 collective-permute-start.1
  121.1 0.8 reshape.159
  122.2 1.9 collective-permute-done.1
  124.3 1.0 convolution_bitcast_fusion.6
  125.3 1.0 convolution_bitcast_fusion.5
  126.7 0.7 squeeze.176
  127.6 0.7 squeeze.177
  128.7 0.7 stack_squeeze.21
  130.2 0.5 fusion.22
  131.9 1.4 pad_add_fusion
  133.5 2.4 copy.673
  135.9 1.4 copy.674
  137.7 1.9 collective-permute-start.2
  139.9 1.0 pad_maximum_fusion.5
  140.9 3.5 collective-permute-done.2
  144.5 1.0 copy.676
  145.5 124.9 %all-reduce.21.cloned.1.call-done = f32[27,128,16]{1,0,2:T(8,128)} async-done(((f32[27,128,16]{1,0,2:T(8,128)}), f32[27,128,16]{1,0,2:T(8,128)}) %all-reduce.21.cloned.1.call-update) | async-done | bytes 221200 | tf_op jit(solution)/shard_map/psum | solution.py:145
  270.4 1.0 multiply_convert_fusion.1
  271.4 0.7 copy.677
  272.1 277.4 %all-reduce.19.cloned.1.call-done = f32[27,64,128]{2,1,0:T(8,128)} async-done(((f32[27,64,128]{2,1,0:T(8,128)}), f32[27,64,128]{2,1,0:T(8,128)}) %all-reduce.19.cloned.1.call-update) | async-done | bytes 884752 | tf_op jit(solution)/shard_map/psum | solution.py:154
  549.5 2.1 multiply_convert_fusion
  (147 shorter events, 15.5 us)
Async XLA Ops:
  7.2 9.9 %copy-start.11 = (bf16[1,64,4,4,128]{4,3,2,1,0:T(4,128)(2,1)S(1)}, bf16[1,64,4,4,128]{4,3,2,1,0:T(4,128)(2,1)}, u32[]{:S(2)}) copy-start(bf16[1,64,4,4,128]{4,3,2,1,0:T(4,128)(2,1)} %param.4) | copy-start | bytes 786436
  7.2 75.3 %all-gather.2.cloned.1.call-start = ((), (), s32[]{:S(2)}) async-start(), calls=%async_computation.2 | async-start | bytes 1114112 | tf_op jit(solution)/shard_map/all_gather | solution.py:124
  8.1 8.9 %collective-permute-start = (bf16[64,1,4,128]{3,2,1,0:T(4,128)(2,1)S(1)}, bf16[64,1,4,128]{3,2,1,0:T(4,128)(2,1)S(1)}, u32[]{:S(2)}, u32[]{:S(2)}) collective-permute-start(bf16[64,1,4,128]{3,2,1,0:T(4,128)(2,1)S(1)} %slice.510), channel_id=1, source_target_pairs={{0,1},{1,2},{2,3},{3,4},{4,5},{5,6},{6,7},{7,8},{8,9},{9,10},{10,1... | collective-permute-start | bytes 196616 | tf_op jit(solution)/shard_map/ppermute | solution.py:12
  31.8 3.2 copy-start.1
  33.9 1.0 copy-start.9
  33.9 1.4 copy-start.10
  34.6 1.1 copy-start.12
  35.0 2.2 copy-start.13
  35.0 13.3 %copy-start = (bf16[27,128,256]{2,1,0:T(8,128)(2,1)S(1)}, bf16[27,128,256]{2,1,0:T(8,128)(2,1)}, u32[]{:S(2)}) copy-start(bf16[27,128,256]{2,1,0:T(8,128)(2,1)} %param.7) | copy-start | bytes 5308420
  38.6 17.0 %all-to-all-start = ((bf16[16,2,256]{2,1,0:T(2,128)(2,1)}), bf16[16,2,256]{2,1,0:T(2,128)(2,1)S(1)}, u32[]{:S(2)}, u32[]{:S(2)}) async-start(bf16[16,2,256]{2,1,0:T(2,128)(2,1)} %reshape.162), calls=%async_computation | async-start | bytes 32768 | tf_op jit(solution)/shard_map/all_to_all | solution.py:133
  99.3 1.0 copy-start.8
  103.1 11.8 %all-to-all-start.1 = ((bf16[16,2,256]{2,1,0:T(2,128)(2,1)}), bf16[16,2,256]{2,1,0:T(2,128)(2,1)S(1)}, u32[]{:S(2)}, u32[]{:S(2)}) async-start(bf16[16,2,256]{2,1,0:T(2,128)(2,1)} %reshape.164), calls=%async_computation.1 | async-start | bytes 32768 | tf_op jit(solution)/shard_map/all_to_all | solution.py:138
  107.5 162.8 %all-reduce.21.cloned.1.call-start = ((), (), s32[]{:S(2)}) async-start(), calls=%async_computation.4 | async-start | bytes 524288 | tf_op jit(solution)/shard_map/psum | solution.py:145
  118.6 5.6 %collective-permute-start.1 = (f32[128,1,2,64]{0,3,2,1:T(8,128)S(1)}, f32[128,1,2,64]{0,3,2,1:T(8,128)S(1)}, u32[]{:S(2)}, u32[]{:S(2)}) collective-permute-start(f32[128,1,2,64]{0,3,2,1:T(8,128)S(1)} %pad_maximum_fusion.15), channel_id=1, source_target_pairs={{1,0},{2,1},{3,2},{4,3},{5,4},{6,5},{7,6},{8,7},{9,8},{10,9},{11,1... | collective-permute-start | bytes 196616 | tf_op jit(solution)/shard_map/ppermute | solution.py:12
  121.9 4.3 copy-start.3
  121.9 427.5 %all-reduce.19.cloned.1.call-start = ((), (), s32[]{:S(2)}) async-start(), calls=%async_computation.3 | async-start | bytes 1769472 | tf_op jit(solution)/shard_map/psum | solution.py:154
  124.3 2.3 copy-start.4
  137.3 2.3 copy-start.2
  137.3 2.3 copy-start.5
  137.5 2.4 copy-start.6
  137.5 2.4 copy-start.7
  137.7 6.7 %collective-permute-start.2 = (bf16[64,1,4,128]{0,3,2,1:T(8,128)(2,1)S(1)}, bf16[64,1,4,128]{0,3,2,1:T(8,128)(2,1)S(1)}, u32[]{:S(2)}, u32[]{:S(2)}) collective-permute-start(bf16[64,1,4,128]{0,3,2,1:T(8,128)(2,1)S(1)} %slice.614), channel_id=1, source_target_pairs={{1,0},{2,1},{3,2},{4,3},{5,4},{6,5},{7,6},{8,7},{9,8},{10,9},{11,1... | collective-permute-start | bytes 196616 | tf_op jit(solution)/shard_map/ppermute | solution.py:12
Sparse Core Ops, SparseCore 0:
  36.7 45.7 all-gather.1
  122.0 148.2 all-reduce.20
  275.4 274.0 all-reduce.18
where the time goes:
time: 559 us; the launch traced here: 558 us
  waiting for transfers between devices  449 us (80%)
  local copies, waits for them, and re-layouts  51.6 us (9%)
  starting transfers between devices  24.1 us (4%)
  between operations  14.8 us (3%)
  other arithmetic  9.86 us (2%)
  matrix products  8.46 us (2%)
    psum x1, waiting for transfers between devices, shards(): first_total = lax.psum(first_part, ('sample', 'space'))  277 us
    psum x1, waiting for transfers between devices, shards(): second_total = lax.psum(second_part, 'sample')  125 us
    all_gather x1, waiting for transfers between devices, shards(): gathered = lax.all_gather(hidden, 'space', axis=1, tiled=True)  26.5 us
    unnamed x80, local copies, waits for them, and re-layouts  13.9 us
  transfers between devices with their start and end apart: 8, of which 8 were waited for; matrix products, arithmetic and copies ran while one was open for 4% of the time, Pallas kernels for 0%

commit v1 on v0

v1 whole, which is shorter than its diff:
```python
import math

import jax
import jax.numpy as jnp
import numpy as np
from jax import lax
from jax.experimental import pallas as pl
from jax.experimental.pallas import tpu as pltpu
from jax.sharding import PartitionSpec as P

BF = jnp.bfloat16
F32 = jnp.float32
PADDED_TAPS = 20


def shifted(value, axis, steps):
    count = lax.axis_size(axis)
    initial, last = (max(0, -steps), min(count, count - steps))
    return lax.ppermute(value, axis, [(source, source + steps) for source in range(initial, last)])


def gradient_silu(values):
    logistic = jax.nn.sigmoid(values)
    return logistic * (1.0 + values * (1.0 - logistic))


def dot(left, right):
    return jnp.dot(left, right, preferred_element_type=F32)


def dot_rows(left, right):
    return lax.dot_general(left, right, (((1,), (1,)), ((), ())), preferred_element_type=F32)


def flat(mask, rows):
    return mask.reshape(rows, -1).astype(BF)


def selections(cells, rows):
    half, quarter = cells // 2, cells // 4
    j, n, e, jj, k = np.indices((rows, cells, 3, rows, half))
    down_first = flat((j == jj) & (n == 2 * k + e - 1), rows * cells)
    j, k, e, jj, n = np.indices((rows, half, 3, rows, cells))
    up_first = flat((j == jj) & (n == 2 * k + e - 1), rows * half)
    b, e, m, j, k = np.indices((2, 3, quarter, rows, half))
    down_second = flat((j == b) & (k == 2 * m + e - 1), 6 * quarter)
    a, j, k, aa, b, e, m = np.indices((3, rows, half, 3, 2, 3, quarter))
    send_second = flat((a == aa) & (j == b) & (k == 2 * m + e - 1), 3 * rows * half)
    width = send_second.shape[1]
    send_second = np.pad(send_second, ((0, 0), (0, -width % 128)))
    i, m, ii, b, e, j, k = np.indices((2, quarter, 2, 2, 3, rows, half))
    up_second = flat((i == ii) & (j == b) & (k == 2 * m + e - 1), 2 * quarter)
    chosen = (down_first, up_first, down_second, send_second, up_second)
    return [jnp.asarray(matrix) for matrix in chosen]


def forward_kernel(
    below, own, above, flipped, second_weight, cotangent, down_first, down_second, send_second,
    pre_ref, delta_ref, payload_ref, blocks, taps,
):
    chan_in = own.shape[2]
    group = 9 * chan_in
    cells = own.shape[3]
    first = 0
    for part in (below, own, above):
        planes = part.shape[0]

        def row(r):
            return part[:, r].reshape(planes * chan_in, cells)

        for b in range(3):
            if b == 0:
                picked = dot(row(1), down_first[cells:, :])
            else:
                picked = dot(jnp.concatenate([row(b - 1), row(b + 1)], 1), down_first[...])
            picked = picked.astype(BF)
            for p in range(planes):
                for e in range(3):
                    start = (first + p) * group + (3 * b + e) * chan_in
                    blocks[start : start + chan_in, :] = picked[
                        p * chan_in : (p + 1) * chan_in, e * 128 : (e + 1) * 128
                    ]
        first += planes
    quarter = cotangent.shape[0] // 2
    hiddens = []
    for h in range(5):
        pre = dot(flipped[...], blocks[2 * h * group : (2 * h + 3) * group, :])
        if 1 <= h <= 3:
            pre_ref[h - 1] = pre
        hidden = (pre * jax.nn.sigmoid(pre)).astype(BF)
        hiddens.append(hidden)
        chan = hidden.shape[0]
        picked = dot_rows(down_second[...], hidden).astype(BF)
        for i in range(2):
            a = h - 2 * i
            if 0 <= a <= 2:
                for be in range(6):
                    taps[i * quarter : (i + 1) * quarter, (6 * a + be) * chan : (6 * a + be + 1) * chan] = (
                        picked[be * quarter : (be + 1) * quarter]
                    )
    chan = hiddens[0].shape[0]
    pre = None
    for a in range(3):
        rows = second_weight[(9 * a + 3) * chan : 9 * (a + 1) * chan, :]
        term = dot(taps[:, 6 * a * chan : 6 * (a + 1) * chan], rows)
        pre = term if pre is None else pre + term
    delta = cotangent[...].astype(F32) * gradient_silu(pre)
    delta_ref[...] = delta.T.astype(BF)
    sent = dot(jnp.concatenate(hiddens[:3], 1), send_second[...]).astype(BF)
    width = sent.shape[1]
    payload_ref[:, :width] = sent
    filters = delta.shape[1]
    for q in range(quarter // 8):
        piece = jnp.concatenate([delta[8 * q : 8 * (q + 1)]] * (chan // 8), 0)
        payload_ref[:, width + q * filters : width + (q + 1) * filters] = piece.astype(BF)


def backward_kernel(
    below, own, delta, pre_ref, first_weight, second_weight, up_first, up_second, volume_ref, grad_ref
):
    chan_in, cells = own.shape[2:]
    chan = pre_ref.shape[1]
    spread = dot(delta[...], up_second[...]).astype(BF)
    lanes = spread.shape[1] // 12
    deltas = []
    for h, pairs in enumerate((((1, 0),), ((2, 0), (0, 1)), ((1, 1),))):
        total = None
        for a, i in pairs:
            for be in range(6):
                start = (9 * a + 3 + be) * chan
                term = dot(
                    second_weight[start : start + chan, :],
                    spread[:, (6 * i + be) * lanes : (6 * i + be + 1) * lanes],
                )
                total = term if total is None else total + term
        deltas.append((total * gradient_silu(pre_ref[h])).astype(BF))
    raised = dot(jnp.concatenate(deltas, 0), up_first[...]).astype(BF)
    wide = 2 * cells
    stacks = [
        jnp.concatenate(
            [raised[h * chan : (h + 1) * chan, e * wide : (e + 1) * wide] for e in range(3)], 0
        )
        for h in range(3)
    ]

    def filters(a):
        return [
            jnp.concatenate([first_weight[9 * a + 3 * b + e] for e in range(3)], 1) for b in range(3)
        ]

    totals = {}
    for h, chosen in enumerate(((1, 2), (0, 1, 2), (0,))):
        left = jnp.concatenate(sum([filters(a) for a in chosen], []), 0)
        result = dot(left, stacks[h])
        for place, a in enumerate(chosen):
            p = 2 * h + a - 1
            for b in range(3):
                for j in range(2):
                    r = 2 * j + b - 1
                    if r < 0:
                        continue
                    start = (3 * place + b) * chan_in
                    term = result[start : start + chan_in, j * cells : (j + 1) * cells]
                    totals[p, r] = totals[p, r] + term if (p, r) in totals else term
    for (p, r), total in totals.items():
        volume_ref[p, r] = total.astype(BF)

    def plane(p, r):
        return below[below.shape[0] - 1, r] if p < 0 else own[p, r]

    blank = jnp.zeros((chan_in, cells), BF)
    lefts = []
    for a in range(3):
        for b in range(3):
            pieces = []
            for i in range(2):
                for j in range(2):
                    r = 2 * j + b - 1
                    pieces.append(blank if r < 0 else plane(2 * i + a - 1, r))
            lefts.append(jnp.concatenate(pieces, 1))
    grads = dot_rows(jnp.concatenate(lefts, 0), jnp.concatenate(stacks[:2], 1)).astype(BF)
    for ab in range(9):
        for e in range(3):
            start = (3 * ab + e) * chan_in
            grad_ref[start : start + chan_in, :] = grads[
                ab * chan_in : (ab + 1) * chan_in, e * chan : (e + 1) * chan
            ]
    grad_ref[27 * chan_in :, :] = jnp.zeros((grad_ref.shape[0] - 27 * chan_in, chan), BF)


def exchanged(parts, axis):
    return lax.all_to_all(parts, axis, split_axis=0, concat_axis=0, tiled=True)


def everywhere(value, axis):
    return exchanged(jnp.broadcast_to(value[None], (lax.axis_size(axis),) + value.shape), axis)


def call(kernel, outs, scratch, flops, moved):
    return pl.pallas_call(
        kernel,
        out_shape=outs,
        scratch_shapes=scratch,
        compiler_params=pltpu.CompilerParams(vmem_limit_bytes=40 << 20),
        cost_estimate=pl.CostEstimate(flops=flops, bytes_accessed=moved, transcendentals=0),
    )


def shards(input_field, out_cotangent, first_weight, second_weight):
    chan_in, planes, height, length = input_field.shape[1:]
    chan_mid, chan_out = second_weight.shape[1:]
    groups = lax.axis_size("space")
    samples_n = lax.axis_size("sample")
    rows, half, quarter = (height // 2, length // 2, length // 4)
    own = input_field[0].transpose(1, 2, 0, 3)
    below = shifted(own[1:], "space", 1)
    above = shifted(own, "space", -1)
    cotangent = out_cotangent[0].reshape(chan_out, quarter).T
    cotangent = jnp.concatenate([cotangent, shifted(cotangent, "space", -1)], 0)
    down_first, up_first, down_second, send_second, up_second = selections(length, rows)
    flipped = first_weight.reshape(27 * chan_in, chan_mid).T
    flat_second = second_weight.reshape(27 * chan_mid, chan_out)
    width = send_second.shape[1]
    pre, delta, payload = call(
        forward_kernel,
        (
            jax.ShapeDtypeStruct((3, chan_mid, rows * half), F32),
            jax.ShapeDtypeStruct((chan_out, 2 * quarter), BF),
            jax.ShapeDtypeStruct((chan_mid, width + quarter // 8 * chan_out), BF),
        ),
        [
            pltpu.VMEM((11 * 9 * chan_in, rows * half), BF),
            pltpu.VMEM((2 * quarter, 18 * chan_mid), BF),
        ],
        2_000_000_000,
        6_000_000,
    )(below, own, above, flipped, flat_second, cotangent, down_first, down_second, send_second)
    own_chan = chan_mid // groups
    moved = exchanged(payload.reshape(groups, own_chan, -1), "space")
    volume, first_part = call(
        backward_kernel,
        (
            jax.ShapeDtypeStruct((planes, height, chan_in, length), BF),
            jax.ShapeDtypeStruct((28 * chan_in, chan_mid), BF),
        ),
        [],
        3_000_000_000,
        6_000_000,
    )(below, own, delta, pre, first_weight, flat_second, up_first, up_second)
    input_grad = volume.transpose(2, 0, 1, 3)[None]
    first_moved = exchanged(first_part.reshape(samples_n, -1, chan_mid), "sample")
    first_chunk = jnp.sum(first_moved.astype(F32), 0).astype(BF)
    fields = moved[:, :, : 18 * quarter].reshape(groups, own_chan, 18, quarter)
    fields = fields.transpose(1, 2, 0, 3).reshape(own_chan * 18, groups * quarter)
    deltas = moved[:, :, width:].reshape(groups, 8, quarter // 8, chan_out)
    deltas = deltas.transpose(0, 2, 1, 3).reshape(groups * quarter, chan_out)
    second_part = dot(fields, deltas).astype(BF).reshape(own_chan, 18, chan_out)
    second_part = jnp.pad(second_part, ((0, 0), (0, PADDED_TAPS - 18), (0, 0)))
    second_moved = exchanged(second_part.reshape(samples_n, -1, chan_out), "sample")
    second_ext = planes // 4 * (height // 4) * quarter
    second_scale = 1.0 / math.sqrt(samples_n * groups * second_ext)
    second_chunk = (jnp.sum(second_moved.astype(F32), 0) * second_scale).astype(BF)
    per_group = chan_out // groups
    rows_n = second_chunk.shape[0]
    count = rows_n * per_group
    packed = -(-count // chan_mid)
    second_chunk = second_chunk.reshape(rows_n, groups, per_group).transpose(1, 0, 2)
    second_chunk = jnp.pad(second_chunk.reshape(groups, count), ((0, 0), (0, packed * chan_mid - count)))
    second_chunk = second_chunk.reshape(groups, packed, chan_mid)
    second_chunk = jnp.pad(second_chunk, ((0, 0), (0, -packed % 8), (0, 0)))
    size = first_chunk.shape[0]
    both = jnp.concatenate(
        [jnp.broadcast_to(first_chunk[None], (groups,) + first_chunk.shape), second_chunk], 1
    )
    both = exchanged(both, "space")
    first_ext = planes // 2 * (height // 2) * half
    first_scale = 1.0 / math.sqrt(samples_n * groups * first_ext)
    first_chunk = (jnp.sum(both[:, :size].astype(F32), 0) * first_scale).astype(BF)
    second_chunk = both[:, size : size + packed].reshape(groups * packed, chan_mid)
    final = everywhere(jnp.concatenate([first_chunk, second_chunk], 0), "sample")
    first_grad = final[:, :size].reshape(28, chan_in, chan_mid)[:27]
    second = final[:, size:].reshape(samples_n, groups, packed * chan_mid)[:, :, :count]
    second = second.reshape(samples_n, groups, rows_n, per_group).transpose(0, 2, 1, 3)
    second = second.reshape(own_chan, PADDED_TAPS, groups, per_group)[:, :18]
    second = second.transpose(1, 2, 0, 3).reshape(3, 2, 3, chan_mid, per_group)
    second_grad = jnp.pad(second, ((0, 0), (1, 0), (0, 0), (0, 0), (0, 0)))
    return input_grad, first_grad, second_grad.reshape(27, chan_mid, per_group)


def solution(mesh):
    placed = (
        P("sample", None, "space", None, None),
        P("sample", None, "space", None, None),
        P(),
        P(),
    )
    return jax.shard_map(
        shards,
        mesh=mesh,
        in_specs=placed,
        out_specs=(P("sample", None, "space", None, None), P(), P(None, None, "space")),
        check_vma=False,
    )
```

time: 559 us -> 130 us (0.23)
  waiting for transfers between devices: 449 us -> 51.2 us
  local copies, waits for them, and re-layouts: 51.6 us -> 16.9 us
  blocking collectives: 0 us -> 16.2 us
  between operations: 14.8 us -> 0.93 us
  starting transfers between devices: 24.1 us -> 37.8 us
  other arithmetic: 9.86 us -> 0.21 us
  matrix products: 8.46 us -> 0.19 us
    psum x2 -> x0, waiting for transfers between devices: 402 us -> none  [the longest x1 277 us: shards(): first_total = lax.psum(first_part, ('sample', 'space'))]
    all_to_all x2 -> x4, waiting for transfers between devices: 13.2 us -> 49.6 us  [exchanged(): return lax.all_to_all(parts, axis, split_axis=0, concat_axis=0, tiled=True)]
    all_gather x1 -> x0, waiting for transfers between devices: 26.5 us -> none  [shards(): gathered = lax.all_gather(hidden, 'space', axis=1, tiled=True)]
    all_to_all x0 -> x1, blocking collectives: none -> 16.2 us  [exchanged(): return lax.all_to_all(parts, axis, split_axis=0, concat_axis=0, tiled=True)]
    slice x24 -> x8, local copies, waits for them, and re-layouts: 18.8 us -> 3 us  [the longest x1 0.97 us: shards(): deltas = moved[:, :, width:].reshape(groups, 8, quarter // 8, chan_out)]
    another operation x19 -> x0, local copies, waits for them, and re-layouts: 10.7 us -> none  [the longest x11 6.6 us: tap_block(): stacked = jnp.stack(slices, 0)]
    all_to_all x2 -> x4, starting transfers between devices: 14.2 us -> 24.7 us  [exchanged(): return lax.all_to_all(parts, axis, split_axis=0, concat_axis=0, tiled=True)]
    dot_general x14 -> x1, matrix products: 8.46 us -> 0.19 us  [dot(): return jnp.dot(left, right, preferred_element_type=F32)]
  transfers between devices with their start and end apart: 8 -> 7, of which waited for: 8 -> 5; matrix products, arithmetic and copies ran while one was open for 4% -> 5% of each run, Pallas kernels for 0% -> 2%
where the time goes in v1:
time: 130 us; the launch traced here: 129 us
  waiting for transfers between devices  51.2 us (39%)
  starting transfers between devices  37.8 us (29%)
  local copies, waits for them, and re-layouts  16.9 us (13%)
  blocking collectives  16.2 us (12%)
  Pallas kernels  5.56 us (4%)
    all_to_all x4, waiting for transfers between devices, exchanged(): return lax.all_to_all(parts, axis, split_axis=0, concat_axis=0, tiled=True)  49.6 us
    all_to_all x4, starting transfers between devices, exchanged(): return lax.all_to_all(parts, axis, split_axis=0, concat_axis=0, tiled=True)  24.7 us
    all_to_all x1, blocking collectives, exchanged(): return lax.all_to_all(parts, axis, split_axis=0, concat_axis=0, tiled=True)  16.2 us
    ppermute x3, starting transfers between devices, shifted(): lax.ppermute(value, axis, [(source, source + steps) for source in range(i...  13.1 us
    unnamed x25, local copies, waits for them, and re-layouts  8.43 us
    pallas_call x1, Pallas kernels, shards(): call(forward_kernel, (jax.ShapeDtypeStruct((3, chan_mid, rows * half), F3...  3.12 us
  transfers between devices with their start and end apart: 7, of which 5 were waited for; matrix products, arithmetic and copies ran while one was open for 5% of the time, Pallas kernels for 2%

profile of v1, /device:TPU:1, one launch (start us, length us, event | category | flops | bytes accessed | tf_op | source)
XLA Modules:
  0.0 129.1 jit_solution(13907874738131479008)
XLA Ops:
  0.6 0.0 copy-start.6
  0.6 0.0 copy-start.9
  0.7 0.0 copy-start.1
  0.7 1.2 copy.57
  1.8 8.8 %collective-permute-start.1 = (bf16[4,4,64,128]{3,2,1,0:T(8,128)(2,1)S(1)}, bf16[4,4,64,128]{3,2,1,0:T(8,128)(2,1)S(1)}, u32[]{:S(2)}, u32[]{:S(2)}) collective-permute-start(bf16[4,4,64,128]{3,2,1,0:T(8,128)(2,1)S(1)} %bitcast.41), channel_id=1, source_target_pairs={{1,0},{2,1},{3,2},{4,3},{5,4},{6,5},{7,6},{8,7},{9,8},{10,9},{11,1... | collective-permute-start | bytes 786440 | tf_op jit(solution)/shard_map/ppermute | solution.py:19
  10.6 1.9 %collective-permute-start = (bf16[3,4,64,128]{3,2,1,0:T(8,128)(2,1)S(1)}, bf16[3,4,64,128]{3,2,1,0:T(8,128)(2,1)S(1)}, u32[]{:S(2)}, u32[]{:S(2)}) collective-permute-start(bf16[3,4,64,128]{3,2,1,0:T(8,128)(2,1)S(1)} %slice.38), channel_id=1, source_target_pairs={{0,1},{1,2},{2,3},{3,4},{4,5},{5,6},{6,7},{7,8},{8,9},{9,10},{10,1... | collective-permute-start | bytes 589832 | tf_op jit(solution)/shard_map/ppermute | solution.py:19
  12.6 2.4 %collective-permute-start.2 = (bf16[32,256]{1,0:T(8,128)(2,1)}, bf16[32,256]{1,0:T(8,128)(2,1)S(1)}, u32[]{:S(2)}, u32[]{:S(2)}) collective-permute-start(bf16[32,256]{1,0:T(8,128)(2,1)} %bitcast.59), channel_id=1, source_target_pairs={{1,0},{2,1},{3,2},{4,3},{5,4},{6,5},{7,6},{8,7},{9,8},{10,9},{11,1... | collective-permute-start | bytes 49160 | tf_op jit(solution)/shard_map/ppermute | solution.py:19
  15.0 1.2 copy.43
  16.2 1.6 %collective-permute-done.2 = bf16[32,256]{1,0:T(8,128)(2,1)S(1)} collective-permute-done((bf16[32,256]{1,0:T(8,128)(2,1)}, bf16[32,256]{1,0:T(8,128)(2,1)S(1)}, u32[]{:S(2)}, u32[]{:S(2)}) %collective-permute-start.2) | collective-permute-done | bytes 16416 | tf_op jit(solution)/shard_map/ppermute | solution.py:19
  17.8 0.0 copy-done.9
  17.8 0.0 collective-permute-done.below
  17.8 0.0 collective-permute-done.1.above
  17.9 0.0 copy-done.6
  17.9 0.0 copy-done.1
  17.9 0.0 copy-start.2
  17.9 1.0 copy-done.2
  18.9 0.0 copy-start.5
  18.9 0.9 copy-done.5
  19.8 0.0 copy-start
  19.8 3.1 %shard_map.112 = (f32[3,128,128]{2,1,0:T(8,128)S(1)}, bf16[256,64]{1,0:T(8,128)(2,1)S(1)}, bf16[128,1664]{1,0:T(8,128)(2,1)}) custom-call(bf16[3,4,64,128]{3,2,1,0:T(8,128)(2,1)S(1)} %collective-permute-done.below, bf16[4,4,64,128]{3,2,1,0:T(8,128)(2,1)S(1)} %bitcast.43, bf16[4,4,64,128]{3,2,1,0:T(8,128)(2,1)S(1)} %collective-permute-done.1.above, ...), custom_call_target="tpu_custom_call" | custom-call | flops 2000000000 | bytes 6000000 | tf_op jit(solution)/shard_map/pallas_call | solution.py:224
  23.0 0.0 copy-start.7
  23.0 0.7 copy-done.7
  23.6 6.4 %all-to-all-start.1 = ((bf16[16,8,1664]{2,1,0:T(8,128)(2,1)}), bf16[16,8,1664]{2,1,0:T(8,128)(2,1)}, u32[]{:S(2)}, u32[]{:S(2)}) async-start(bf16[16,8,1664]{2,1,0:T(8,128)(2,1)} %bitcast.12), calls=%async_computation.1 | async-start | bytes 851968 | tf_op jit(solution)/shard_map/all_to_all | solution.py:192
  30.1 0.0 copy-done
  30.1 0.0 copy-start.3
  30.1 0.9 copy-done.3
  31.0 0.0 copy-start.4
  31.0 0.9 copy-done.4
  31.9 0.0 copy-start.8
  31.9 0.9 copy-done.8
  32.9 2.4 %shard_map.113 = (bf16[4,4,64,128]{3,2,1,0:T(8,128)(2,1)S(1)}, bf16[1792,128]{1,0:T(8,128)(2,1)}) custom-call(bf16[3,4,64,128]{3,2,1,0:T(8,128)(2,1)S(1)} %collective-permute-done.below, bf16[4,4,64,128]{3,2,1,0:T(8,128)(2,1)S(1)} %bitcast.44, bf16[256,64]{1,0:T(8,128)(2,1)S(1)} %get-tuple-element.8.delta, f32[3,128,128]{2,1,0:T(8,128)S(1)} %copy-done.8, ...), custom_call_target="tpu_custom_call" | custom-call | flops 3000000000 | bytes 6000000 | tf_op jit(solution)/shard_map/pallas_call | solution.py:240
  35.3 10.1 %all-to-all-done.1 = bf16[16,8,1664]{2,1,0:T(8,128)(2,1)} async-done(((bf16[16,8,1664]{2,1,0:T(8,128)(2,1)}), bf16[16,8,1664]{2,1,0:T(8,128)(2,1)}, u32[]{:S(2)}, u32[]{:S(2)}) %all-to-all-start.1) | async-done | bytes 426016 | tf_op jit(solution)/shard_map/all_to_all | solution.py:192
  45.4 9.7 %all-to-all-start = ((bf16[32,56,128]{2,1,0:T(8,128)(2,1)}), bf16[32,56,128]{2,1,0:T(8,128)(2,1)S(1)}, u32[]{:S(2)}, u32[]{:S(2)}) async-start(bf16[32,56,128]{2,1,0:T(8,128)(2,1)} %bitcast.11), calls=%async_computation | async-start | bytes 917504 | tf_op jit(solution)/shard_map/all_to_all | solution.py:192
  55.1 0.9 slice.39
  56.0 0.4 reshape.71
  56.5 0.4 copy.44
  56.9 0.5 reshape.72
  57.4 1.0 slice.40
  58.3 0.2 convolution_convert_fusion
  58.6 0.7 reshape.76
  59.3 11.9 %all-to-all-done = bf16[32,56,128]{2,1,0:T(8,128)(2,1)S(1)} async-done(((bf16[32,56,128]{2,1,0:T(8,128)(2,1)}), bf16[32,56,128]{2,1,0:T(8,128)(2,1)S(1)}, u32[]{:S(2)}, u32[]{:S(2)}) %all-to-all-start) | async-done | bytes 458784 | tf_op jit(solution)/shard_map/all_to_all | solution.py:192
  71.2 4.7 %all-to-all-start.2 = ((bf16[32,5,256]{2,1,0:T(8,128)(2,1)}), bf16[32,5,256]{2,1,0:T(8,128)(2,1)S(1)}, u32[]{:S(2)}, u32[]{:S(2)}) async-start(bf16[32,5,256]{2,1,0:T(8,128)(2,1)} %reshape.76), calls=%async_computation.2 | async-start | bytes 262144 | tf_op jit(solution)/shard_map/all_to_all | solution.py:192
  76.0 0.1 reduce_sum.30
  76.0 9.4 %all-to-all-done.2 = bf16[32,5,256]{2,1,0:T(8,128)(2,1)S(1)} async-done(((bf16[32,5,256]{2,1,0:T(8,128)(2,1)}), bf16[32,5,256]{2,1,0:T(8,128)(2,1)S(1)}, u32[]{:S(2)}, u32[]{:S(2)}) %all-to-all-start.2) | async-done | bytes 81952 | tf_op jit(solution)/shard_map/all_to_all | solution.py:192
  85.5 0.1 convert_element_type.32
  85.6 0.1 reshape.77
  85.8 16.2 %all_to_all.25 = bf16[16,64,128]{2,1,0:T(8,128)(2,1)S(1)} all-to-all(bf16[16,64,128]{2,1,0:T(8,128)(2,1)S(1)} %fusion.1), channel_id=1, replica_groups=mesh['sample'=32,'space'=16] {'space'}, dimensions={0} | all-to-all | bytes 524288 | tf_op jit(solution)/shard_map/all_to_all | solution.py:192
  102.1 0.9 broadcast_in_dim.8
  103.0 3.9 %all-to-all-start.4 = ((bf16[32,72,128]{2,1,0:T(8,128)(2,1)}), bf16[32,72,128]{2,1,0:T(8,128)(2,1)S(1)}, u32[]{:S(2)}, u32[]{:S(2)}) async-start(bf16[32,72,128]{2,1,0:T(8,128)(2,1)} %broadcast_in_dim.8), calls=%async_computation.4 | async-start | bytes 1179648 | tf_op jit(solution)/shard_map/all_to_all | solution.py:192
  106.9 0.9 copy.51
  107.8 18.2 %all-to-all-done.4 = bf16[32,72,128]{2,1,0:T(8,128)(2,1)S(1)} async-done(((bf16[32,72,128]{2,1,0:T(8,128)(2,1)}), bf16[32,72,128]{2,1,0:T(8,128)(2,1)S(1)}, u32[]{:S(2)}, u32[]{:S(2)}) %all-to-all-start.4) | async-done | bytes 589856 | tf_op jit(solution)/shard_map/all_to_all | solution.py:192
  126.0 0.8 slice.44
  126.8 0.2 copy.48
  127.1 0.5 copy.49
  127.6 0.1 slice_bitcast_fusion
  127.7 0.2 copy.50
  128.0 0.2 pad.19
  128.2 0.9 copy.52
  (18 shorter events, 0.3 us)
Async XLA Ops:
  0.6 17.2 %copy-start.6 = (bf16[192,128]{1,0:T(8,128)(2,1)S(1)}, bf16[192,128]{1,0:T(8,128)(2,1)}, u32[]{:S(2)}) copy-start(bf16[192,128]{1,0:T(8,128)(2,1)} %constant.22.clone.down_second) | copy-start | bytes 147460
  0.6 17.2 %copy-start.9 = (bf16[1,256,1,1,32]{1,4,3,2,0:T(8,128)(2,1)S(1)}, bf16[1,256,1,1,32]{1,4,3,2,0:T(8,128)(2,1)}, u32[]{:S(2)}) copy-start(bf16[1,256,1,1,32]{1,4,3,2,0:T(8,128)(2,1)} %param.10) | copy-start | bytes 49156
  0.7 17.2 %copy-start.1 = (bf16[27,128,256]{2,1,0:T(8,128)(2,1)S(1)}, bf16[27,128,256]{2,1,0:T(8,128)(2,1)}, u32[]{:S(2)}) copy-start(bf16[27,128,256]{2,1,0:T(8,128)(2,1)} %param.12) | copy-start | bytes 5308420
  1.8 16.0 %collective-permute-start.1 = (bf16[4,4,64,128]{3,2,1,0:T(8,128)(2,1)S(1)}, bf16[4,4,64,128]{3,2,1,0:T(8,128)(2,1)S(1)}, u32[]{:S(2)}, u32[]{:S(2)}) collective-permute-start(bf16[4,4,64,128]{3,2,1,0:T(8,128)(2,1)S(1)} %bitcast.41), channel_id=1, source_target_pairs={{1,0},{2,1},{3,2},{4,3},{5,4},{6,5},{7,6},{8,7},{9,8},{10,9},{11,1... | collective-permute-start | bytes 786440 | tf_op jit(solution)/shard_map/ppermute | solution.py:19
  10.6 7.2 %collective-permute-start = (bf16[3,4,64,128]{3,2,1,0:T(8,128)(2,1)S(1)}, bf16[3,4,64,128]{3,2,1,0:T(8,128)(2,1)S(1)}, u32[]{:S(2)}, u32[]{:S(2)}) collective-permute-start(bf16[3,4,64,128]{3,2,1,0:T(8,128)(2,1)S(1)} %slice.38), channel_id=1, source_target_pairs={{0,1},{1,2},{2,3},{3,4},{4,5},{5,6},{6,7},{7,8},{8,9},{9,10},{10,1... | collective-permute-start | bytes 589832 | tf_op jit(solution)/shard_map/ppermute | solution.py:19
  12.6 5.3 %collective-permute-start.2 = (bf16[32,256]{1,0:T(8,128)(2,1)}, bf16[32,256]{1,0:T(8,128)(2,1)S(1)}, u32[]{:S(2)}, u32[]{:S(2)}) collective-permute-start(bf16[32,256]{1,0:T(8,128)(2,1)} %bitcast.59), channel_id=1, source_target_pairs={{1,0},{2,1},{3,2},{4,3},{5,4},{6,5},{7,6},{8,7},{9,8},{10,9},{11,1... | collective-permute-start | bytes 49160 | tf_op jit(solution)/shard_map/ppermute | solution.py:19
  17.9 1.0 copy-start.2
  18.9 0.9 copy-start.5
  19.8 10.2 %copy-start = (bf16[27,64,128]{2,1,0:T(8,128)(2,1)S(1)}, bf16[27,64,128]{2,1,0:T(8,128)(2,1)}, u32[]{:S(2)}) copy-start(bf16[27,64,128]{2,1,0:T(8,128)(2,1)} %first_weight.1) | copy-start | bytes 1327108
  23.0 0.7 copy-start.7
  23.6 21.8 %all-to-all-start.1 = ((bf16[16,8,1664]{2,1,0:T(8,128)(2,1)}), bf16[16,8,1664]{2,1,0:T(8,128)(2,1)}, u32[]{:S(2)}, u32[]{:S(2)}) async-start(bf16[16,8,1664]{2,1,0:T(8,128)(2,1)} %bitcast.12), calls=%async_computation.1 | async-start | bytes 851968 | tf_op jit(solution)/shard_map/all_to_all | solution.py:192
  30.1 0.9 copy-start.3
  31.0 0.9 copy-start.4
  31.9 0.9 copy-start.8
  45.4 25.8 %all-to-all-start = ((bf16[32,56,128]{2,1,0:T(8,128)(2,1)}), bf16[32,56,128]{2,1,0:T(8,128)(2,1)S(1)}, u32[]{:S(2)}, u32[]{:S(2)}) async-start(bf16[32,56,128]{2,1,0:T(8,128)(2,1)} %bitcast.11), calls=%async_computation | async-start | bytes 917504 | tf_op jit(solution)/shard_map/all_to_all | solution.py:192
  71.2 14.2 %all-to-all-start.2 = ((bf16[32,5,256]{2,1,0:T(8,128)(2,1)}), bf16[32,5,256]{2,1,0:T(8,128)(2,1)S(1)}, u32[]{:S(2)}, u32[]{:S(2)}) async-start(bf16[32,5,256]{2,1,0:T(8,128)(2,1)} %reshape.76), calls=%async_computation.2 | async-start | bytes 262144 | tf_op jit(solution)/shard_map/all_to_all | solution.py:192
  103.0 23.0 %all-to-all-start.4 = ((bf16[32,72,128]{2,1,0:T(8,128)(2,1)}), bf16[32,72,128]{2,1,0:T(8,128)(2,1)S(1)}, u32[]{:S(2)}, u32[]{:S(2)}) async-start(bf16[32,72,128]{2,1,0:T(8,128)(2,1)} %broadcast_in_dim.8), calls=%async_computation.4 | async-start | bytes 1179648 | tf_op jit(solution)/shard_map/all_to_all | solution.py:192

commit v2 on v1

v2 whole, which is shorter than its diff:
```python
import math

import jax
import jax.numpy as jnp
from jax import lax
from jax.experimental import pallas as pl
from jax.experimental.pallas import tpu as pltpu
from jax.sharding import PartitionSpec as P

BF = jnp.bfloat16
F32 = jnp.float32


def shifted(value, axis, steps):
    count = lax.axis_size(axis)
    initial, last = (max(0, -steps), min(count, count - steps))
    return lax.ppermute(value, axis, [(source, source + steps) for source in range(initial, last)])


def gradient_silu(values):
    logistic = jax.nn.sigmoid(values)
    return logistic * (1.0 + values * (1.0 - logistic))


def dot(left, right):
    return jnp.dot(left, right, preferred_element_type=F32)


def dot_rows(left, right):
    return lax.dot_general(left, right, (((1,), (1,)), ((), ())), preferred_element_type=F32)


def picker(rows, columns, test):
    r = lax.broadcasted_iota(jnp.int32, (rows, columns), 0)
    c = lax.broadcasted_iota(jnp.int32, (rows, columns), 1)
    return jnp.where(test(r, c), 1.0, 0.0).astype(BF)


def down_first_test(r, c):
    return ((r >> 7) == ((c >> 6) & 1)) & ((r & 127) == 2 * (c & 63) + (c >> 7) - 1)


def up_first_test(r, c):
    return ((r >> 6) == ((c >> 7) & 1)) & ((c & 127) == 2 * (r & 63) + (c >> 8) - 1)


def down_second_test(r, c):
    be = r >> 5
    b = jnp.where(be >= 3, 1, 0)
    return (b == (c >> 6)) & ((c & 63) == 2 * (r & 31) + be - 3 * b - 1)


def up_second_test(r, c):
    ibe = c >> 7
    i = jnp.where(ibe >= 6, 1, 0)
    be = ibe - 6 * i
    b = jnp.where(be >= 3, 1, 0)
    return ((r >> 5) == i) & (b == ((c >> 6) & 1)) & ((c & 63) == 2 * (r & 31) + be - 3 * b - 1)


def reorder_test(r, c):
    return ((r >> 4) == (c & 15)) & ((r & 15) == (c >> 4))


def forward_kernel(
    parity, below, own, above, flipped, second_weight, pre_ref, delta_ref, kept_ref, sent_ref, blocks, taps
):
    chan_in, cells = 64, 128
    group = 9 * chan_in
    down_first = picker(2 * cells, 3 * 128, down_first_test)
    down_second = picker(192, 128, down_second_test)
    first = 0
    for part, planes in ((below, 3), (own, 4), (above, 4)):

        def row(r):
            lines = [
                part[(4 * p + r) * chan_in : (4 * p + r + 1) * chan_in, :] for p in range(planes)
            ]
            return jnp.concatenate(lines, 0)

        for b in range(3):
            if b == 0:
                picked = dot(row(1), down_first[cells:, :])
            else:
                picked = dot(jnp.concatenate([row(b - 1), row(b + 1)], 1), down_first)
            picked = picked.astype(BF)
            for p in range(planes):
                for e in range(3):
                    start = (first + p) * group + (3 * b + e) * chan_in
                    blocks[start : start + chan_in, :] = picked[
                        p * chan_in : (p + 1) * chan_in, e * 128 : (e + 1) * 128
                    ]
        first += planes
    quarter = 32
    lines = 16 * chan_in
    cotangent = jnp.concatenate(
        [
            jnp.concatenate([part[lines : lines + 32, :], part[lines + 32 : lines + 64, :]], 1)
            for part in (own, above)
        ],
        0,
    )
    for h in range(5):
        pre = dot(flipped[...], blocks[2 * h * group : (2 * h + 3) * group, :])
        if 1 <= h <= 3:
            pre_ref[h - 1] = pre
        hidden = (pre * jax.nn.sigmoid(pre)).astype(BF)
        chan = hidden.shape[0]
        picked = dot_rows(down_second, hidden).astype(BF)
        for i in range(2):
            a = h - 2 * i
            if 0 <= a <= 2:
                for be in range(6):
                    taps[i * quarter : (i + 1) * quarter, (6 * a + be) * chan : (6 * a + be + 1) * chan] = (
                        picked[be * quarter : (be + 1) * quarter]
                    )
    pre = None
    for a in range(3):
        rows = second_weight[(9 * a + 3) * chan : 9 * (a + 1) * chan, :]
        term = dot(taps[:, 6 * a * chan : 6 * (a + 1) * chan], rows)
        pre = term if pre is None else pre + term
    delta = cotangent.astype(F32) * gradient_silu(pre)
    delta_ref[...] = delta.T.astype(BF)
    share = 9 * chan
    for ref, half in ((kept_ref, parity[0]), (sent_ref, 1 - parity[0])):
        start = pl.multiple_of(half * share, 128)
        ref[:, :share] = taps[:quarter, pl.ds(start, share)]
        ref[:, share:] = delta[:quarter].astype(BF)


def backward_kernel(
    below, own, delta, pre_ref, kept, got, first_weight, second_weight, volume_ref, grad_ref
):
    chan_in, cells = 64, 128
    chan = pre_ref.shape[1]
    up_first = picker(128, 768, up_first_test)
    up_second = picker(64, 1536, up_second_test)
    spread = dot(delta[...], up_second).astype(BF)
    lanes = spread.shape[1] // 12
    deltas = []
    for h, pairs in enumerate((((1, 0),), ((2, 0), (0, 1)), ((1, 1),))):
        total = None
        for a, i in pairs:
            for be in range(6):
                start = (9 * a + 3 + be) * chan
                term = dot(
                    second_weight[start : start + chan, :],
                    spread[:, (6 * i + be) * lanes : (6 * i + be + 1) * lanes],
                )
                total = term if total is None else total + term
        deltas.append((total * gradient_silu(pre_ref[h])).astype(BF))
    raised = dot(jnp.concatenate(deltas, 0), up_first).astype(BF)
    wide = 2 * cells
    stacks = [
        jnp.concatenate(
            [raised[h * chan : (h + 1) * chan, e * wide : (e + 1) * wide] for e in range(3)], 0
        )
        for h in range(3)
    ]

    def filters(a):
        return [
            jnp.concatenate([first_weight[9 * a + 3 * b + e] for e in range(3)], 1) for b in range(3)
        ]

    totals = {}
    for h, chosen in enumerate(((1, 2), (0, 1, 2), (0,))):
        left = jnp.concatenate(sum([filters(a) for a in chosen], []), 0)
        result = dot(left, stacks[h])
        for place, a in enumerate(chosen):
            p = 2 * h + a - 1
            for b in range(3):
                for j in range(2):
                    r = 2 * j + b - 1
                    if r < 0:
                        continue
                    start = (3 * place + b) * chan_in
                    term = result[start : start + chan_in, j * cells : (j + 1) * cells]
                    totals[p, r] = totals[p, r] + term if (p, r) in totals else term
    for (p, r), total in totals.items():
        volume_ref[p, r] = total.astype(BF)

    def plane(p, r):
        ref, start = (below, (8 + r) * chan_in) if p < 0 else (own, (4 * p + r) * chan_in)
        return ref[start : start + chan_in, :]

    blank = jnp.zeros((chan_in, cells), BF)
    lefts = []
    for a in range(3):
        for b in range(3):
            pieces = []
            for i in range(2):
                for j in range(2):
                    r = 2 * j + b - 1
                    pieces.append(blank if r < 0 else plane(2 * i + a - 1, r))
            lefts.append(jnp.concatenate(pieces, 1))
    grads = dot_rows(jnp.concatenate(lefts, 0), jnp.concatenate(stacks[:2], 1)).astype(BF)
    chunk = 28 * chan_in // grad_ref.shape[0]
    for tap in range(28):
        if tap < 27:
            ab, e = tap // 3, tap % 3
            value = grads[ab * chan_in : (ab + 1) * chan_in, e * chan : (e + 1) * chan]
        else:
            value = jnp.zeros((chan_in, chan), BF)
        at, stop = tap * chan_in, (tap + 1) * chan_in
        while at < stop:
            m, offset = at // chunk, at % chunk
            count = min(stop - at, chunk - offset)
            begin = at - tap * chan_in
            grad_ref[m, offset : offset + count, :] = value[begin : begin + count]
            at += count
    share = 9 * chan
    both = jnp.concatenate([kept[...], got[...]], 0)
    ordered = dot(both[:, share:], picker(256, 256, reorder_test)).astype(BF)
    second = lax.dot_general(
        ordered, both[:, :share], (((0,), (0,)), ((), ())), preferred_element_type=F32
    ).astype(BF)
    second = jnp.concatenate([second, jnp.zeros((second.shape[0], chan), BF)], 1)
    per = 32 // grad_ref.shape[0]
    for piece in range(32):
        o, h = piece // 2, piece % 2
        for lane in range(5):
            start = chunk + (piece % per * 5 + lane) * 16
            grad_ref[piece // per, start : start + 16, :] = second[
                o * 16 : (o + 1) * 16, (5 * h + lane) * chan : (5 * h + lane + 1) * chan
            ]


def exchanged(parts, axis):
    return lax.all_to_all(parts, axis, split_axis=0, concat_axis=0, tiled=True)


def everywhere(value, axis):
    return exchanged(jnp.broadcast_to(value[None], (lax.axis_size(axis),) + value.shape), axis)


def call(kernel, outs, scratch, flops, moved, scalars=0, inputs=0):
    places = [pltpu.SMEM] * scalars + [pltpu.VMEM] * inputs
    return pl.pallas_call(
        kernel,
        out_shape=outs,
        in_specs=[pl.BlockSpec(memory_space=place) for place in places],
        scratch_shapes=scratch,
        compiler_params=pltpu.CompilerParams(vmem_limit_bytes=24 << 20),
        cost_estimate=pl.CostEstimate(flops=flops, bytes_accessed=moved, transcendentals=0),
    )


def shards(input_field, out_cotangent, first_weight, second_weight):
    chan_in, planes, height, length = input_field.shape[1:]
    chan_mid, chan_out = second_weight.shape[1:]
    groups = lax.axis_size("space")
    samples_n = lax.axis_size("sample")
    rows, half, quarter = (height // 2, length // 2, length // 4)
    per_group = chan_out // groups
    own = input_field[0].transpose(1, 2, 0, 3).reshape(-1, length)
    below = shifted(own[height * chan_in :], "space", 1)
    cotangent = out_cotangent[0].reshape(2, chan_out // 2, quarter).transpose(0, 2, 1)
    own = jnp.concatenate([own, cotangent.reshape(2 * quarter, chan_out // 2)], 0)
    above = shifted(own, "space", -1)
    flipped = first_weight.reshape(27 * chan_in, chan_mid).T
    flat_second = second_weight.reshape(27 * chan_mid, chan_out)
    share = 9 * chan_mid
    parity = (lax.axis_index("space") % 2).astype(jnp.int32).reshape(1)
    pre, delta, kept, sent = call(
        forward_kernel,
        (
            jax.ShapeDtypeStruct((3, chan_mid, rows * half), F32),
            jax.ShapeDtypeStruct((chan_out, 2 * quarter), BF),
            jax.ShapeDtypeStruct((quarter, share + chan_out), BF),
            jax.ShapeDtypeStruct((quarter, share + chan_out), BF),
        ),
        [
            pltpu.VMEM((11 * 9 * chan_in, rows * half), BF),
            pltpu.VMEM((2 * quarter, 18 * chan_mid), BF),
        ],
        2_000_000_000,
        6_000_000,
        1,
        5,
    )(parity, below, own, above, flipped, flat_second)
    got = lax.ppermute(sent, "space", [(i, i ^ 1) for i in range(groups)])
    size = 28 * chan_in // samples_n
    pieces = 32 // samples_n * 5
    volume, partial = call(
        backward_kernel,
        (
            jax.ShapeDtypeStruct((planes, height, chan_in, length), BF),
            jax.ShapeDtypeStruct((samples_n, size + pieces * groups, chan_mid), BF),
        ),
        [],
        3_000_000_000,
        6_000_000,
        0,
        8,
    )(below, own, delta, pre, kept, got, first_weight, flat_second)
    input_grad = volume.transpose(2, 0, 1, 3)[None]
    chunk = jnp.sum(exchanged(partial, "sample").astype(F32), 0)
    first_chunk = jnp.broadcast_to(chunk[None, :size], (groups, size, chan_mid))
    second_chunk = chunk[size:].reshape(pieces, groups, chan_mid).transpose(1, 0, 2)
    second_chunk = jnp.pad(second_chunk, ((0, 0), (0, -pieces % 8), (0, 0)))
    both = exchanged(jnp.concatenate([first_chunk, second_chunk], 1).astype(BF), "space")
    first_ext = planes // 2 * rows * half
    first_scale = 1.0 / math.sqrt(samples_n * groups * first_ext)
    second_scale = 1.0 / math.sqrt(samples_n * groups * (planes // 4) * (height // 4) * quarter)
    first_chunk = jnp.sum(both[:, :size].astype(F32), 0) * first_scale
    second_chunk = both[:, size : size + pieces].astype(F32).reshape(groups // 2, 2, pieces, chan_mid)
    second_chunk = (jnp.sum(second_chunk, 0) * second_scale).reshape(2 * pieces, chan_mid)
    second_chunk = jnp.pad(second_chunk, ((0, -2 * pieces % 8), (0, 0)))
    final = everywhere(jnp.concatenate([first_chunk, second_chunk], 0).astype(BF), "sample")
    first_grad = final[:, :size].reshape(28, chan_in, chan_mid)[:27]
    second = final[:, size : size + 2 * pieces].reshape(samples_n, 2, 32 // samples_n, 5, chan_mid)
    second = second.transpose(0, 2, 1, 3, 4).reshape(per_group, 2, 2, 5, chan_mid)
    second = second.transpose(2, 1, 3, 0, 4).reshape(2, 10, per_group, chan_mid)[:, :9]
    second = second.reshape(3, 2, 3, per_group, chan_mid)
    second = jnp.pad(second, ((0, 0), (1, 0), (0, 0), (0, 0), (0, 0)))
    second_grad = second.reshape(27, per_group, chan_mid).transpose(0, 2, 1)
    return input_grad, first_grad, second_grad


def solution(mesh):
    placed = (
        P("sample", None, "space", None, None),
        P("sample", None, "space", None, None),
        P(),
        P(),
    )
    return jax.shard_map(
        shards,
        mesh=mesh,
        in_specs=placed,
        out_specs=(P("sample", None, "space", None, None), P(), P(None, None, "space")),
        check_vma=False,
    )
```

time: 130 us -> 113 us (0.87)
  blocking collectives: 16.2 us -> 61.8 us
  waiting for transfers between devices: 51.2 us -> 22.1 us
  starting transfers between devices: 37.8 us -> 16.6 us
  local copies, waits for them, and re-layouts: 16.9 us -> 6.24 us
    all_to_all x1 -> x2, blocking collectives: 16.2 us -> 61.8 us  [exchanged(): return lax.all_to_all(parts, axis, split_axis=0, concat_axis=0, tiled=True)]
    all_to_all x4 -> x1, waiting for transfers between devices: 49.6 us -> 18.2 us  [exchanged(): return lax.all_to_all(parts, axis, split_axis=0, concat_axis=0, tiled=True)]
    all_to_all x4 -> x1, starting transfers between devices: 24.7 us -> 3.89 us  [exchanged(): return lax.all_to_all(parts, axis, split_axis=0, concat_axis=0, tiled=True)]
    unnamed x25 -> x9, local copies, waits for them, and re-layouts: 8.43 us -> 0.94 us
    ppermute x3 -> x2, starting transfers between devices: 13.1 us -> 10.8 us  [shifted(): lax.ppermute(value, axis, [(source, source + steps) for source in range(i...]
    ppermute x0 -> x1, starting transfers between devices: none -> 1.92 us  [shards(): got = lax.ppermute(sent, 'space', [(i, i ^ 1) for i in range(groups)])]
    reshape x6 -> x0, local copies, waits for them, and re-layouts: 1.77 us -> none  [the longest x1 0.69 us: shards(): second_part.reshape(samples_n, -1, chan_out)]
    slice x6 -> x8, local copies, waits for them, and re-layouts: 2.17 us -> 0.84 us  [the longest x2 0.78 us: shards(): below = shifted(own[height * chan_in:], 'space', 1)]
  transfers between devices with their start and end apart: 7 -> 4, of which waited for: 5 -> 3; matrix products, arithmetic and copies ran while one was open for 5% -> 2% of each run, Pallas kernels for 2% -> 0%
where the time goes in v2:
time: 113 us
  blocking collectives  61.8 us (55%)
  waiting for transfers between devices  22.1 us (20%)
  starting transfers between devices  16.6 us (15%)
  local copies, waits for them, and re-layouts  6.24 us (6%)
  Pallas kernels  4.59 us (4%)
    all_to_all x2, blocking collectives, exchanged(): return lax.all_to_all(parts, axis, split_axis=0, concat_axis=0, tiled=True)  61.8 us
    all_to_all x1, waiting for transfers between devices, exchanged(): return lax.all_to_all(parts, axis, split_axis=0, concat_axis=0, tiled=True)  18.2 us
    ppermute x2, starting transfers between devices, shifted(): lax.ppermute(value, axis, [(source, source + steps) for source in range(i...  10.8 us
    all_to_all x1, starting transfers between devices, exchanged(): return lax.all_to_all(parts, axis, split_axis=0, concat_axis=0, tiled=True)  3.89 us
    ppermute x2, waiting for transfers between devices, shifted(): lax.ppermute(value, axis, [(source, source + steps) for source in range(i...  2.67 us
    pallas_call x1, Pallas kernels, shards(): call(forward_kernel, (jax.ShapeDtypeStruct((3, chan_mid, rows * half), F3...  2.58 us
  transfers between devices with their start and end apart: 4, of which 3 were waited for; matrix products, arithmetic and copies ran while one was open for 2% of the time, Pallas kernels for 0%

profile of v2, /device:TPU:1, one launch (start us, length us, event | category | flops | bytes accessed | tf_op | source)
XLA Modules:
  0.0 112.5 jit_solution(15488272704617270345)
XLA Ops:
  0.6 0.0 copy-start.2
  0.6 0.0 copy-start
  0.7 0.8 reshape_squeeze.3
  1.5 1.0 copy.45
  2.5 0.0 copy-start.1
  2.5 8.9 %collective-permute-start.1 = (bf16[1088,128]{1,0:T(8,128)(2,1)S(1)}, bf16[1088,128]{1,0:T(8,128)(2,1)S(1)}, u32[]{:S(2)}, u32[]{:S(2)}) collective-permute-start(bf16[1088,128]{1,0:T(8,128)(2,1)S(1)} %pad_maximum_fusion.own), channel_id=1, source_target_pairs={{1,0},{2,1},{3,2},{4,3},{5,4},{6,5},{7,6},{8,7},{9,8},{10,9},{11,1... | collective-permute-start | bytes 835592 | tf_op jit(solution)/shard_map/ppermute | solution.py:17
  11.4 0.0 copy-done.2
  11.5 0.1 slice.41
  11.5 0.7 copy.44
  12.2 1.9 %collective-permute-start = (bf16[768,128]{1,0:T(8,128)(2,1)}, bf16[768,128]{1,0:T(8,128)(2,1)S(1)}, u32[]{:S(2)}, u32[]{:S(2)}) collective-permute-start(bf16[768,128]{1,0:T(8,128)(2,1)} %bitcast.2), channel_id=1, source_target_pairs={{0,1},{1,2},{2,3},{3,4},{4,5},{5,6},{6,7},{7,8},{8,9},{9,10},{10,1... | collective-permute-start | bytes 589832 | tf_op jit(solution)/shard_map/ppermute | solution.py:17
  14.2 0.0 copy-done
  14.2 0.2 copy.47
  14.4 2.7 %collective-permute-done.below = bf16[768,128]{1,0:T(8,128)(2,1)S(1)} collective-permute-done((bf16[768,128]{1,0:T(8,128)(2,1)}, bf16[768,128]{1,0:T(8,128)(2,1)S(1)}, u32[]{:S(2)}, u32[]{:S(2)}) %collective-permute-start) | collective-permute-done | bytes 196640 | tf_op jit(solution)/shard_map/ppermute | solution.py:17
  17.1 0.0 collective-permute-done.1.above
  17.1 0.0 copy-done.1
  17.1 2.6 %shard_map.67 = (f32[3,128,128]{2,1,0:T(8,128)S(1)}, bf16[256,64]{1,0:T(8,128)(2,1)S(1)}, bf16[32,1408]{1,0:T(8,128)(2,1)S(1)}, bf16[32,1408]{1,0:T(8,128)(2,1)S(1)}) custom-call(s32[1]{0:T(128)} %bitcast.7.parity, bf16[768,128]{1,0:T(8,128)(2,1)S(1)} %collective-permute-done.below, bf16[1088,128]{1,0:T(8,128)(2,1)S(1)} %pad_maximum_fusion.own, ...), custom_call_target="tpu_custom_call" | custom-call | flops 2000000000 | bytes 6000000 | tf_op jit(solution)/shard_map/pallas_call | solution.py:265
  19.7 1.9 %collective-permute-start.2 = (bf16[32,1408]{1,0:T(8,128)(2,1)S(1)}, bf16[32,1408]{1,0:T(8,128)(2,1)S(1)}, u32[]{:S(2)}, u32[]{:S(2)}) collective-permute-start(bf16[32,1408]{1,0:T(8,128)(2,1)S(1)} %get-tuple-element.12), channel_id=1, source_target_pairs={{0,1},{1,0},{2,3},{3,2},{4,5},{5,4},{6,7},{7,6},{8,9},{9,8},{10,11... | collective-permute-start | bytes 270344 | tf_op jit(solution)/shard_map/ppermute | solution.py:282
  21.6 1.3 %collective-permute-done.2.got = bf16[32,1408]{1,0:T(8,128)(2,1)S(1)} collective-permute-done((bf16[32,1408]{1,0:T(8,128)(2,1)S(1)}, bf16[32,1408]{1,0:T(8,128)(2,1)S(1)}, u32[]{:S(2)}, u32[]{:S(2)}) %collective-permute-start.2) | collective-permute-done | bytes 90144 | tf_op jit(solution)/shard_map/ppermute | solution.py:282
  22.8 2.0 %shard_map.68 = (bf16[4,4,64,128]{3,2,1,0:T(8,128)(2,1)S(1)}, bf16[32,136,128]{2,1,0:T(8,128)(2,1)S(1)}) custom-call(bf16[768,128]{1,0:T(8,128)(2,1)S(1)} %collective-permute-done.below, bf16[1088,128]{1,0:T(8,128)(2,1)S(1)} %pad_maximum_fusion.own, bf16[256,64]{1,0:T(8,128)(2,1)S(1)} %get-tuple-element.9.delta, ...), custom_call_target="tpu_custom_call" | custom-call | flops 3000000000 | bytes 6000000 | tf_op jit(solution)/shard_map/pallas_call | solution.py:285
  24.9 37.3 %all_to_all.15 = bf16[32,136,128]{2,1,0:T(8,128)(2,1)S(1)} all-to-all(bf16[32,136,128]{2,1,0:T(8,128)(2,1)S(1)} %get-tuple-element.14), channel_id=1, replica_groups=mesh['sample'=32,'space'=16] {'sample'}, dimensions={0} | all-to-all | bytes 2228224 | tf_op jit(solution)/shard_map/all_to_all | solution.py:230
  62.2 0.2 convert_reduce_fusion
  62.4 24.5 %all_to_all.16 = bf16[16,64,128]{2,1,0:T(8,128)(2,1)S(1)} all-to-all(bf16[16,64,128]{2,1,0:T(8,128)(2,1)S(1)} %fusion.1), channel_id=1, replica_groups=mesh['sample'=32,'space'=16] {'space'}, dimensions={0} | all-to-all | bytes 524288 | tf_op jit(solution)/shard_map/all_to_all | solution.py:230
  87.1 0.9 broadcast_in_dim.8
  88.0 3.9 %all-to-all-start.2 = ((bf16[32,72,128]{2,1,0:T(8,128)(2,1)}), bf16[32,72,128]{2,1,0:T(8,128)(2,1)S(1)}, u32[]{:S(2)}, u32[]{:S(2)}) async-start(bf16[32,72,128]{2,1,0:T(8,128)(2,1)} %broadcast_in_dim.8), calls=%async_computation.2 | async-start | bytes 1179648 | tf_op jit(solution)/shard_map/all_to_all | solution.py:230
  91.9 0.9 copy.53
  92.8 18.2 %all-to-all-done.2 = bf16[32,72,128]{2,1,0:T(8,128)(2,1)S(1)} async-done(((bf16[32,72,128]{2,1,0:T(8,128)(2,1)}), bf16[32,72,128]{2,1,0:T(8,128)(2,1)S(1)}, u32[]{:S(2)}, u32[]{:S(2)}) %all-to-all-start.2) | async-done | bytes 589856 | tf_op jit(solution)/shard_map/all_to_all | solution.py:230
  111.1 0.8 slice.47
  111.9 0.7 pad.16
  (20 shorter events, 0.3 us)
Async XLA Ops:
  0.6 10.8 %copy-start.2 = (bf16[1,64,4,4,128]{4,3,2,1,0:T(4,128)(2,1)S(1)}, bf16[1,64,4,4,128]{4,3,2,1,0:T(4,128)(2,1)}, u32[]{:S(2)}) copy-start(bf16[1,64,4,4,128]{4,3,2,1,0:T(4,128)(2,1)} %param.4) | copy-start | bytes 786436
  0.6 13.5 %copy-start = (bf16[27,64,128]{2,1,0:T(8,128)(2,1)S(1)}, bf16[27,64,128]{2,1,0:T(8,128)(2,1)}, u32[]{:S(2)}) copy-start(bf16[27,64,128]{2,1,0:T(8,128)(2,1)} %first_weight.1) | copy-start | bytes 1327108
  2.5 14.6 %copy-start.1 = (bf16[27,128,256]{2,1,0:T(8,128)(2,1)S(1)}, bf16[27,128,256]{2,1,0:T(8,128)(2,1)}, u32[]{:S(2)}) copy-start(bf16[27,128,256]{2,1,0:T(8,128)(2,1)} %param.7) | copy-start | bytes 5308420
  2.5 14.6 %collective-permute-start.1 = (bf16[1088,128]{1,0:T(8,128)(2,1)S(1)}, bf16[1088,128]{1,0:T(8,128)(2,1)S(1)}, u32[]{:S(2)}, u32[]{:S(2)}) collective-permute-start(bf16[1088,128]{1,0:T(8,128)(2,1)S(1)} %pad_maximum_fusion.own), channel_id=1, source_target_pairs={{1,0},{2,1},{3,2},{4,3},{5,4},{6,5},{7,6},{8,7},{9,8},{10,9},{11,1... | collective-permute-start | bytes 835592 | tf_op jit(solution)/shard_map/ppermute | solution.py:17
  12.2 4.8 %collective-permute-start = (bf16[768,128]{1,0:T(8,128)(2,1)}, bf16[768,128]{1,0:T(8,128)(2,1)S(1)}, u32[]{:S(2)}, u32[]{:S(2)}) collective-permute-start(bf16[768,128]{1,0:T(8,128)(2,1)} %bitcast.2), channel_id=1, source_target_pairs={{0,1},{1,2},{2,3},{3,4},{4,5},{5,6},{6,7},{7,8},{8,9},{9,10},{10,1... | collective-permute-start | bytes 589832 | tf_op jit(solution)/shard_map/ppermute | solution.py:17
  19.7 3.2 %collective-permute-start.2 = (bf16[32,1408]{1,0:T(8,128)(2,1)S(1)}, bf16[32,1408]{1,0:T(8,128)(2,1)S(1)}, u32[]{:S(2)}, u32[]{:S(2)}) collective-permute-start(bf16[32,1408]{1,0:T(8,128)(2,1)S(1)} %get-tuple-element.12), channel_id=1, source_target_pairs={{0,1},{1,0},{2,3},{3,2},{4,5},{5,4},{6,7},{7,6},{8,9},{9,8},{10,11... | collective-permute-start | bytes 270344 | tf_op jit(solution)/shard_map/ppermute | solution.py:282
  88.0 23.0 %all-to-all-start.2 = ((bf16[32,72,128]{2,1,0:T(8,128)(2,1)}), bf16[32,72,128]{2,1,0:T(8,128)(2,1)S(1)}, u32[]{:S(2)}, u32[]{:S(2)}) async-start(bf16[32,72,128]{2,1,0:T(8,128)(2,1)} %broadcast_in_dim.8), calls=%async_computation.2 | async-start | bytes 1179648 | tf_op jit(solution)/shard_map/all_to_all | solution.py:230

commit v3 on v2

--- a/solution.py
+++ b/solution.py
@@ -11,12 +11,6 @@
 F32 = jnp.float32
 
 
-def shifted(value, axis, steps):
-    count = lax.axis_size(axis)
-    initial, last = (max(0, -steps), min(count, count - steps))
-    return lax.ppermute(value, axis, [(source, source + steps) for source in range(initial, last)])
-
-
 def gradient_silu(values):
     logistic = jax.nn.sigmoid(values)
     return logistic * (1.0 + values * (1.0 - logistic))
@@ -62,19 +56,21 @@
     return ((r >> 4) == (c & 15)) & ((r & 15) == (c >> 4))
 
 
-def forward_kernel(
-    parity, below, own, above, flipped, second_weight, pre_ref, delta_ref, kept_ref, sent_ref, blocks, taps
+def kernel(
+    scalars, below, own, above, flipped, first_weight, second_weight, volume_ref, grad_ref, blocks, taps
 ):
+    parity, inside = scalars[0], scalars[1] > 0
     chan_in, cells = 64, 128
     group = 9 * chan_in
     down_first = picker(2 * cells, 3 * 128, down_first_test)
     down_second = picker(192, 128, down_second_test)
     first = 0
-    for part, planes in ((below, 3), (own, 4), (above, 4)):
+    for part, planes, skip in ((below, 3, 4), (own, 4, 0), (above, 4, 0)):
 
         def row(r):
             lines = [
-                part[(4 * p + r) * chan_in : (4 * p + r + 1) * chan_in, :] for p in range(planes)
+                part[(4 * p + r + skip) * chan_in : (4 * p + r + skip + 1) * chan_in, :]
+                for p in range(planes)
             ]
             return jnp.concatenate(lines, 0)
 
@@ -95,47 +91,45 @@
     lines = 16 * chan_in
     cotangent = jnp.concatenate(
         [
-            jnp.concatenate([part[lines : lines + 32, :], part[lines + 32 : lines + 64, :]], 1)
+            part[lines + 16 * tile + 8 * half : lines + 16 * tile + 8 * half + 8, :].astype(F32)
+            for half in range(2)
             for part in (own, above)
+            for tile in range(4)
         ],
         0,
     )
+    cotangent = jnp.concatenate([cotangent[:64], cotangent[64:]], 1)
+    pres = []
     for h in range(5):
-        pre = dot(flipped[...], blocks[2 * h * group : (2 * h + 3) * group, :])
-        if 1 <= h <= 3:
-            pre_ref[h - 1] = pre
+        if h == 3:
+            pre = jnp.where(inside, dot(flipped[:, :group], blocks[6 * group : 7 * group, :]), 0.0)
+            pre = pre + dot(flipped[:, group:], blocks[7 * group : 9 * group, :])
+        else:
+            pre = dot(flipped[...], blocks[2 * h * group : (2 * h + 3) * group, :])
+        pres.append(pre)
         hidden = (pre * jax.nn.sigmoid(pre)).astype(BF)
         chan = hidden.shape[0]
-        picked = dot_rows(down_second, hidden).astype(BF)
+        picked = dot_rows(down_second, hidden)
         for i in range(2):
             a = h - 2 * i
             if 0 <= a <= 2:
+                masked = jnp.where(inside, picked, 0.0) if (i, a) == (1, 0) else picked
+                masked = masked.astype(BF)
                 for be in range(6):
                     taps[i * quarter : (i + 1) * quarter, (6 * a + be) * chan : (6 * a + be + 1) * chan] = (
-                        picked[be * quarter : (be + 1) * quarter]
+                        masked[be * quarter : (be + 1) * quarter]
                     )
     pre = None
     for a in range(3):
         rows = second_weight[(9 * a + 3) * chan : 9 * (a + 1) * chan, :]
         term = dot(taps[:, 6 * a * chan : 6 * (a + 1) * chan], rows)
         pre = term if pre is None else pre + term
-    delta = cotangent.astype(F32) * gradient_silu(pre)
-    delta_ref[...] = delta.T.astype(BF)
-    share = 9 * chan
-    for ref, half in ((kept_ref, parity[0]), (sent_ref, 1 - parity[0])):
-        start = pl.multiple_of(half * share, 128)
-        ref[:, :share] = taps[:quarter, pl.ds(start, share)]
-        ref[:, share:] = delta[:quarter].astype(BF)
-
-
-def backward_kernel(
-    below, own, delta, pre_ref, kept, got, first_weight, second_weight, volume_ref, grad_ref
-):
-    chan_in, cells = 64, 128
-    chan = pre_ref.shape[1]
+    ended = cotangent * gradient_silu(pre)
+    delta = jnp.concatenate([ended[:quarter], jnp.where(inside, ended[quarter:], 0.0)], 0).T
+    delta = delta.astype(BF)
     up_first = picker(128, 768, up_first_test)
     up_second = picker(64, 1536, up_second_test)
-    spread = dot(delta[...], up_second).astype(BF)
+    spread = dot(delta, up_second).astype(BF)
     lanes = spread.shape[1] // 12
     deltas = []
     for h, pairs in enumerate((((1, 0),), ((2, 0), (0, 1)), ((1, 1),))):
@@ -148,7 +142,7 @@
                     spread[:, (6 * i + be) * lanes : (6 * i + be + 1) * lanes],
                 )
                 total = term if total is None else total + term
-        deltas.append((total * gradient_silu(pre_ref[h])).astype(BF))
+        deltas.append((total * gradient_silu(pres[h + 1])).astype(BF))
     raised = dot(jnp.concatenate(deltas, 0), up_first).astype(BF)
     wide = 2 * cells
     stacks = [
@@ -181,7 +175,7 @@
         volume_ref[p, r] = total.astype(BF)
 
     def plane(p, r):
-        ref, start = (below, (8 + r) * chan_in) if p < 0 else (own, (4 * p + r) * chan_in)
+        ref, start = (below, (12 + r) * chan_in) if p < 0 else (own, (4 * p + r) * chan_in)
         return ref[start : start + chan_in, :]
 
     blank = jnp.zeros((chan_in, cells), BF)
@@ -210,10 +204,10 @@
             grad_ref[m, offset : offset + count, :] = value[begin : begin + count]
             at += count
     share = 9 * chan
-    both = jnp.concatenate([kept[...], got[...]], 0)
-    ordered = dot(both[:, share:], picker(256, 256, reorder_test)).astype(BF)
+    fields = taps[:, pl.ds(pl.multiple_of(parity * share, 128), share)]
+    ordered = dot(ended.astype(BF), picker(256, 256, reorder_test)).astype(BF)
     second = lax.dot_general(
-        ordered, both[:, :share], (((0,), (0,)), ((), ())), preferred_element_type=F32
+        ordered, fields, (((0,), (0,)), ((), ())), preferred_element_type=F32
     ).astype(BF)
     second = jnp.concatenate([second, jnp.zeros((second.shape[0], chan), BF)], 1)
     per = 32 // grad_ref.shape[0]
@@ -234,18 +228,6 @@
     return exchanged(jnp.broadcast_to(value[None], (lax.axis_size(axis),) + value.shape), axis)
 
 
-def call(kernel, outs, scratch, flops, moved, scalars=0, inputs=0):
-    places = [pltpu.SMEM] * scalars + [pltpu.VMEM] * inputs
-    return pl.pallas_call(
-        kernel,
-        out_shape=outs,
-        in_specs=[pl.BlockSpec(memory_space=place) for place in places],
-        scratch_shapes=scratch,
-        compiler_params=pltpu.CompilerParams(vmem_limit_bytes=24 << 20),
-        cost_estimate=pl.CostEstimate(flops=flops, bytes_accessed=moved, transcendentals=0),
-    )
-
-
 def shards(input_field, out_cotangent, first_weight, second_weight):
     chan_in, planes, height, length = input_field.shape[1:]
     chan_mid, chan_out = second_weight.shape[1:]
@@ -254,46 +236,35 @@
     rows, half, quarter = (height // 2, length // 2, length // 4)
     per_group = chan_out // groups
     own = input_field[0].transpose(1, 2, 0, 3).reshape(-1, length)
-    below = shifted(own[height * chan_in :], "space", 1)
-    cotangent = out_cotangent[0].reshape(2, chan_out // 2, quarter).transpose(0, 2, 1)
-    own = jnp.concatenate([own, cotangent.reshape(2 * quarter, chan_out // 2)], 0)
-    above = shifted(own, "space", -1)
+    cotangent = out_cotangent[0].reshape(chan_out, quarter).T.reshape(4, 8, 2, 128)
+    own = jnp.concatenate([own, cotangent.transpose(0, 2, 1, 3).reshape(64, 128)], 0)
+    above = lax.ppermute(own, "space", [(i, (i - 1) % groups) for i in range(groups)])
+    below = lax.ppermute(own, "space", [(i, i + 1) for i in range(groups - 1)])
     flipped = first_weight.reshape(27 * chan_in, chan_mid).T
     flat_second = second_weight.reshape(27 * chan_mid, chan_out)
-    share = 9 * chan_mid
-    parity = (lax.axis_index("space") % 2).astype(jnp.int32).reshape(1)
-    pre, delta, kept, sent = call(
-        forward_kernel,
-        (
-            jax.ShapeDtypeStruct((3, chan_mid, rows * half), F32),
-            jax.ShapeDtypeStruct((chan_out, 2 * quarter), BF),
-            jax.ShapeDtypeStruct((quarter, share + chan_out), BF),
-            jax.ShapeDtypeStruct((quarter, share + chan_out), BF),
+    place = lax.axis_index("space")
+    scalars = jnp.where(
+        jnp.arange(2) == 0, place % 2, jnp.where(place == groups - 1, 0, 1)
+    ).astype(jnp.int32)
+    size = 28 * chan_in // samples_n
+    pieces = 32 // samples_n * 5
+    volume, partial = pl.pallas_call(
+        kernel,
+        out_shape=(
+            jax.ShapeDtypeStruct((planes, height, chan_in, length), BF),
+            jax.ShapeDtypeStruct((samples_n, size + pieces * groups, chan_mid), BF),
         ),
-        [
+        in_specs=[pl.BlockSpec(memory_space=pltpu.SMEM)]
+        + [pl.BlockSpec(memory_space=pltpu.VMEM)] * 6,
+        scratch_shapes=[
             pltpu.VMEM((11 * 9 * chan_in, rows * half), BF),
             pltpu.VMEM((2 * quarter, 18 * chan_mid), BF),
         ],
-        2_000_000_000,
-        6_000_000,
-        1,
-        5,
-    )(parity, below, own, above, flipped, flat_second)
-    got = lax.ppermute(sent, "space", [(i, i ^ 1) for i in range(groups)])
-    size = 28 * chan_in // samples_n
-    pieces = 32 // samples_n * 5
-    volume, partial = call(
-        backward_kernel,
-        (
-            jax.ShapeDtypeStruct((planes, height, chan_in, length), BF),
-            jax.ShapeDtypeStruct((samples_n, size + pieces * groups, chan_mid), BF),
+        compiler_params=pltpu.CompilerParams(vmem_limit_bytes=24 << 20),
+        cost_estimate=pl.CostEstimate(
+            flops=5_000_000_000, bytes_accessed=8_000_000, transcendentals=0
         ),
-        [],
-        3_000_000_000,
-        6_000_000,
-        0,
-        8,
-    )(below, own, delta, pre, kept, got, first_weight, flat_second)
+    )(scalars, below, own, above, flipped, first_weight, flat_second)
     input_grad = volume.transpose(2, 0, 1, 3)[None]
     chunk = jnp.sum(exchanged(partial, "sample").astype(F32), 0)
     first_chunk = jnp.broadcast_to(chunk[None, :size], (groups, size, chan_mid))

time: 113 us -> 107 us (0.947)
  starting transfers between devices: 16.6 us -> 12.7 us
  blocking collectives: 61.8 us -> 59.7 us
    ppermute x3 -> x2, starting transfers between devices: 12.7 us -> 8.8 us  [the longest x1 6.89 us: shards(): lax.ppermute(own, 'space', [(i, (i - 1) % groups) for i in range(groups)])]
    all_to_all x2, blocking collectives: 61.8 us -> 59.7 us  [exchanged(): return lax.all_to_all(parts, axis, split_axis=0, concat_axis=0, tiled=True)]
    unnamed x9 -> x7, local copies, waits for them, and re-layouts: 0.94 us -> 2.4 us
    ppermute x3 -> x2, waiting for transfers between devices: 3.92 us -> 3.23 us  [the longest x1 3.23 us: shards(): below = lax.ppermute(own, 'space', [(i, i + 1) for i in range(groups - 1)])]
    pallas_call x2 -> x1, Pallas kernels: 4.59 us -> 5 us  [shards(): pl.pallas_call(kernel, out_shape=(jax.ShapeDtypeStruct((planes, height, c...]
  transfers between devices with their start and end apart: 4 -> 3, of which waited for: 3 -> 2; matrix products, arithmetic and copies ran while one was open for 2% -> 1% of each run, Pallas kernels for 0% -> 0%
where the time goes in v3:
time: 107 us
  blocking collectives  59.7 us (56%)
  waiting for transfers between devices  21.4 us (20%)
  starting transfers between devices  12.7 us (12%)
  local copies, waits for them, and re-layouts  6.17 us (6%)
  Pallas kernels  5 us (5%)
    all_to_all x2, blocking collectives, exchanged(): return lax.all_to_all(parts, axis, split_axis=0, concat_axis=0, tiled=True)  59.7 us
    all_to_all x1, waiting for transfers between devices, exchanged(): return lax.all_to_all(parts, axis, split_axis=0, concat_axis=0, tiled=True)  18.2 us
    ppermute x1, starting transfers between devices, shards(): lax.ppermute(own, 'space', [(i, (i - 1) % groups) for i in range(groups)])  6.89 us
    pallas_call x1, Pallas kernels, shards(): pl.pallas_call(kernel, out_shape=(jax.ShapeDtypeStruct((planes, height, c...  5 us
    all_to_all x1, starting transfers between devices, exchanged(): return lax.all_to_all(parts, axis, split_axis=0, concat_axis=0, tiled=True)  3.89 us
    ppermute x1, waiting for transfers between devices, shards(): below = lax.ppermute(own, 'space', [(i, i + 1) for i in range(groups - 1)])  3.23 us
    unnamed x7, local copies, waits for them, and re-layouts  2.4 us
  transfers between devices with their start and end apart: 3, of which 2 were waited for; matrix products, arithmetic and copies ran while one was open for 1% of the time, Pallas kernels for 0%

profile of v3, /device:TPU:1, one launch (start us, length us, event | category | flops | bytes accessed | tf_op | source)
XLA Modules:
  0.0 106.8 jit_solution(8321795225682831227)
XLA Ops:
  0.6 0.0 copy-start
  0.6 1.1 %copy.34 = bf16[4,4,64,128]{3,2,1,0:T(8,128)(2,1)S(1)} copy(bf16[4,4,64,128]{3,1,0,2:T(4,128)(2,1)} %bitcast.42) | data formatting | bytes 524288 | tf_op jit(solution)/shard_map/transpose | solution.py:238
  1.7 0.7 pad_maximum_fusion.own
  2.5 6.9 %collective-permute-start.1 = (bf16[1088,128]{1,0:T(8,128)(2,1)S(1)}, bf16[1088,128]{1,0:T(8,128)(2,1)S(1)}, u32[]{:S(2)}, u32[]{:S(2)}) collective-permute-start(bf16[1088,128]{1,0:T(8,128)(2,1)S(1)} %pad_maximum_fusion.own), channel_id=1, source_target_pairs={{0,15},{1,0},{2,1},{3,2},{4,3},{5,4},{6,5},{7,6},{8,7},{9,8},{10,9... | collective-permute-start | bytes 835592 | tf_op jit(solution)/shard_map/ppermute | solution.py:241
  9.3 1.9 %collective-permute-start = (bf16[1088,128]{1,0:T(8,128)(2,1)S(1)}, bf16[1088,128]{1,0:T(8,128)(2,1)S(1)}, u32[]{:S(2)}, u32[]{:S(2)}) collective-permute-start(bf16[1088,128]{1,0:T(8,128)(2,1)S(1)} %pad_maximum_fusion.own), channel_id=1, source_target_pairs={{0,1},{1,2},{2,3},{3,4},{4,5},{5,6},{6,7},{7,8},{8,9},{9,10},{10,1... | collective-permute-start | bytes 835592 | tf_op jit(solution)/shard_map/ppermute | solution.py:242
  11.3 0.0 copy-done
  11.3 0.2 copy.35
  11.5 0.0 collective-permute-done.1.above
  11.5 3.2 %collective-permute-done.below = bf16[1088,128]{1,0:T(8,128)(2,1)S(1)} collective-permute-done((bf16[1088,128]{1,0:T(8,128)(2,1)S(1)}, bf16[1088,128]{1,0:T(8,128)(2,1)S(1)}, u32[]{:S(2)}, u32[]{:S(2)}) %collective-permute-start) | collective-permute-done | bytes 278560 | tf_op jit(solution)/shard_map/ppermute | solution.py:242
  14.8 0.0 copy-start.1
  14.8 1.5 %copy-done.1 = bf16[27,128,256]{2,1,0:T(8,128)(2,1)S(1)} copy-done((bf16[27,128,256]{2,1,0:T(8,128)(2,1)S(1)}, bf16[27,128,256]{2,1,0:T(8,128)(2,1)}, u32[]{:S(2)}) %copy-start.1) | copy-done | bytes 1769496
  16.2 5.0 %shard_map.67 = (bf16[4,4,64,128]{3,2,1,0:T(8,128)(2,1)S(1)}, bf16[32,136,128]{2,1,0:T(8,128)(2,1)S(1)}) custom-call(s32[2]{0:T(128)S(1)} %compare_select_fusion.scalars, bf16[1088,128]{1,0:T(8,128)(2,1)S(1)} %collective-permute-done.below, bf16[1088,128]{1,0:T(8,128)(2,1)S(1)} %pad_maximum_fusion.own, bf16[1088,128]{1,0:T(8,128)(2,1)S(1)} %collective-permute-done.1.above, ...), custom_call_target="tpu_custom_call" | custom-call | flops 5000000000 | bytes 8000000 | tf_op jit(solution)/shard_map/pallas_call | solution.py:251
  21.3 38.6 %all_to_all.15 = bf16[32,136,128]{2,1,0:T(8,128)(2,1)S(1)} all-to-all(bf16[32,136,128]{2,1,0:T(8,128)(2,1)S(1)} %get-tuple-element.6), channel_id=1, replica_groups=mesh['sample'=32,'space'=16] {'sample'}, dimensions={0} | all-to-all | bytes 2228224 | tf_op jit(solution)/shard_map/all_to_all | solution.py:224
  59.9 0.2 convert_reduce_fusion
  60.1 21.1 %all_to_all.16 = bf16[16,64,128]{2,1,0:T(8,128)(2,1)S(1)} all-to-all(bf16[16,64,128]{2,1,0:T(8,128)(2,1)S(1)} %fusion.1), channel_id=1, replica_groups=mesh['sample'=32,'space'=16] {'space'}, dimensions={0} | all-to-all | bytes 524288 | tf_op jit(solution)/shard_map/all_to_all | solution.py:224
  81.4 0.9 broadcast_in_dim.27
  82.3 3.9 %all-to-all-start.2 = ((bf16[32,72,128]{2,1,0:T(8,128)(2,1)}), bf16[32,72,128]{2,1,0:T(8,128)(2,1)S(1)}, u32[]{:S(2)}, u32[]{:S(2)}) async-start(bf16[32,72,128]{2,1,0:T(8,128)(2,1)} %broadcast_in_dim.27), calls=%async_computation.2 | async-start | bytes 1179648 | tf_op jit(solution)/shard_map/all_to_all | solution.py:224
  86.2 0.9 copy.41
  87.1 18.2 %all-to-all-done.2 = bf16[32,72,128]{2,1,0:T(8,128)(2,1)S(1)} async-done(((bf16[32,72,128]{2,1,0:T(8,128)(2,1)}), bf16[32,72,128]{2,1,0:T(8,128)(2,1)S(1)}, u32[]{:S(2)}, u32[]{:S(2)}) %all-to-all-start.2) | async-done | bytes 589856 | tf_op jit(solution)/shard_map/all_to_all | solution.py:224
  105.4 0.8 slice.38
  106.2 0.7 pad.16
  (19 shorter events, 0.3 us)
Async XLA Ops:
  0.6 10.6 %copy-start = (bf16[27,64,128]{2,1,0:T(8,128)(2,1)S(1)}, bf16[27,64,128]{2,1,0:T(8,128)(2,1)}, u32[]{:S(2)}) copy-start(bf16[27,64,128]{2,1,0:T(8,128)(2,1)} %first_weight.1) | copy-start | bytes 1327108
  2.5 9.1 %collective-permute-start.1 = (bf16[1088,128]{1,0:T(8,128)(2,1)S(1)}, bf16[1088,128]{1,0:T(8,128)(2,1)S(1)}, u32[]{:S(2)}, u32[]{:S(2)}) collective-permute-start(bf16[1088,128]{1,0:T(8,128)(2,1)S(1)} %pad_maximum_fusion.own), channel_id=1, source_target_pairs={{0,15},{1,0},{2,1},{3,2},{4,3},{5,4},{6,5},{7,6},{8,7},{9,8},{10,9... | collective-permute-start | bytes 835592 | tf_op jit(solution)/shard_map/ppermute | solution.py:241
  9.3 5.4 %collective-permute-start = (bf16[1088,128]{1,0:T(8,128)(2,1)S(1)}, bf16[1088,128]{1,0:T(8,128)(2,1)S(1)}, u32[]{:S(2)}, u32[]{:S(2)}) collective-permute-start(bf16[1088,128]{1,0:T(8,128)(2,1)S(1)} %pad_maximum_fusion.own), channel_id=1, source_target_pairs={{0,1},{1,2},{2,3},{3,4},{4,5},{5,6},{6,7},{7,8},{8,9},{9,10},{10,1... | collective-permute-start | bytes 835592 | tf_op jit(solution)/shard_map/ppermute | solution.py:242
  14.8 1.5 %copy-start.1 = (bf16[27,128,256]{2,1,0:T(8,128)(2,1)S(1)}, bf16[27,128,256]{2,1,0:T(8,128)(2,1)}, u32[]{:S(2)}) copy-start(bf16[27,128,256]{2,1,0:T(8,128)(2,1)} %param.7) | copy-start | bytes 5308420
  82.3 23.0 %all-to-all-start.2 = ((bf16[32,72,128]{2,1,0:T(8,128)(2,1)}), bf16[32,72,128]{2,1,0:T(8,128)(2,1)S(1)}, u32[]{:S(2)}, u32[]{:S(2)}) async-start(bf16[32,72,128]{2,1,0:T(8,128)(2,1)} %broadcast_in_dim.27), calls=%async_computation.2 | async-start | bytes 1179648 | tf_op jit(solution)/shard_map/all_to_all | solution.py:224

commit v4 on v3

--- a/solution.py
+++ b/solution.py
@@ -56,9 +56,19 @@
     return ((r >> 4) == (c & 15)) & ((r & 15) == (c >> 4))
 
 
-def kernel(
-    scalars, below, own, above, flipped, first_weight, second_weight, volume_ref, grad_ref, blocks, taps
+def main_kernel(
+    scalars, below, own, above, flipped, second_hbm,
+    stacks_ref, kept_ref, sent_ref, second_ref,
+    blocks, taps, grads, second_weight, sems,
 ):
+    copies = []
+    for a in range(3):
+        size = second_weight.shape[1]
+        start = 3 * a * size // 2 + size // 2
+        copies.append(
+            pltpu.make_async_copy(second_hbm.at[start : start + size], second_weight.at[a], sems.at[a])
+        )
+        copies[a].start()
     parity, inside = scalars[0], scalars[1] > 0
     chan_in, cells = 64, 128
     group = 9 * chan_in
@@ -121,8 +131,8 @@
                     )
     pre = None
     for a in range(3):
-        rows = second_weight[(9 * a + 3) * chan : 9 * (a + 1) * chan, :]
-        term = dot(taps[:, 6 * a * chan : 6 * (a + 1) * chan], rows)
+        copies[a].wait()
+        term = dot(taps[:, 6 * a * chan : 6 * (a + 1) * chan], second_weight[a])
         pre = term if pre is None else pre + term
     ended = cotangent * gradient_silu(pre)
     delta = jnp.concatenate([ended[:quarter], jnp.where(inside, ended[quarter:], 0.0)], 0).T
@@ -136,9 +146,8 @@
         total = None
         for a, i in pairs:
             for be in range(6):
-                start = (9 * a + 3 + be) * chan
                 term = dot(
-                    second_weight[start : start + chan, :],
+                    second_weight[a, be * chan : (be + 1) * chan, :],
                     spread[:, (6 * i + be) * lanes : (6 * i + be + 1) * lanes],
                 )
                 total = term if total is None else total + term
@@ -151,6 +160,59 @@
         )
         for h in range(3)
     ]
+
+    for h in range(3):
+        stacks_ref[h] = stacks[h]
+
+    def plane(p, r):
+        ref, start = (below, (12 + r) * chan_in) if p < 0 else (own, (4 * p + r) * chan_in)
+        return ref[start : start + chan_in, :]
+
+    blank = jnp.zeros((chan_in, cells), BF)
+    lefts = []
+    for a in range(3):
+        for b in range(3):
+            pieces = []
+            for i in range(2):
+                for j in range(2):
+                    r = 2 * j + b - 1
+                    pieces.append(blank if r < 0 else plane(2 * i + a - 1, r))
+            lefts.append(jnp.concatenate(pieces, 1))
+    result = dot_rows(jnp.concatenate(lefts, 0), jnp.concatenate(stacks[:2], 1))
+    for ab in range(9):
+        for e in range(3):
+            start = (3 * ab + e) * chan_in
+            grads[start : start + chan_in, :] = result[
+                ab * chan_in : (ab + 1) * chan_in, e * chan : (e + 1) * chan
+            ]
+    grads[27 * chan_in :, :] = jnp.zeros((chan_in, chan), F32)
+    samples_n, size = kept_ref.shape[:2]
+    for m in range(samples_n):
+        lower = grads[2 * m * size : (2 * m + 1) * size, :]
+        upper = grads[(2 * m + 1) * size : (2 * m + 2) * size, :]
+        kept_ref[m] = jnp.where(parity == 0, lower, upper).astype(BF)
+        sent_ref[m] = jnp.where(parity == 0, upper, lower).astype(BF)
+    share = 9 * chan
+    fields = taps[:, pl.ds(pl.multiple_of(parity * share, 128), share)]
+    ordered = dot(ended.astype(BF), picker(256, 256, reorder_test)).astype(BF)
+    second = lax.dot_general(
+        ordered, fields, (((0,), (0,)), ((), ())), preferred_element_type=F32
+    ).astype(BF)
+    per = 32 // samples_n
+    for piece in range(32):
+        m, at = piece // per, piece % per * 72
+        first = piece // 2 * 16
+        for lane in range(4, 9) if piece % 2 else range(5):
+            begin = first + 8 if lane == 4 and piece % 2 else first
+            count = 8 if lane == 4 else 16
+            second_ref[m, at : at + count, :] = second[
+                begin : begin + count, lane * chan : (lane + 1) * chan
+            ]
+            at += count
+
+
+def volume_kernel(stacks, first_weight, volume_ref):
+    chan_in, cells = volume_ref.shape[2:]
 
     def filters(a):
         return [
@@ -174,50 +236,12 @@
     for (p, r), total in totals.items():
         volume_ref[p, r] = total.astype(BF)
 
-    def plane(p, r):
-        ref, start = (below, (12 + r) * chan_in) if p < 0 else (own, (4 * p + r) * chan_in)
-        return ref[start : start + chan_in, :]
-
-    blank = jnp.zeros((chan_in, cells), BF)
-    lefts = []
-    for a in range(3):
-        for b in range(3):
-            pieces = []
-            for i in range(2):
-                for j in range(2):
-                    r = 2 * j + b - 1
-                    pieces.append(blank if r < 0 else plane(2 * i + a - 1, r))
-            lefts.append(jnp.concatenate(pieces, 1))
-    grads = dot_rows(jnp.concatenate(lefts, 0), jnp.concatenate(stacks[:2], 1)).astype(BF)
-    chunk = 28 * chan_in // grad_ref.shape[0]
-    for tap in range(28):
-        if tap < 27:
-            ab, e = tap // 3, tap % 3
-            value = grads[ab * chan_in : (ab + 1) * chan_in, e * chan : (e + 1) * chan]
-        else:
-            value = jnp.zeros((chan_in, chan), BF)
-        at, stop = tap * chan_in, (tap + 1) * chan_in
-        while at < stop:
-            m, offset = at // chunk, at % chunk
-            count = min(stop - at, chunk - offset)
-            begin = at - tap * chan_in
-            grad_ref[m, offset : offset + count, :] = value[begin : begin + count]
-            at += count
-    share = 9 * chan
-    fields = taps[:, pl.ds(pl.multiple_of(parity * share, 128), share)]
-    ordered = dot(ended.astype(BF), picker(256, 256, reorder_test)).astype(BF)
-    second = lax.dot_general(
-        ordered, fields, (((0,), (0,)), ((), ())), preferred_element_type=F32
-    ).astype(BF)
-    second = jnp.concatenate([second, jnp.zeros((second.shape[0], chan), BF)], 1)
-    per = 32 // grad_ref.shape[0]
-    for piece in range(32):
-        o, h = piece // 2, piece % 2
-        for lane in range(5):
-            start = chunk + (piece % per * 5 + lane) * 16
-            grad_ref[piece // per, start : start + 16, :] = second[
-                o * 16 : (o + 1) * 16, (5 * h + lane) * chan : (5 * h + lane + 1) * chan
-            ]
+
+def pack_kernel(second, kept, got, payload_ref):
+    rows = second.shape[1]
+    for m in range(second.shape[0]):
+        payload_ref[m, :rows, :] = second[m]
+        payload_ref[m, rows:, :] = (kept[m].astype(F32) + got[m].astype(F32)).astype(BF)
 
 
 def exchanged(parts, axis):
@@ -246,43 +270,75 @@
     scalars = jnp.where(
         jnp.arange(2) == 0, place % 2, jnp.where(place == groups - 1, 0, 1)
     ).astype(jnp.int32)
-    size = 28 * chan_in // samples_n
-    pieces = 32 // samples_n * 5
-    volume, partial = pl.pallas_call(
-        kernel,
+    size = 14 * chan_in // samples_n
+    per = 32 // samples_n
+    vmem = pl.BlockSpec(memory_space=pltpu.VMEM)
+    stacks, kept, sent, second = pl.pallas_call(
+        main_kernel,
         out_shape=(
-            jax.ShapeDtypeStruct((planes, height, chan_in, length), BF),
-            jax.ShapeDtypeStruct((samples_n, size + pieces * groups, chan_mid), BF),
+            jax.ShapeDtypeStruct((3, 3 * chan_mid, 2 * length), BF),
+            jax.ShapeDtypeStruct((samples_n, size, chan_mid), BF),
+            jax.ShapeDtypeStruct((samples_n, size, chan_mid), BF),
+            jax.ShapeDtypeStruct((samples_n, per * 72, chan_mid), BF),
         ),
         in_specs=[pl.BlockSpec(memory_space=pltpu.SMEM)]
-        + [pl.BlockSpec(memory_space=pltpu.VMEM)] * 6,
+        + [vmem] * 4
+        + [pl.BlockSpec(memory_space=pl.ANY)],
         scratch_shapes=[
             pltpu.VMEM((11 * 9 * chan_in, rows * half), BF),
             pltpu.VMEM((2 * quarter, 18 * chan_mid), BF),
+            pltpu.VMEM((28 * chan_in, chan_mid), F32),
+            pltpu.VMEM((3, 6 * chan_mid, chan_out), BF),
+            pltpu.SemaphoreType.DMA((3,)),
         ],
         compiler_params=pltpu.CompilerParams(vmem_limit_bytes=24 << 20),
         cost_estimate=pl.CostEstimate(
-            flops=5_000_000_000, bytes_accessed=8_000_000, transcendentals=0
+            flops=4_000_000_000, bytes_accessed=8_000_000, transcendentals=0
         ),
-    )(scalars, below, own, above, flipped, first_weight, flat_second)
+    )(scalars, below, own, above, flipped, flat_second)
+    got = lax.ppermute(sent, "space", [(i, i ^ 1) for i in range(groups)])
+    payload = pl.pallas_call(
+        pack_kernel,
+        out_shape=jax.ShapeDtypeStruct((samples_n, per * 72 + size, chan_mid), BF),
+        cost_estimate=pl.CostEstimate(flops=1_000_000, bytes_accessed=2_000_000, transcendentals=0),
+    )(second, kept, got)
+    volume = pl.pallas_call(
+        volume_kernel,
+        out_shape=jax.ShapeDtypeStruct((planes, height, chan_in, length), BF),
+        compiler_params=pltpu.CompilerParams(vmem_limit_bytes=24 << 20),
+        cost_estimate=pl.CostEstimate(
+            flops=1_000_000_000, bytes_accessed=2_000_000, transcendentals=0
+        ),
+    )(stacks, first_weight)
     input_grad = volume.transpose(2, 0, 1, 3)[None]
-    chunk = jnp.sum(exchanged(partial, "sample").astype(F32), 0)
-    first_chunk = jnp.broadcast_to(chunk[None, :size], (groups, size, chan_mid))
-    second_chunk = chunk[size:].reshape(pieces, groups, chan_mid).transpose(1, 0, 2)
-    second_chunk = jnp.pad(second_chunk, ((0, 0), (0, -pieces % 8), (0, 0)))
+    chunk = jnp.sum(exchanged(payload, "sample").astype(F32), 0)
+    first_chunk = jnp.broadcast_to(chunk[None, per * 72 :], (groups, size, chan_mid))
+    second_chunk = chunk[: per * 72].reshape(per, 72, chan_mid)
+    odd = (lax.axis_index("sample") * per + jnp.arange(per)) % 2 == 1
+    second_chunk = jnp.where(
+        odd[:, None, None],
+        jnp.pad(second_chunk, ((0, 0), (8, 0), (0, 0))),
+        jnp.pad(second_chunk, ((0, 0), (0, 8), (0, 0))),
+    )
+    pieces = 5 * per
+    second_chunk = second_chunk.reshape(pieces, groups, chan_mid).transpose(1, 0, 2)
+    second_chunk = jnp.pad(second_chunk, ((0, 0), (0, -(size + pieces) % 8), (0, 0)))
     both = exchanged(jnp.concatenate([first_chunk, second_chunk], 1).astype(BF), "space")
+    both = jnp.sum(both.astype(F32).reshape(groups // 2, 2, -1, chan_mid), 0)
     first_ext = planes // 2 * rows * half
     first_scale = 1.0 / math.sqrt(samples_n * groups * first_ext)
     second_scale = 1.0 / math.sqrt(samples_n * groups * (planes // 4) * (height // 4) * quarter)
-    first_chunk = jnp.sum(both[:, :size].astype(F32), 0) * first_scale
-    second_chunk = both[:, size : size + pieces].astype(F32).reshape(groups // 2, 2, pieces, chan_mid)
-    second_chunk = (jnp.sum(second_chunk, 0) * second_scale).reshape(2 * pieces, chan_mid)
-    second_chunk = jnp.pad(second_chunk, ((0, -2 * pieces % 8), (0, 0)))
-    final = everywhere(jnp.concatenate([first_chunk, second_chunk], 0).astype(BF), "sample")
-    first_grad = final[:, :size].reshape(28, chan_in, chan_mid)[:27]
-    second = final[:, size : size + 2 * pieces].reshape(samples_n, 2, 32 // samples_n, 5, chan_mid)
+    first_chunk = both[:, :size].reshape(2 * size, chan_mid) * first_scale
+    second_chunk = both[:, size : size + pieces].reshape(2 * pieces, chan_mid) * second_scale
+    both = jnp.concatenate([first_chunk, second_chunk], 0)
+    both = jnp.pad(both, ((0, -both.shape[0] % 8), (0, 0)))
+    final = everywhere(both.astype(BF), "sample")
+    first_grad = final[:, : 2 * size].reshape(28, chan_in, chan_mid)[:27]
+    second = final[:, 2 * size : 2 * size + 2 * pieces].reshape(samples_n, 2, per, 5, chan_mid)
     second = second.transpose(0, 2, 1, 3, 4).reshape(per_group, 2, 2, 5, chan_mid)
-    second = second.transpose(2, 1, 3, 0, 4).reshape(2, 10, per_group, chan_mid)[:, :9]
+    second = second.transpose(2, 1, 3, 0, 4)
+    shared = second[:, 0, 4:] + second[:, 1, :1]
+    second = jnp.concatenate([second[:, 0, :4], shared, second[:, 1, 1:]], 1)
     second = second.reshape(3, 2, 3, per_group, chan_mid)
     second = jnp.pad(second, ((0, 0), (1, 0), (0, 0), (0, 0), (0, 0)))
     second_grad = second.reshape(27, per_group, chan_mid).transpose(0, 2, 1)

time: 107 us -> 109 us (1.019)
  blocking collectives: 59.7 us -> 19 us
  waiting for transfers between devices: 21.4 us -> 43 us
  starting transfers between devices: 12.7 us -> 27 us
  Pallas kernels: 5 us -> 8.38 us
  local copies, waits for them, and re-layouts: 6.17 us -> 8.91 us
    all_to_all x2 -> x1, blocking collectives: 59.7 us -> 19 us  [exchanged(): return lax.all_to_all(parts, axis, split_axis=0, concat_axis=0, tiled=True)]
    all_to_all x1 -> x2, waiting for transfers between devices: 18.2 us -> 39.6 us  [exchanged(): return lax.all_to_all(parts, axis, split_axis=0, concat_axis=0, tiled=True)]
    all_to_all x1 -> x2, starting transfers between devices: 3.89 us -> 14.5 us  [exchanged(): return lax.all_to_all(parts, axis, split_axis=0, concat_axis=0, tiled=True)]
    ppermute x0 -> x1, starting transfers between devices: none -> 3.65 us  [shards(): got = lax.ppermute(sent, 'space', [(i, i ^ 1) for i in range(groups)])]
    pallas_call x1 -> x3, Pallas kernels: 5 us -> 8.38 us  [the longest x1 5.69 us: shards(): pl.pallas_call(main_kernel, out_shape=(jax.ShapeDtypeStruct((3, 3 * chan_...]
    unnamed x7 -> x18, local copies, waits for them, and re-layouts: 2.4 us -> 3.99 us
    ppermute x0 -> x1, waiting for transfers between devices: none -> 1.14 us  [shards(): got = lax.ppermute(sent, 'space', [(i, i ^ 1) for i in range(groups)])]
  transfers between devices with their start and end apart: 3 -> 5, of which waited for: 2 -> 4; matrix products, arithmetic and copies ran while one was open for 1% -> 2% of each run, Pallas kernels for 0% -> 0%
where the time goes in v4:
time: 109 us; the launch traced here: 108 us
  waiting for transfers between devices  43 us (39%)
  starting transfers between devices  27 us (25%)
  blocking collectives  19 us (17%)
  local copies, waits for them, and re-layouts  8.91 us (8%)
  Pallas kernels  8.38 us (8%)
    all_to_all x2, waiting for transfers between devices, exchanged(): return lax.all_to_all(parts, axis, split_axis=0, concat_axis=0, tiled=True)  39.6 us
    all_to_all x1, blocking collectives, exchanged(): return lax.all_to_all(parts, axis, split_axis=0, concat_axis=0, tiled=True)  19 us
    all_to_all x2, starting transfers between devices, exchanged(): return lax.all_to_all(parts, axis, split_axis=0, concat_axis=0, tiled=True)  14.5 us
    ppermute x1, starting transfers between devices, shards(): lax.ppermute(own, 'space', [(i, (i - 1) % groups) for i in range(groups)])  6.89 us
    pallas_call x1, Pallas kernels, shards(): pl.pallas_call(main_kernel, out_shape=(jax.ShapeDtypeStruct((3, 3 * chan_...  5.69 us
    unnamed x18, local copies, waits for them, and re-layouts  3.99 us
    ppermute x1, starting transfers between devices, shards(): got = lax.ppermute(sent, 'space', [(i, i ^ 1) for i in range(groups)])  3.65 us
    ppermute x1, waiting for transfers between devices, shards(): below = lax.ppermute(own, 'space', [(i, i + 1) for i in range(groups - 1)])  2.24 us
  transfers between devices with their start and end apart: 5, of which 4 were waited for; matrix products, arithmetic and copies ran while one was open for 2% of the time, Pallas kernels for 0%

profile of v4, /device:TPU:1, one launch (start us, length us, event | category | flops | bytes accessed | tf_op | source)
XLA Modules:
  0.0 108.1 jit_solution(6521455675269625663)
XLA Ops:
  0.6 0.0 copy-start.3
  0.6 1.1 %copy.37 = bf16[4,4,64,128]{3,2,1,0:T(8,128)(2,1)S(1)} copy(bf16[4,4,64,128]{3,1,0,2:T(4,128)(2,1)} %bitcast.55) | data formatting | bytes 524288 | tf_op jit(solution)/shard_map/transpose | solution.py:262
  1.8 0.7 pad_maximum_fusion.own
  2.5 6.9 %collective-permute-start.1 = (bf16[1088,128]{1,0:T(8,128)(2,1)S(1)}, bf16[1088,128]{1,0:T(8,128)(2,1)S(1)}, u32[]{:S(2)}, u32[]{:S(2)}) collective-permute-start(bf16[1088,128]{1,0:T(8,128)(2,1)S(1)} %pad_maximum_fusion.own), channel_id=1, source_target_pairs={{0,15},{1,0},{2,1},{3,2},{4,3},{5,4},{6,5},{7,6},{8,7},{9,8},{10,9... | collective-permute-start | bytes 835592 | tf_op jit(solution)/shard_map/ppermute | solution.py:265
  9.4 1.9 %collective-permute-start = (bf16[1088,128]{1,0:T(8,128)(2,1)S(1)}, bf16[1088,128]{1,0:T(8,128)(2,1)S(1)}, u32[]{:S(2)}, u32[]{:S(2)}) collective-permute-start(bf16[1088,128]{1,0:T(8,128)(2,1)S(1)} %pad_maximum_fusion.own), channel_id=1, source_target_pairs={{0,1},{1,2},{2,3},{3,4},{4,5},{5,6},{6,7},{7,8},{8,9},{9,10},{10,1... | collective-permute-start | bytes 835592 | tf_op jit(solution)/shard_map/ppermute | solution.py:266
  11.4 1.2 %copy.38 = bf16[1728,128]{0,1:T(8,128)(2,1)S(1)} copy(bf16[1728,128]{1,0:T(8,128)(2,1)} %bitcast.46) | data formatting | bytes 884736 | tf_op jit(solution)/shard_map/reshape | solution.py:267
  12.6 0.0 collective-permute-done.1.above
  12.6 2.2 %collective-permute-done.below = bf16[1088,128]{1,0:T(8,128)(2,1)S(1)} collective-permute-done((bf16[1088,128]{1,0:T(8,128)(2,1)S(1)}, bf16[1088,128]{1,0:T(8,128)(2,1)S(1)}, u32[]{:S(2)}, u32[]{:S(2)}) %collective-permute-start) | collective-permute-done | bytes 278560 | tf_op jit(solution)/shard_map/ppermute | solution.py:266
  14.8 0.0 copy-done.3
  14.8 5.7 %shard_map.67 = (bf16[3,384,256]{2,1,0:T(8,128)(2,1)S(1)}, bf16[32,28,128]{2,1,0:T(8,128)(2,1)S(1)}, bf16[32,28,128]{2,1,0:T(8,128)(2,1)S(1)}, bf16[32,72,128]{2,1,0:T(8,128)(2,1)S(1)}) custom-call(s32[2]{0:T(128)S(1)} %compare_select_fusion.scalars, bf16[1088,128]{1,0:T(8,128)(2,1)S(1)} %collective-permute-done.below, ...), custom_call_target="tpu_custom_call" | custom-call | flops 4000000000 | bytes 8000000 | tf_op jit(solution)/shard_map/pallas_call | solution.py:276
  20.5 0.0 copy-start
  20.6 0.8 copy-done
  21.4 0.0 copy-start.2
  21.4 0.7 copy-done.2
  22.1 0.0 copy-start.4
  22.1 0.8 copy-done.4
  22.9 3.6 %collective-permute-start.2 = (bf16[32,28,128]{2,1,0:T(8,128)(2,1)S(1)}, bf16[32,28,128]{2,1,0:T(8,128)(2,1)S(1)}, u32[]{:S(2)}, u32[]{:S(2)}) collective-permute-start(bf16[32,28,128]{2,1,0:T(8,128)(2,1)S(1)} %get-tuple-element.10), channel_id=1, source_target_pairs={{0,1},{1,0},{2,3},{3,2},{4,5},{5,4},{6,7},{7,6},{8,9},{9,8},{10,11... | collective-permute-start | bytes 688136 | tf_op jit(solution)/shard_map/ppermute | solution.py:299
  26.6 1.1 %collective-permute-done.2.got = bf16[32,28,128]{2,1,0:T(8,128)(2,1)S(1)} collective-permute-done((bf16[32,28,128]{2,1,0:T(8,128)(2,1)S(1)}, bf16[32,28,128]{2,1,0:T(8,128)(2,1)S(1)}, u32[]{:S(2)}, u32[]{:S(2)}) %collective-permute-start.2) | collective-permute-done | bytes 229408 | tf_op jit(solution)/shard_map/ppermute | solution.py:299
  27.7 0.0 copy-start.6
  27.7 0.7 copy-done.6
  28.4 2.2 %shard_map.69 = bf16[32,100,128]{2,1,0:T(8,128)(2,1)} custom-call(bf16[32,72,128]{2,1,0:T(8,128)(2,1)} %copy-done, bf16[32,28,128]{2,1,0:T(8,128)(2,1)} %copy-done.2, bf16[32,28,128]{2,1,0:T(8,128)(2,1)} %copy-done.6), custom_call_target="tpu_custom_call" | custom-call | flops 1000000 | bytes 2000000 | tf_op jit(solution)/shard_map/pallas_call | solution.py:300
  30.6 9.7 %all-to-all-start = ((bf16[32,100,128]{2,1,0:T(8,128)(2,1)}), bf16[32,100,128]{2,1,0:T(8,128)(2,1)S(1)}, u32[]{:S(2)}, u32[]{:S(2)}) async-start(bf16[32,100,128]{2,1,0:T(8,128)(2,1)} %shard_map.69), calls=%async_computation | async-start | bytes 1703936 | tf_op jit(solution)/shard_map/all_to_all | solution.py:248
  40.3 0.0 copy-start.1
  40.3 0.0 copy-start.5
  40.3 22.5 %all-to-all-done = bf16[32,100,128]{2,1,0:T(8,128)(2,1)S(1)} async-done(((bf16[32,100,128]{2,1,0:T(8,128)(2,1)}), bf16[32,100,128]{2,1,0:T(8,128)(2,1)S(1)}, u32[]{:S(2)}, u32[]{:S(2)}) %all-to-all-start) | async-done | bytes 819232 | tf_op jit(solution)/shard_map/all_to_all | solution.py:248
  62.8 0.1 convert_reduce_fusion
  63.1 19.0 %all_to_all.15 = bf16[16,40,128]{2,1,0:T(8,128)(2,1)S(1)} all-to-all(bf16[16,40,128]{2,1,0:T(8,128)(2,1)S(1)} %fusion.1), channel_id=1, replica_groups=mesh['sample'=32,'space'=16] {'space'}, dimensions={0} | all-to-all | bytes 327680 | tf_op jit(solution)/shard_map/all_to_all | solution.py:248
  82.2 0.9 broadcast_in_dim.40
  83.1 4.9 %all-to-all-start.2 = ((bf16[32,72,128]{2,1,0:T(8,128)(2,1)}), bf16[32,72,128]{2,1,0:T(8,128)(2,1)S(1)}, u32[]{:S(2)}, u32[]{:S(2)}) async-start(bf16[32,72,128]{2,1,0:T(8,128)(2,1)} %broadcast_in_dim.40), calls=%async_computation.2 | async-start | bytes 1179648 | tf_op jit(solution)/shard_map/all_to_all | solution.py:248
  87.9 0.0 copy-done.1
  87.9 0.0 copy-done.5
  87.9 0.5 shard_map.68
  88.4 0.9 copy.42
  89.3 17.1 %all-to-all-done.2 = bf16[32,72,128]{2,1,0:T(8,128)(2,1)S(1)} async-done(((bf16[32,72,128]{2,1,0:T(8,128)(2,1)}), bf16[32,72,128]{2,1,0:T(8,128)(2,1)S(1)}, u32[]{:S(2)}, u32[]{:S(2)}) %all-to-all-start.2) | async-done | bytes 589856 | tf_op jit(solution)/shard_map/all_to_all | solution.py:248
  106.5 0.1 fusion.7
  106.7 0.8 slice.49
  107.5 0.7 pad.26
  (20 shorter events, 0.3 us)
Async XLA Ops:
  0.6 14.2 %copy-start.3 = (bf16[27,128,256]{2,1,0:T(8,128)(2,1)S(1)}, bf16[27,128,256]{2,1,0:T(8,128)(2,1)}, u32[]{:S(2)}) copy-start(bf16[27,128,256]{2,1,0:T(8,128)(2,1)} %param.7) | copy-start | bytes 5308420
  2.5 10.1 %collective-permute-start.1 = (bf16[1088,128]{1,0:T(8,128)(2,1)S(1)}, bf16[1088,128]{1,0:T(8,128)(2,1)S(1)}, u32[]{:S(2)}, u32[]{:S(2)}) collective-permute-start(bf16[1088,128]{1,0:T(8,128)(2,1)S(1)} %pad_maximum_fusion.own), channel_id=1, source_target_pairs={{0,15},{1,0},{2,1},{3,2},{4,3},{5,4},{6,5},{7,6},{8,7},{9,8},{10,9... | collective-permute-start | bytes 835592 | tf_op jit(solution)/shard_map/ppermute | solution.py:265
  9.4 5.4 %collective-permute-start = (bf16[1088,128]{1,0:T(8,128)(2,1)S(1)}, bf16[1088,128]{1,0:T(8,128)(2,1)S(1)}, u32[]{:S(2)}, u32[]{:S(2)}) collective-permute-start(bf16[1088,128]{1,0:T(8,128)(2,1)S(1)} %pad_maximum_fusion.own), channel_id=1, source_target_pairs={{0,1},{1,2},{2,3},{3,4},{4,5},{5,6},{6,7},{7,8},{8,9},{9,10},{10,1... | collective-permute-start | bytes 835592 | tf_op jit(solution)/shard_map/ppermute | solution.py:266
  20.5 0.8 copy-start
  21.4 0.7 copy-start.2
  22.1 0.8 copy-start.4
  22.9 4.8 %collective-permute-start.2 = (bf16[32,28,128]{2,1,0:T(8,128)(2,1)S(1)}, bf16[32,28,128]{2,1,0:T(8,128)(2,1)S(1)}, u32[]{:S(2)}, u32[]{:S(2)}) collective-permute-start(bf16[32,28,128]{2,1,0:T(8,128)(2,1)S(1)} %get-tuple-element.10), channel_id=1, source_target_pairs={{0,1},{1,0},{2,3},{3,2},{4,5},{5,4},{6,7},{7,6},{8,9},{9,8},{10,11... | collective-permute-start | bytes 688136 | tf_op jit(solution)/shard_map/ppermute | solution.py:299
  27.7 0.7 copy-start.6
  30.6 32.2 %all-to-all-start = ((bf16[32,100,128]{2,1,0:T(8,128)(2,1)}), bf16[32,100,128]{2,1,0:T(8,128)(2,1)S(1)}, u32[]{:S(2)}, u32[]{:S(2)}) async-start(bf16[32,100,128]{2,1,0:T(8,128)(2,1)} %shard_map.69), calls=%async_computation | async-start | bytes 1703936 | tf_op jit(solution)/shard_map/all_to_all | solution.py:248
  40.3 47.6 %copy-start.1 = (bf16[27,64,128]{2,1,0:T(8,128)(2,1)S(1)}, bf16[27,64,128]{2,1,0:T(8,128)(2,1)}, u32[]{:S(2)}) copy-start(bf16[27,64,128]{2,1,0:T(8,128)(2,1)} %first_weight.1) | copy-start | bytes 1327108
  40.3 47.6 %copy-start.5 = (bf16[3,384,256]{2,1,0:T(8,128)(2,1)S(1)}, bf16[3,384,256]{2,1,0:T(8,128)(2,1)}, u32[]{:S(2)}) copy-start(bf16[3,384,256]{2,1,0:T(8,128)(2,1)} %copy-done.4) | copy-start | bytes 1769476
  83.1 23.4 %all-to-all-start.2 = ((bf16[32,72,128]{2,1,0:T(8,128)(2,1)}), bf16[32,72,128]{2,1,0:T(8,128)(2,1)S(1)}, u32[]{:S(2)}, u32[]{:S(2)}) async-start(bf16[32,72,128]{2,1,0:T(8,128)(2,1)} %broadcast_in_dim.40), calls=%async_computation.2 | async-start | bytes 1179648 | tf_op jit(solution)/shard_map/all_to_all | solution.py:248

commit v5 on v4

--- a/solution.py
+++ b/solution.py
@@ -57,18 +57,10 @@
 
 
 def main_kernel(
-    scalars, below, own, above, flipped, second_hbm,
-    stacks_ref, kept_ref, sent_ref, second_ref,
-    blocks, taps, grads, second_weight, sems,
+    scalars, below, own, above, flipped, second_weight,
+    stacks_ref, kept_ref, sent_ref, fields_ref, ordered_ref,
+    blocks, taps, grads,
 ):
-    copies = []
-    for a in range(3):
-        size = second_weight.shape[1]
-        start = 3 * a * size // 2 + size // 2
-        copies.append(
-            pltpu.make_async_copy(second_hbm.at[start : start + size], second_weight.at[a], sems.at[a])
-        )
-        copies[a].start()
     parity, inside = scalars[0], scalars[1] > 0
     chan_in, cells = 64, 128
     group = 9 * chan_in
@@ -131,8 +123,8 @@
                     )
     pre = None
     for a in range(3):
-        copies[a].wait()
-        term = dot(taps[:, 6 * a * chan : 6 * (a + 1) * chan], second_weight[a])
+        rows = second_weight[(9 * a + 3) * chan : 9 * (a + 1) * chan, :]
+        term = dot(taps[:, 6 * a * chan : 6 * (a + 1) * chan], rows)
         pre = term if pre is None else pre + term
     ended = cotangent * gradient_silu(pre)
     delta = jnp.concatenate([ended[:quarter], jnp.where(inside, ended[quarter:], 0.0)], 0).T
@@ -146,8 +138,9 @@
         total = None
         for a, i in pairs:
             for be in range(6):
+                start = (9 * a + 3 + be) * chan
                 term = dot(
-                    second_weight[a, be * chan : (be + 1) * chan, :],
+                    second_weight[start : start + chan, :],
                     spread[:, (6 * i + be) * lanes : (6 * i + be + 1) * lanes],
                 )
                 total = term if total is None else total + term
@@ -193,11 +186,17 @@
         kept_ref[m] = jnp.where(parity == 0, lower, upper).astype(BF)
         sent_ref[m] = jnp.where(parity == 0, upper, lower).astype(BF)
     share = 9 * chan
-    fields = taps[:, pl.ds(pl.multiple_of(parity * share, 128), share)]
-    ordered = dot(ended.astype(BF), picker(256, 256, reorder_test)).astype(BF)
+    fields_ref[...] = taps[:, pl.ds(pl.multiple_of(parity * share, 128), share)]
+    ordered_ref[...] = dot(ended.astype(BF), picker(256, 256, reorder_test)).astype(BF)
+
+
+def middle_kernel(stacks, first_weight, fields, ordered, volume_ref, second_ref):
+    chan_in, cells = volume_ref.shape[2:]
+    chan = fields.shape[1] // 9
     second = lax.dot_general(
-        ordered, fields, (((0,), (0,)), ((), ())), preferred_element_type=F32
+        ordered[...], fields[...], (((0,), (0,)), ((), ())), preferred_element_type=F32
     ).astype(BF)
+    samples_n = second_ref.shape[0]
     per = 32 // samples_n
     for piece in range(32):
         m, at = piece // per, piece % per * 72
@@ -209,10 +208,6 @@
                 begin : begin + count, lane * chan : (lane + 1) * chan
             ]
             at += count
-
-
-def volume_kernel(stacks, first_weight, volume_ref):
-    chan_in, cells = volume_ref.shape[2:]
 
     def filters(a):
         return [
@@ -273,43 +268,45 @@
     size = 14 * chan_in // samples_n
     per = 32 // samples_n
     vmem = pl.BlockSpec(memory_space=pltpu.VMEM)
-    stacks, kept, sent, second = pl.pallas_call(
+    stacks, kept, sent, fields, ordered = pl.pallas_call(
         main_kernel,
         out_shape=(
             jax.ShapeDtypeStruct((3, 3 * chan_mid, 2 * length), BF),
             jax.ShapeDtypeStruct((samples_n, size, chan_mid), BF),
             jax.ShapeDtypeStruct((samples_n, size, chan_mid), BF),
-            jax.ShapeDtypeStruct((samples_n, per * 72, chan_mid), BF),
+            jax.ShapeDtypeStruct((2 * quarter, 9 * chan_mid), BF),
+            jax.ShapeDtypeStruct((2 * quarter, chan_out), BF),
         ),
         in_specs=[pl.BlockSpec(memory_space=pltpu.SMEM)]
-        + [vmem] * 4
-        + [pl.BlockSpec(memory_space=pl.ANY)],
+        + [vmem] * 5,
         scratch_shapes=[
             pltpu.VMEM((11 * 9 * chan_in, rows * half), BF),
             pltpu.VMEM((2 * quarter, 18 * chan_mid), BF),
             pltpu.VMEM((28 * chan_in, chan_mid), F32),
-            pltpu.VMEM((3, 6 * chan_mid, chan_out), BF),
-            pltpu.SemaphoreType.DMA((3,)),
         ],
-        compiler_params=pltpu.CompilerParams(vmem_limit_bytes=24 << 20),
+        compiler_params=pltpu.CompilerParams(vmem_limit_bytes=16 << 20),
         cost_estimate=pl.CostEstimate(
             flops=4_000_000_000, bytes_accessed=8_000_000, transcendentals=0
         ),
     )(scalars, below, own, above, flipped, flat_second)
     got = lax.ppermute(sent, "space", [(i, i ^ 1) for i in range(groups)])
+    volume, second = pl.pallas_call(
+        middle_kernel,
+        out_shape=(
+            jax.ShapeDtypeStruct((planes, height, chan_in, length), BF),
+            jax.ShapeDtypeStruct((samples_n, per * 72, chan_mid), BF),
+        ),
+        compiler_params=pltpu.CompilerParams(vmem_limit_bytes=8 << 20),
+        cost_estimate=pl.CostEstimate(
+            flops=1_000_000_000, bytes_accessed=2_000_000, transcendentals=0
+        ),
+    )(stacks, first_weight, fields, ordered)
     payload = pl.pallas_call(
         pack_kernel,
         out_shape=jax.ShapeDtypeStruct((samples_n, per * 72 + size, chan_mid), BF),
+        compiler_params=pltpu.CompilerParams(vmem_limit_bytes=8 << 20),
         cost_estimate=pl.CostEstimate(flops=1_000_000, bytes_accessed=2_000_000, transcendentals=0),
     )(second, kept, got)
-    volume = pl.pallas_call(
-        volume_kernel,
-        out_shape=jax.ShapeDtypeStruct((planes, height, chan_in, length), BF),
-        compiler_params=pltpu.CompilerParams(vmem_limit_bytes=24 << 20),
-        cost_estimate=pl.CostEstimate(
-            flops=1_000_000_000, bytes_accessed=2_000_000, transcendentals=0
-        ),
-    )(stacks, first_weight)
     input_grad = volume.transpose(2, 0, 1, 3)[None]
     chunk = jnp.sum(exchanged(payload, "sample").astype(F32), 0)
     first_chunk = jnp.broadcast_to(chunk[None, per * 72 :], (groups, size, chan_mid))

time: 109 us -> 103 us (0.945)
  local copies, waits for them, and re-layouts: 8.91 us -> 5.86 us
  Pallas kernels: 8.38 us -> 6.12 us
    unnamed x18 -> x8, local copies, waits for them, and re-layouts: 3.99 us -> 0.94 us
    pallas_call x1, Pallas kernels: 5.69 us -> 4.46 us  [shards(): pl.pallas_call(main_kernel, out_shape=(jax.ShapeDtypeStruct((3, 3 * chan_...]
    pallas_call x1, Pallas kernels: 2.21 us -> 1.01 us  [shards(): pl.pallas_call(pack_kernel, out_shape=jax.ShapeDtypeStruct((samples_n, pe...]
  transfers between devices with their start and end apart: 5 -> 5, of which waited for: 4 -> 4; matrix products, arithmetic and copies ran while one was open for 2% -> 2% of each run, Pallas kernels for 0% -> 1%
where the time goes in v5:
time: 103 us
  waiting for transfers between devices  42.8 us (42%)
  starting transfers between devices  27 us (26%)
  blocking collectives  19 us (18%)
  Pallas kernels  6.12 us (6%)
  local copies, waits for them, and re-layouts  5.86 us (6%)
    all_to_all x2, waiting for transfers between devices, exchanged(): return lax.all_to_all(parts, axis, split_axis=0, concat_axis=0, tiled=True)  40.1 us
    all_to_all x1, blocking collectives, exchanged(): return lax.all_to_all(parts, axis, split_axis=0, concat_axis=0, tiled=True)  19 us
    all_to_all x2, starting transfers between devices, exchanged(): return lax.all_to_all(parts, axis, split_axis=0, concat_axis=0, tiled=True)  14.5 us
    ppermute x1, starting transfers between devices, shards(): lax.ppermute(own, 'space', [(i, (i - 1) % groups) for i in range(groups)])  6.89 us
    pallas_call x1, Pallas kernels, shards(): pl.pallas_call(main_kernel, out_shape=(jax.ShapeDtypeStruct((3, 3 * chan_...  4.46 us
    ppermute x1, starting transfers between devices, shards(): got = lax.ppermute(sent, 'space', [(i, i ^ 1) for i in range(groups)])  3.66 us
    ppermute x1, waiting for transfers between devices, shards(): below = lax.ppermute(own, 'space', [(i, i + 1) for i in range(groups - 1)])  2.24 us
  transfers between devices with their start and end apart: 5, of which 4 were waited for; matrix products, arithmetic and copies ran while one was open for 2% of the time, Pallas kernels for 1%

profile of v5, /device:TPU:1, one launch (start us, length us, event | category | flops | bytes accessed | tf_op | source)
XLA Modules:
  0.0 102.7 jit_solution(15648254135986021149)
XLA Ops:
  0.6 0.0 copy-start.1
  0.6 1.1 %copy.37 = bf16[4,4,64,128]{3,2,1,0:T(8,128)(2,1)S(1)} copy(bf16[4,4,64,128]{3,1,0,2:T(4,128)(2,1)} %bitcast.55) | data formatting | bytes 524288 | tf_op jit(solution)/shard_map/transpose | solution.py:257
  1.8 0.7 pad_maximum_fusion.own
  2.5 6.9 %collective-permute-start.1 = (bf16[1088,128]{1,0:T(8,128)(2,1)S(1)}, bf16[1088,128]{1,0:T(8,128)(2,1)S(1)}, u32[]{:S(2)}, u32[]{:S(2)}) collective-permute-start(bf16[1088,128]{1,0:T(8,128)(2,1)S(1)} %pad_maximum_fusion.own), channel_id=1, source_target_pairs={{0,15},{1,0},{2,1},{3,2},{4,3},{5,4},{6,5},{7,6},{8,7},{9,8},{10,9... | collective-permute-start | bytes 835592 | tf_op jit(solution)/shard_map/ppermute | solution.py:260
  9.4 1.9 %collective-permute-start = (bf16[1088,128]{1,0:T(8,128)(2,1)S(1)}, bf16[1088,128]{1,0:T(8,128)(2,1)S(1)}, u32[]{:S(2)}, u32[]{:S(2)}) collective-permute-start(bf16[1088,128]{1,0:T(8,128)(2,1)S(1)} %pad_maximum_fusion.own), channel_id=1, source_target_pairs={{0,1},{1,2},{2,3},{3,4},{4,5},{5,6},{6,7},{7,8},{8,9},{9,10},{10,1... | collective-permute-start | bytes 835592 | tf_op jit(solution)/shard_map/ppermute | solution.py:261
  11.4 1.2 %copy.38 = bf16[1728,128]{0,1:T(8,128)(2,1)S(1)} copy(bf16[1728,128]{1,0:T(8,128)(2,1)} %bitcast.46) | data formatting | bytes 884736 | tf_op jit(solution)/shard_map/reshape | solution.py:262
  12.6 0.0 collective-permute-done.1.above
  12.6 2.2 %collective-permute-done.below = bf16[1088,128]{1,0:T(8,128)(2,1)S(1)} collective-permute-done((bf16[1088,128]{1,0:T(8,128)(2,1)S(1)}, bf16[1088,128]{1,0:T(8,128)(2,1)S(1)}, u32[]{:S(2)}, u32[]{:S(2)}) %collective-permute-start) | collective-permute-done | bytes 278560 | tf_op jit(solution)/shard_map/ppermute | solution.py:261
  14.8 0.0 copy-done.1
  14.8 0.0 copy-start
  14.9 4.5 %shard_map.67 = (bf16[3,384,256]{2,1,0:T(8,128)(2,1)S(1)}, bf16[32,28,128]{2,1,0:T(8,128)(2,1)S(1)}, bf16[32,28,128]{2,1,0:T(8,128)(2,1)S(1)}, bf16[64,1152]{1,0:T(8,128)(2,1)S(1)}, bf16[64,256]{1,0:T(8,128)(2,1)S(1)}) custom-call(s32[2]{0:T(128)S(1)} %compare_select_fusion.scalars, bf16[1088,128]{1,0:T(8,128)(2,1)S(1)} %collective-permute-done.below, ...), custom_call_target="tpu_custom_call" | custom-call | flops 4000000000 | bytes 8000000 | tf_op jit(solution)/shard_map/pallas_call | solution.py:271
  19.3 3.7 %collective-permute-start.2 = (bf16[32,28,128]{2,1,0:T(8,128)(2,1)S(1)}, bf16[32,28,128]{2,1,0:T(8,128)(2,1)S(1)}, u32[]{:S(2)}, u32[]{:S(2)}) collective-permute-start(bf16[32,28,128]{2,1,0:T(8,128)(2,1)S(1)} %get-tuple-element.16), channel_id=1, source_target_pairs={{0,1},{1,0},{2,3},{3,2},{4,5},{5,4},{6,7},{7,6},{8,9},{9,8},{10,11... | collective-permute-start | bytes 688136 | tf_op jit(solution)/shard_map/ppermute | solution.py:292
  23.0 0.0 copy-done
  23.0 0.6 shard_map.68
  23.7 0.5 collective-permute-done.2.got
  24.1 1.0 shard_map.69
  25.1 9.7 %all-to-all-start = ((bf16[32,100,128]{2,1,0:T(8,128)(2,1)}), bf16[32,100,128]{2,1,0:T(8,128)(2,1)S(1)}, u32[]{:S(2)}, u32[]{:S(2)}) async-start(bf16[32,100,128]{2,1,0:T(8,128)(2,1)} %shard_map.69), calls=%async_computation | async-start | bytes 1703936 | tf_op jit(solution)/shard_map/all_to_all | solution.py:243
  34.8 22.5 %all-to-all-done = bf16[32,100,128]{2,1,0:T(8,128)(2,1)S(1)} async-done(((bf16[32,100,128]{2,1,0:T(8,128)(2,1)}), bf16[32,100,128]{2,1,0:T(8,128)(2,1)S(1)}, u32[]{:S(2)}, u32[]{:S(2)}) %all-to-all-start) | async-done | bytes 819232 | tf_op jit(solution)/shard_map/all_to_all | solution.py:243
  57.3 0.1 convert_reduce_fusion
  57.6 19.0 %all_to_all.15 = bf16[16,40,128]{2,1,0:T(8,128)(2,1)S(1)} all-to-all(bf16[16,40,128]{2,1,0:T(8,128)(2,1)S(1)} %fusion.1), channel_id=1, replica_groups=mesh['sample'=32,'space'=16] {'space'}, dimensions={0} | all-to-all | bytes 327680 | tf_op jit(solution)/shard_map/all_to_all | solution.py:243
  76.7 0.9 broadcast_in_dim.40
  77.6 4.9 %all-to-all-start.2 = ((bf16[32,72,128]{2,1,0:T(8,128)(2,1)}), bf16[32,72,128]{2,1,0:T(8,128)(2,1)S(1)}, u32[]{:S(2)}, u32[]{:S(2)}) async-start(bf16[32,72,128]{2,1,0:T(8,128)(2,1)} %broadcast_in_dim.40), calls=%async_computation.2 | async-start | bytes 1179648 | tf_op jit(solution)/shard_map/all_to_all | solution.py:243
  82.4 0.9 copy.42
  83.4 17.6 %all-to-all-done.2 = bf16[32,72,128]{2,1,0:T(8,128)(2,1)S(1)} async-done(((bf16[32,72,128]{2,1,0:T(8,128)(2,1)}), bf16[32,72,128]{2,1,0:T(8,128)(2,1)S(1)}, u32[]{:S(2)}, u32[]{:S(2)}) %all-to-all-start.2) | async-done | bytes 589856 | tf_op jit(solution)/shard_map/all_to_all | solution.py:243
  101.0 0.1 fusion.7
  101.2 0.8 slice.49
  102.0 0.7 pad.26
  (20 shorter events, 0.3 us)
Async XLA Ops:
  0.6 14.2 %copy-start.1 = (bf16[27,128,256]{2,1,0:T(8,128)(2,1)S(1)}, bf16[27,128,256]{2,1,0:T(8,128)(2,1)}, u32[]{:S(2)}) copy-start(bf16[27,128,256]{2,1,0:T(8,128)(2,1)} %param.7) | copy-start | bytes 5308420
  2.5 10.1 %collective-permute-start.1 = (bf16[1088,128]{1,0:T(8,128)(2,1)S(1)}, bf16[1088,128]{1,0:T(8,128)(2,1)S(1)}, u32[]{:S(2)}, u32[]{:S(2)}) collective-permute-start(bf16[1088,128]{1,0:T(8,128)(2,1)S(1)} %pad_maximum_fusion.own), channel_id=1, source_target_pairs={{0,15},{1,0},{2,1},{3,2},{4,3},{5,4},{6,5},{7,6},{8,7},{9,8},{10,9... | collective-permute-start | bytes 835592 | tf_op jit(solution)/shard_map/ppermute | solution.py:260
  9.4 5.4 %collective-permute-start = (bf16[1088,128]{1,0:T(8,128)(2,1)S(1)}, bf16[1088,128]{1,0:T(8,128)(2,1)S(1)}, u32[]{:S(2)}, u32[]{:S(2)}) collective-permute-start(bf16[1088,128]{1,0:T(8,128)(2,1)S(1)} %pad_maximum_fusion.own), channel_id=1, source_target_pairs={{0,1},{1,2},{2,3},{3,4},{4,5},{5,6},{6,7},{7,8},{8,9},{9,10},{10,1... | collective-permute-start | bytes 835592 | tf_op jit(solution)/shard_map/ppermute | solution.py:261
  14.8 8.1 %copy-start = (bf16[27,64,128]{2,1,0:T(8,128)(2,1)S(1)}, bf16[27,64,128]{2,1,0:T(8,128)(2,1)}, u32[]{:S(2)}) copy-start(bf16[27,64,128]{2,1,0:T(8,128)(2,1)} %first_weight.1) | copy-start | bytes 1327108
  19.3 4.8 %collective-permute-start.2 = (bf16[32,28,128]{2,1,0:T(8,128)(2,1)S(1)}, bf16[32,28,128]{2,1,0:T(8,128)(2,1)S(1)}, u32[]{:S(2)}, u32[]{:S(2)}) collective-permute-start(bf16[32,28,128]{2,1,0:T(8,128)(2,1)S(1)} %get-tuple-element.16), channel_id=1, source_target_pairs={{0,1},{1,0},{2,3},{3,2},{4,5},{5,4},{6,7},{7,6},{8,9},{9,8},{10,11... | collective-permute-start | bytes 688136 | tf_op jit(solution)/shard_map/ppermute | solution.py:292
  25.1 32.2 %all-to-all-start = ((bf16[32,100,128]{2,1,0:T(8,128)(2,1)}), bf16[32,100,128]{2,1,0:T(8,128)(2,1)S(1)}, u32[]{:S(2)}, u32[]{:S(2)}) async-start(bf16[32,100,128]{2,1,0:T(8,128)(2,1)} %shard_map.69), calls=%async_computation | async-start | bytes 1703936 | tf_op jit(solution)/shard_map/all_to_all | solution.py:243
  77.6 23.4 %all-to-all-start.2 = ((bf16[32,72,128]{2,1,0:T(8,128)(2,1)}), bf16[32,72,128]{2,1,0:T(8,128)(2,1)S(1)}, u32[]{:S(2)}, u32[]{:S(2)}) async-start(bf16[32,72,128]{2,1,0:T(8,128)(2,1)} %broadcast_in_dim.40), calls=%async_computation.2 | async-start | bytes 1179648 | tf_op jit(solution)/shard_map/all_to_all | solution.py:243

commit v6 on v5

--- a/solution.py
+++ b/solution.py
@@ -56,10 +56,9 @@
     return ((r >> 4) == (c & 15)) & ((r & 15) == (c >> 4))
 
 
-def main_kernel(
+def forward_kernel(
     scalars, below, own, above, flipped, second_weight,
-    stacks_ref, kept_ref, sent_ref, fields_ref, ordered_ref,
-    blocks, taps, grads,
+    pre_ref, delta_ref, kept_ref, sent_ref, blocks, taps,
 ):
     parity, inside = scalars[0], scalars[1] > 0
     chan_in, cells = 64, 128
@@ -129,6 +128,25 @@
     ended = cotangent * gradient_silu(pre)
     delta = jnp.concatenate([ended[:quarter], jnp.where(inside, ended[quarter:], 0.0)], 0).T
     delta = delta.astype(BF)
+    delta_ref[...] = delta
+    for h in range(3):
+        pre_ref[h] = pres[h + 1]
+    share = 5 * chan
+    ordered = dot(ended.astype(BF), picker(256, 256, reorder_test)).astype(BF)
+    for ref, end in ((kept_ref, scalars[2]), (sent_ref, 1 - scalars[2])):
+        start = pl.multiple_of((9 * parity + 4 * end) * chan, 128)
+        ref[:, :share] = taps[:, pl.ds(start, share)]
+        ref[:, share:] = ordered
+
+
+def backward_kernel(
+    scalars, below, own, delta_ref, pre_ref, first_weight, second_weight,
+    volume_ref, kept_ref, sent_ref, grads,
+):
+    parity = scalars[0]
+    chan_in, cells = 64, 128
+    chan = pre_ref.shape[1]
+    delta = delta_ref[...]
     up_first = picker(128, 768, up_first_test)
     up_second = picker(64, 1536, up_second_test)
     spread = dot(delta, up_second).astype(BF)
@@ -144,7 +162,7 @@
                     spread[:, (6 * i + be) * lanes : (6 * i + be + 1) * lanes],
                 )
                 total = term if total is None else total + term
-        deltas.append((total * gradient_silu(pres[h + 1])).astype(BF))
+        deltas.append((total * gradient_silu(pre_ref[h])).astype(BF))
     raised = dot(jnp.concatenate(deltas, 0), up_first).astype(BF)
     wide = 2 * cells
     stacks = [
@@ -154,8 +172,27 @@
         for h in range(3)
     ]
 
-    for h in range(3):
-        stacks_ref[h] = stacks[h]
+    def filters(a):
+        return [
+            jnp.concatenate([first_weight[9 * a + 3 * b + e] for e in range(3)], 1) for b in range(3)
+        ]
+
+    totals = {}
+    for h, chosen in enumerate(((1, 2), (0, 1, 2), (0,))):
+        left = jnp.concatenate(sum([filters(a) for a in chosen], []), 0)
+        result = dot(left, stacks[h])
+        for place, a in enumerate(chosen):
+            p = 2 * h + a - 1
+            for b in range(3):
+                for j in range(2):
+                    r = 2 * j + b - 1
+                    if r < 0:
+                        continue
+                    start = (3 * place + b) * chan_in
+                    term = result[start : start + chan_in, j * cells : (j + 1) * cells]
+                    totals[p, r] = totals[p, r] + term if (p, r) in totals else term
+    for (p, r), total in totals.items():
+        volume_ref[p, r] = total.astype(BF)
 
     def plane(p, r):
         ref, start = (below, (12 + r) * chan_in) if p < 0 else (own, (4 * p + r) * chan_in)
@@ -185,58 +222,34 @@
         upper = grads[(2 * m + 1) * size : (2 * m + 2) * size, :]
         kept_ref[m] = jnp.where(parity == 0, lower, upper).astype(BF)
         sent_ref[m] = jnp.where(parity == 0, upper, lower).astype(BF)
-    share = 9 * chan
-    fields_ref[...] = taps[:, pl.ds(pl.multiple_of(parity * share, 128), share)]
-    ordered_ref[...] = dot(ended.astype(BF), picker(256, 256, reorder_test)).astype(BF)
-
-
-def middle_kernel(stacks, first_weight, fields, ordered, volume_ref, second_ref):
-    chan_in, cells = volume_ref.shape[2:]
-    chan = fields.shape[1] // 9
+
+
+def second_kernel(mine, theirs, second_ref):
+    chan = second_ref.shape[2]
+    share = 5 * chan
+    both = jnp.concatenate([mine[...], theirs[...]], 0)
     second = lax.dot_general(
-        ordered[...], fields[...], (((0,), (0,)), ((), ())), preferred_element_type=F32
+        both[:, share:], both[:, :share], (((0,), (0,)), ((), ())), preferred_element_type=F32
     ).astype(BF)
-    samples_n = second_ref.shape[0]
-    per = 32 // samples_n
+    per = 32 // second_ref.shape[0]
     for piece in range(32):
-        m, at = piece // per, piece % per * 72
+        m, at = piece // per, piece % per * 40
         first = piece // 2 * 16
-        for lane in range(4, 9) if piece % 2 else range(5):
-            begin = first + 8 if lane == 4 and piece % 2 else first
-            count = 8 if lane == 4 else 16
+        for lane in range(2, 5) if piece % 2 else range(3):
+            begin = first + 8 if lane == 2 and piece % 2 else first
+            count = 8 if lane == 2 else 16
             second_ref[m, at : at + count, :] = second[
                 begin : begin + count, lane * chan : (lane + 1) * chan
             ]
             at += count
 
-    def filters(a):
-        return [
-            jnp.concatenate([first_weight[9 * a + 3 * b + e] for e in range(3)], 1) for b in range(3)
-        ]
-
-    totals = {}
-    for h, chosen in enumerate(((1, 2), (0, 1, 2), (0,))):
-        left = jnp.concatenate(sum([filters(a) for a in chosen], []), 0)
-        result = dot(left, stacks[h])
-        for place, a in enumerate(chosen):
-            p = 2 * h + a - 1
-            for b in range(3):
-                for j in range(2):
-                    r = 2 * j + b - 1
-                    if r < 0:
-                        continue
-                    start = (3 * place + b) * chan_in
-                    term = result[start : start + chan_in, j * cells : (j + 1) * cells]
-                    totals[p, r] = totals[p, r] + term if (p, r) in totals else term
-    for (p, r), total in totals.items():
-        volume_ref[p, r] = total.astype(BF)
-
 
 def pack_kernel(second, kept, got, payload_ref):
     rows = second.shape[1]
-    for m in range(second.shape[0]):
+    for m in range(kept.shape[0]):
         payload_ref[m, :rows, :] = second[m]
-        payload_ref[m, rows:, :] = (kept[m].astype(F32) + got[m].astype(F32)).astype(BF)
+        total = kept[m].astype(F32) + got[m].astype(F32)
+        payload_ref[m, rows:, :] = total.astype(BF)
 
 
 def exchanged(parts, axis):
@@ -262,80 +275,97 @@
     flipped = first_weight.reshape(27 * chan_in, chan_mid).T
     flat_second = second_weight.reshape(27 * chan_mid, chan_out)
     place = lax.axis_index("space")
-    scalars = jnp.where(
-        jnp.arange(2) == 0, place % 2, jnp.where(place == groups - 1, 0, 1)
-    ).astype(jnp.int32)
+    marks = [place % 2, jnp.where(place == groups - 1, 0, 1), place // 2 % 2]
+    index = jnp.arange(3)
+    scalars = jnp.where(index == 0, marks[0], jnp.where(index == 1, marks[1], marks[2]))
+    scalars = scalars.astype(jnp.int32)
     size = 14 * chan_in // samples_n
     per = 32 // samples_n
+    smem = pl.BlockSpec(memory_space=pltpu.SMEM)
     vmem = pl.BlockSpec(memory_space=pltpu.VMEM)
-    stacks, kept, sent, fields, ordered = pl.pallas_call(
-        main_kernel,
+    swapped = jax.ShapeDtypeStruct((2 * quarter, 5 * chan_mid + chan_out), BF)
+    halved = jax.ShapeDtypeStruct((samples_n, size, chan_mid), BF)
+    pre, delta, mine, theirs = pl.pallas_call(
+        forward_kernel,
         out_shape=(
-            jax.ShapeDtypeStruct((3, 3 * chan_mid, 2 * length), BF),
-            jax.ShapeDtypeStruct((samples_n, size, chan_mid), BF),
-            jax.ShapeDtypeStruct((samples_n, size, chan_mid), BF),
-            jax.ShapeDtypeStruct((2 * quarter, 9 * chan_mid), BF),
-            jax.ShapeDtypeStruct((2 * quarter, chan_out), BF),
-        ),
-        in_specs=[pl.BlockSpec(memory_space=pltpu.SMEM)]
-        + [vmem] * 5,
+            jax.ShapeDtypeStruct((3, chan_mid, rows * half), F32),
+            jax.ShapeDtypeStruct((chan_out, 2 * quarter), BF),
+            swapped,
+            swapped,
+        ),
+        in_specs=[smem] + [vmem] * 5,
         scratch_shapes=[
             pltpu.VMEM((11 * 9 * chan_in, rows * half), BF),
             pltpu.VMEM((2 * quarter, 18 * chan_mid), BF),
-            pltpu.VMEM((28 * chan_in, chan_mid), F32),
         ],
         compiler_params=pltpu.CompilerParams(vmem_limit_bytes=16 << 20),
         cost_estimate=pl.CostEstimate(
-            flops=4_000_000_000, bytes_accessed=8_000_000, transcendentals=0
+            flops=2_000_000_000, bytes_accessed=5_000_000, transcendentals=0
         ),
     )(scalars, below, own, above, flipped, flat_second)
+    theirs = lax.ppermute(theirs, "space", [(i, i ^ 2) for i in range(groups)])
+    volume, kept, sent = pl.pallas_call(
+        backward_kernel,
+        out_shape=(
+            jax.ShapeDtypeStruct((planes, height, chan_in, length), BF), halved, halved
+        ),
+        in_specs=[smem] + [vmem] * 6,
+        scratch_shapes=[pltpu.VMEM((28 * chan_in, chan_mid), F32)],
+        compiler_params=pltpu.CompilerParams(vmem_limit_bytes=16 << 20),
+        cost_estimate=pl.CostEstimate(
+            flops=3_000_000_000, bytes_accessed=5_000_000, transcendentals=0
+        ),
+    )(scalars, below, own, delta, pre, first_weight, flat_second)
     got = lax.ppermute(sent, "space", [(i, i ^ 1) for i in range(groups)])
-    volume, second = pl.pallas_call(
-        middle_kernel,
-        out_shape=(
-            jax.ShapeDtypeStruct((planes, height, chan_in, length), BF),
-            jax.ShapeDtypeStruct((samples_n, per * 72, chan_mid), BF),
-        ),
+    second = pl.pallas_call(
+        second_kernel,
+        out_shape=jax.ShapeDtypeStruct((samples_n, per * 40, chan_mid), BF),
         compiler_params=pltpu.CompilerParams(vmem_limit_bytes=8 << 20),
         cost_estimate=pl.CostEstimate(
-            flops=1_000_000_000, bytes_accessed=2_000_000, transcendentals=0
-        ),
-    )(stacks, first_weight, fields, ordered)
+            flops=2_000_000_000, bytes_accessed=2_000_000, transcendentals=0
+        ),
+    )(mine, theirs)
     payload = pl.pallas_call(
         pack_kernel,
-        out_shape=jax.ShapeDtypeStruct((samples_n, per * 72 + size, chan_mid), BF),
+        out_shape=jax.ShapeDtypeStruct((samples_n, per * 40 + size, chan_mid), BF),
         compiler_params=pltpu.CompilerParams(vmem_limit_bytes=8 << 20),
-        cost_estimate=pl.CostEstimate(flops=1_000_000, bytes_accessed=2_000_000, transcendentals=0),
+        cost_estimate=pl.CostEstimate(
+            flops=50_000_000, bytes_accessed=2_000_000, transcendentals=0
+        ),
     )(second, kept, got)
     input_grad = volume.transpose(2, 0, 1, 3)[None]
     chunk = jnp.sum(exchanged(payload, "sample").astype(F32), 0)
-    first_chunk = jnp.broadcast_to(chunk[None, per * 72 :], (groups, size, chan_mid))
-    second_chunk = chunk[: per * 72].reshape(per, 72, chan_mid)
+    first_chunk = jnp.broadcast_to(chunk[None, per * 40 :], (groups, size, chan_mid))
+    second_chunk = chunk[: per * 40].reshape(per, 40, chan_mid)
     odd = (lax.axis_index("sample") * per + jnp.arange(per)) % 2 == 1
     second_chunk = jnp.where(
         odd[:, None, None],
         jnp.pad(second_chunk, ((0, 0), (8, 0), (0, 0))),
         jnp.pad(second_chunk, ((0, 0), (0, 8), (0, 0))),
     )
-    pieces = 5 * per
+    pieces = 3 * per
     second_chunk = second_chunk.reshape(pieces, groups, chan_mid).transpose(1, 0, 2)
     second_chunk = jnp.pad(second_chunk, ((0, 0), (0, -(size + pieces) % 8), (0, 0)))
     both = exchanged(jnp.concatenate([first_chunk, second_chunk], 1).astype(BF), "space")
-    both = jnp.sum(both.astype(F32).reshape(groups // 2, 2, -1, chan_mid), 0)
+    both = both.astype(F32)
+    first_chunk = jnp.sum(both[:, :size].reshape(groups // 2, 2, size, chan_mid), 0)
+    second_chunk = both[:, size : size + pieces].reshape(groups // 4, 4, pieces, chan_mid)
+    second_chunk = jnp.sum(second_chunk, 0)
     first_ext = planes // 2 * rows * half
     first_scale = 1.0 / math.sqrt(samples_n * groups * first_ext)
     second_scale = 1.0 / math.sqrt(samples_n * groups * (planes // 4) * (height // 4) * quarter)
-    first_chunk = both[:, :size].reshape(2 * size, chan_mid) * first_scale
-    second_chunk = both[:, size : size + pieces].reshape(2 * pieces, chan_mid) * second_scale
+    first_chunk = first_chunk.reshape(2 * size, chan_mid) * first_scale
+    second_chunk = second_chunk.reshape(4 * pieces, chan_mid) * second_scale
     both = jnp.concatenate([first_chunk, second_chunk], 0)
     both = jnp.pad(both, ((0, -both.shape[0] % 8), (0, 0)))
     final = everywhere(both.astype(BF), "sample")
     first_grad = final[:, : 2 * size].reshape(28, chan_in, chan_mid)[:27]
-    second = final[:, 2 * size : 2 * size + 2 * pieces].reshape(samples_n, 2, per, 5, chan_mid)
-    second = second.transpose(0, 2, 1, 3, 4).reshape(per_group, 2, 2, 5, chan_mid)
-    second = second.transpose(2, 1, 3, 0, 4)
-    shared = second[:, 0, 4:] + second[:, 1, :1]
-    second = jnp.concatenate([second[:, 0, :4], shared, second[:, 1, 1:]], 1)
+    second = final[:, 2 * size : 2 * size + 4 * pieces].reshape(samples_n, 2, 2, per, 3, chan_mid)
+    second = second.transpose(0, 3, 1, 2, 4, 5).reshape(per_group, 2, 2, 2, 3, chan_mid)
+    second = second.transpose(1, 4, 2, 3, 0, 5)
+    low, high = second[0], second[1]
+    blocks = [low[0], low[1], low[2] + high[0], high[1], high[2]]
+    second = jnp.stack([block[0] for block in blocks] + [block[1] for block in blocks[1:]], 1)
     second = second.reshape(3, 2, 3, per_group, chan_mid)
     second = jnp.pad(second, ((0, 0), (1, 0), (0, 0), (0, 0), (0, 0)))
     second_grad = second.reshape(27, per_group, chan_mid).transpose(0, 2, 1)

time: 103 us -> 101 us (0.981)
  waiting for transfers between devices: 42.8 us -> 38.3 us
  starting transfers between devices: 27 us -> 28.5 us
    all_to_all x2, waiting for transfers between devices: 40.1 us -> 35.2 us  [exchanged(): return lax.all_to_all(parts, axis, split_axis=0, concat_axis=0, tiled=True)]
    ppermute x0 -> x1, starting transfers between devices: none -> 1.92 us  [shards(): theirs = lax.ppermute(theirs, 'space', [(i, i ^ 2) for i in range(groups)])]
    all_to_all x2, starting transfers between devices: 14.5 us -> 13.1 us  [exchanged(): return lax.all_to_all(parts, axis, split_axis=0, concat_axis=0, tiled=True)]
    ppermute x1, starting transfers between devices: 3.66 us -> 4.74 us  [shards(): got = lax.ppermute(sent, 'space', [(i, i ^ 1) for i in range(groups)])]
    pallas_call x2 -> x3, Pallas kernels: 5.11 us -> 5.63 us  [the longest x1 3.05 us: shards(): pl.pallas_call(forward_kernel, out_shape=(jax.ShapeDtypeStruct((3, chan_m...]
  transfers between devices with their start and end apart: 5 -> 6, of which waited for: 4 -> 4; matrix products, arithmetic and copies ran while one was open for 2% -> 2% of each run, Pallas kernels for 1% -> 3%
where the time goes in v6:
time: 101 us; the launch traced here: 100 us
  waiting for transfers between devices  38.3 us (38%)
  starting transfers between devices  28.5 us (28%)
  blocking collectives  18.7 us (19%)
  Pallas kernels  6.54 us (6%)
  local copies, waits for them, and re-layouts  6.02 us (6%)
  other arithmetic  1.12 us (1%)
    all_to_all x2, waiting for transfers between devices, exchanged(): return lax.all_to_all(parts, axis, split_axis=0, concat_axis=0, tiled=True)  35.2 us
    all_to_all x1, blocking collectives, exchanged(): return lax.all_to_all(parts, axis, split_axis=0, concat_axis=0, tiled=True)  18.7 us
    all_to_all x2, starting transfers between devices, exchanged(): return lax.all_to_all(parts, axis, split_axis=0, concat_axis=0, tiled=True)  13.1 us
    ppermute x1, starting transfers between devices, shards(): lax.ppermute(own, 'space', [(i, (i - 1) % groups) for i in range(groups)])  6.89 us
    ppermute x1, starting transfers between devices, shards(): got = lax.ppermute(sent, 'space', [(i, i ^ 1) for i in range(groups)])  4.74 us
    pallas_call x1, Pallas kernels, shards(): pl.pallas_call(forward_kernel, out_shape=(jax.ShapeDtypeStruct((3, chan_m...  3.05 us
    pallas_call x1, Pallas kernels, shards(): pl.pallas_call(backward_kernel, out_shape=(jax.ShapeDtypeStruct((planes,...  2.3 us
    ppermute x1, waiting for transfers between devices, shards(): below = lax.ppermute(own, 'space', [(i, i + 1) for i in range(groups - 1)])  2.21 us
  transfers between devices with their start and end apart: 6, of which 4 were waited for; matrix products, arithmetic and copies ran while one was open for 2% of the time, Pallas kernels for 3%

profile of v6, /device:TPU:1, one launch (start us, length us, event | category | flops | bytes accessed | tf_op | source)
XLA Modules:
  0.0 100.2 jit_solution(9067643936970757393)
XLA Ops:
  0.6 0.0 copy-start.1
  0.6 1.1 %copy.138 = bf16[4,4,64,128]{3,2,1,0:T(8,128)(2,1)S(1)} copy(bf16[4,4,64,128]{3,1,0,2:T(4,128)(2,1)} %bitcast.65) | data formatting | bytes 524288 | tf_op jit(solution)/shard_map/transpose | solution.py:270
  1.8 0.7 pad_maximum_fusion.own
  2.5 6.9 %collective-permute-start.1 = (bf16[1088,128]{1,0:T(8,128)(2,1)S(1)}, bf16[1088,128]{1,0:T(8,128)(2,1)S(1)}, u32[]{:S(2)}, u32[]{:S(2)}) collective-permute-start(bf16[1088,128]{1,0:T(8,128)(2,1)S(1)} %pad_maximum_fusion.own), channel_id=1, source_target_pairs={{0,15},{1,0},{2,1},{3,2},{4,3},{5,4},{6,5},{7,6},{8,7},{9,8},{10,9... | collective-permute-start | bytes 835592 | tf_op jit(solution)/shard_map/ppermute | solution.py:273
  9.4 1.9 %collective-permute-start = (bf16[1088,128]{1,0:T(8,128)(2,1)S(1)}, bf16[1088,128]{1,0:T(8,128)(2,1)S(1)}, u32[]{:S(2)}, u32[]{:S(2)}) collective-permute-start(bf16[1088,128]{1,0:T(8,128)(2,1)S(1)} %pad_maximum_fusion.own), channel_id=1, source_target_pairs={{0,1},{1,2},{2,3},{3,4},{4,5},{5,6},{6,7},{7,8},{8,9},{9,10},{10,1... | collective-permute-start | bytes 835592 | tf_op jit(solution)/shard_map/ppermute | solution.py:274
  11.4 1.2 %copy.139 = bf16[1728,128]{0,1:T(8,128)(2,1)S(1)} copy(bf16[1728,128]{1,0:T(8,128)(2,1)} %bitcast.55) | data formatting | bytes 884736 | tf_op jit(solution)/shard_map/reshape | solution.py:275
  12.6 0.0 collective-permute-done.1.above
  12.6 2.2 %collective-permute-done.below = bf16[1088,128]{1,0:T(8,128)(2,1)S(1)} collective-permute-done((bf16[1088,128]{1,0:T(8,128)(2,1)S(1)}, bf16[1088,128]{1,0:T(8,128)(2,1)S(1)}, u32[]{:S(2)}, u32[]{:S(2)}) %collective-permute-start) | collective-permute-done | bytes 278560 | tf_op jit(solution)/shard_map/ppermute | solution.py:274
  14.8 0.0 copy-done.1
  14.8 0.0 copy-start
  14.9 3.1 %shard_map.67 = (f32[3,128,128]{2,1,0:T(8,128)S(1)}, bf16[256,64]{1,0:T(8,128)(2,1)S(1)}, bf16[64,896]{1,0:T(8,128)(2,1)S(1)}, bf16[64,896]{1,0:T(8,128)(2,1)S(1)}) custom-call(s32[3]{0:T(128)S(1)} %compare_select_fusion.1.scalars, bf16[1088,128]{1,0:T(8,128)(2,1)S(1)} %collective-permute-done.below, bf16[1088,128]{1,0:T(8,128)(2,1)S(1)} %pad_maximum_fusion.own, ...), custom_call_target="tpu_custom_call" | custom-call | flops 2000000000 | bytes 5000000 | tf_op jit(solution)/shard_map/pallas_call | solution.py:288
  17.9 1.9 %collective-permute-start.2 = (bf16[64,896]{1,0:T(8,128)(2,1)S(1)}, bf16[64,896]{1,0:T(8,128)(2,1)S(1)}, u32[]{:S(2)}, u32[]{:S(2)}) collective-permute-start(bf16[64,896]{1,0:T(8,128)(2,1)S(1)} %get-tuple-element.14), channel_id=1, source_target_pairs={{0,2},{1,3},{2,0},{3,1},{4,6},{5,7},{6,4},{7,5},{8,10},{9,11},{10,... | collective-permute-start | bytes 344072 | tf_op jit(solution)/shard_map/ppermute | solution.py:306
  19.8 0.0 copy-done
  19.9 2.3 %shard_map.68 = (bf16[4,4,64,128]{3,2,1,0:T(8,128)(2,1)S(1)}, bf16[32,28,128]{2,1,0:T(8,128)(2,1)S(1)}, bf16[32,28,128]{2,1,0:T(8,128)(2,1)S(1)}) custom-call(s32[3]{0:T(128)S(1)} %compare_select_fusion.1.scalars, bf16[1088,128]{1,0:T(8,128)(2,1)S(1)} %collective-permute-done.below, bf16[1088,128]{1,0:T(8,128)(2,1)S(1)} %pad_maximum_fusion.own, ...), custom_call_target="tpu_custom_call" | custom-call | flops 3000000000 | bytes 5000000 | tf_op jit(solution)/shard_map/pallas_call | solution.py:307
  22.2 4.7 %collective-permute-start.3 = (bf16[32,28,128]{2,1,0:T(8,128)(2,1)S(1)}, bf16[32,28,128]{2,1,0:T(8,128)(2,1)S(1)}, u32[]{:S(2)}, u32[]{:S(2)}) collective-permute-start(bf16[32,28,128]{2,1,0:T(8,128)(2,1)S(1)} %get-tuple-element.16), channel_id=1, source_target_pairs={{0,1},{1,0},{2,3},{3,2},{4,5},{5,4},{6,7},{7,6},{8,9},{9,8},{10,11... | collective-permute-start | bytes 688136 | tf_op jit(solution)/shard_map/ppermute | solution.py:319
  26.9 0.0 collective-permute-done.2.theirs
  26.9 0.3 shard_map.69.second
  27.2 0.8 collective-permute-done.3.got
  28.0 0.9 shard_map.70
  28.9 8.6 %all-to-all-start = ((bf16[32,68,128]{2,1,0:T(8,128)(2,1)}), bf16[32,68,128]{2,1,0:T(8,128)(2,1)S(1)}, u32[]{:S(2)}, u32[]{:S(2)}) async-start(bf16[32,68,128]{2,1,0:T(8,128)(2,1)} %shard_map.70), calls=%async_computation | async-start | bytes 1179648 | tf_op jit(solution)/shard_map/all_to_all | solution.py:256
  37.6 17.6 %all-to-all-done = bf16[32,68,128]{2,1,0:T(8,128)(2,1)S(1)} async-done(((bf16[32,68,128]{2,1,0:T(8,128)(2,1)}), bf16[32,68,128]{2,1,0:T(8,128)(2,1)S(1)}, u32[]{:S(2)}, u32[]{:S(2)}) %all-to-all-start) | async-done | bytes 557088 | tf_op jit(solution)/shard_map/all_to_all | solution.py:256
  55.2 0.1 convert_reduce_fusion
  55.4 18.7 %all_to_all.15 = bf16[16,32,128]{2,1,0:T(8,128)(2,1)S(1)} all-to-all(bf16[16,32,128]{2,1,0:T(8,128)(2,1)S(1)} %fusion.1), channel_id=1, replica_groups=mesh['sample'=32,'space'=16] {'space'}, dimensions={0} | all-to-all | bytes 262144 | tf_op jit(solution)/shard_map/all_to_all | solution.py:256
  74.2 0.1 reduce_sum.28
  74.4 0.9 broadcast_in_dim.45
  75.3 4.5 %all-to-all-start.2 = ((bf16[32,72,128]{2,1,0:T(8,128)(2,1)}), bf16[32,72,128]{2,1,0:T(8,128)(2,1)S(1)}, u32[]{:S(2)}, u32[]{:S(2)}) async-start(bf16[32,72,128]{2,1,0:T(8,128)(2,1)} %broadcast_in_dim.45), calls=%async_computation.2 | async-start | bytes 1179648 | tf_op jit(solution)/shard_map/all_to_all | solution.py:256
  79.8 0.9 copy.147
  80.7 17.6 %all-to-all-done.2 = bf16[32,72,128]{2,1,0:T(8,128)(2,1)S(1)} async-done(((bf16[32,72,128]{2,1,0:T(8,128)(2,1)}), bf16[32,72,128]{2,1,0:T(8,128)(2,1)S(1)}, u32[]{:S(2)}, u32[]{:S(2)}) %all-to-all-start.2) | async-done | bytes 589856 | tf_op jit(solution)/shard_map/all_to_all | solution.py:256
  98.3 0.1 slice_add_fusion
  98.4 0.1 fusion.6
  98.5 0.8 slice.111
  99.5 0.7 pad.26
  (31 shorter events, 0.4 us)
Async XLA Ops:
  0.6 14.2 %copy-start.1 = (bf16[27,128,256]{2,1,0:T(8,128)(2,1)S(1)}, bf16[27,128,256]{2,1,0:T(8,128)(2,1)}, u32[]{:S(2)}) copy-start(bf16[27,128,256]{2,1,0:T(8,128)(2,1)} %param.7) | copy-start | bytes 5308420
  2.5 10.1 %collective-permute-start.1 = (bf16[1088,128]{1,0:T(8,128)(2,1)S(1)}, bf16[1088,128]{1,0:T(8,128)(2,1)S(1)}, u32[]{:S(2)}, u32[]{:S(2)}) collective-permute-start(bf16[1088,128]{1,0:T(8,128)(2,1)S(1)} %pad_maximum_fusion.own), channel_id=1, source_target_pairs={{0,15},{1,0},{2,1},{3,2},{4,3},{5,4},{6,5},{7,6},{8,7},{9,8},{10,9... | collective-permute-start | bytes 835592 | tf_op jit(solution)/shard_map/ppermute | solution.py:273
  9.4 5.4 %collective-permute-start = (bf16[1088,128]{1,0:T(8,128)(2,1)S(1)}, bf16[1088,128]{1,0:T(8,128)(2,1)S(1)}, u32[]{:S(2)}, u32[]{:S(2)}) collective-permute-start(bf16[1088,128]{1,0:T(8,128)(2,1)S(1)} %pad_maximum_fusion.own), channel_id=1, source_target_pairs={{0,1},{1,2},{2,3},{3,4},{4,5},{5,6},{6,7},{7,8},{8,9},{9,10},{10,1... | collective-permute-start | bytes 835592 | tf_op jit(solution)/shard_map/ppermute | solution.py:274
  14.8 5.0 %copy-start = (bf16[27,64,128]{2,1,0:T(8,128)(2,1)S(1)}, bf16[27,64,128]{2,1,0:T(8,128)(2,1)}, u32[]{:S(2)}) copy-start(bf16[27,64,128]{2,1,0:T(8,128)(2,1)} %first_weight.1) | copy-start | bytes 1327108
  17.9 9.0 %collective-permute-start.2 = (bf16[64,896]{1,0:T(8,128)(2,1)S(1)}, bf16[64,896]{1,0:T(8,128)(2,1)S(1)}, u32[]{:S(2)}, u32[]{:S(2)}) collective-permute-start(bf16[64,896]{1,0:T(8,128)(2,1)S(1)} %get-tuple-element.14), channel_id=1, source_target_pairs={{0,2},{1,3},{2,0},{3,1},{4,6},{5,7},{6,4},{7,5},{8,10},{9,11},{10,... | collective-permute-start | bytes 344072 | tf_op jit(solution)/shard_map/ppermute | solution.py:306
  22.2 5.9 %collective-permute-start.3 = (bf16[32,28,128]{2,1,0:T(8,128)(2,1)S(1)}, bf16[32,28,128]{2,1,0:T(8,128)(2,1)S(1)}, u32[]{:S(2)}, u32[]{:S(2)}) collective-permute-start(bf16[32,28,128]{2,1,0:T(8,128)(2,1)S(1)} %get-tuple-element.16), channel_id=1, source_target_pairs={{0,1},{1,0},{2,3},{3,2},{4,5},{5,4},{6,7},{7,6},{8,9},{9,8},{10,11... | collective-permute-start | bytes 688136 | tf_op jit(solution)/shard_map/ppermute | solution.py:319
  28.9 26.2 %all-to-all-start = ((bf16[32,68,128]{2,1,0:T(8,128)(2,1)}), bf16[32,68,128]{2,1,0:T(8,128)(2,1)S(1)}, u32[]{:S(2)}, u32[]{:S(2)}) async-start(bf16[32,68,128]{2,1,0:T(8,128)(2,1)} %shard_map.70), calls=%async_computation | async-start | bytes 1179648 | tf_op jit(solution)/shard_map/all_to_all | solution.py:256
  75.3 23.0 %all-to-all-start.2 = ((bf16[32,72,128]{2,1,0:T(8,128)(2,1)}), bf16[32,72,128]{2,1,0:T(8,128)(2,1)S(1)}, u32[]{:S(2)}, u32[]{:S(2)}) async-start(bf16[32,72,128]{2,1,0:T(8,128)(2,1)} %broadcast_in_dim.45), calls=%async_computation.2 | async-start | bytes 1179648 | tf_op jit(solution)/shard_map/all_to_all | solution.py:256

commit v7 on v6

--- a/solution.py
+++ b/solution.py
@@ -252,6 +252,36 @@
         payload_ref[m, rows:, :] = total.astype(BF)
 
 
+def final_kernel(chunks, first_ref, second_ref):
+    taps, chan_in, chan = first_ref.shape
+    samples_n, rows = chunks.shape[0], chunks.shape[1] - 16
+    for m in range(samples_n):
+        at, stop = m * rows, min((m + 1) * rows, taps * chan_in)
+        while at < stop:
+            tap, channel = at // chan_in, at % chan_in
+            count = min(stop - at, chan_in - channel)
+            begin = 16 + at - m * rows
+            first_ref[tap, channel : channel + count, :] = chunks[m, begin : begin + count, :]
+            at += count
+    per_group = second_ref.shape[1]
+
+    def test(r, c):
+        tap, o = r >> 4, r & 15
+        q = jnp.where(tap >= 9, 1, 0)
+        w = jnp.where(tap - 9 * q >= 5, 1, 0)
+        block = tap - 9 * q - 4 * w - 2 * ((c >> 4) & 1)
+        right = (block >= 0) & (block <= 2) & ((c & 15) == 6 * w + 3 * q + block)
+        return right & ((c >> 5) == o)
+
+    parts = jnp.concatenate([chunks[m, :16, :] for m in range(samples_n)], 0)
+    live = dot(picker(18 * per_group, 16 * samples_n, test), parts).astype(BF)
+    for a in range(3):
+        for b in range(9):
+            tap = 6 * a + b - 3
+            value = live[tap * per_group : (tap + 1) * per_group]
+            second_ref[9 * a + b] = jnp.zeros((per_group, chan), BF) if b < 3 else value
+
+
 def exchanged(parts, axis):
     return lax.all_to_all(parts, axis, split_axis=0, concat_axis=0, tiled=True)
 
@@ -356,19 +386,20 @@
     second_scale = 1.0 / math.sqrt(samples_n * groups * (planes // 4) * (height // 4) * quarter)
     first_chunk = first_chunk.reshape(2 * size, chan_mid) * first_scale
     second_chunk = second_chunk.reshape(4 * pieces, chan_mid) * second_scale
-    both = jnp.concatenate([first_chunk, second_chunk], 0)
-    both = jnp.pad(both, ((0, -both.shape[0] % 8), (0, 0)))
-    final = everywhere(both.astype(BF), "sample")
-    first_grad = final[:, : 2 * size].reshape(28, chan_in, chan_mid)[:27]
-    second = final[:, 2 * size : 2 * size + 4 * pieces].reshape(samples_n, 2, 2, per, 3, chan_mid)
-    second = second.transpose(0, 3, 1, 2, 4, 5).reshape(per_group, 2, 2, 2, 3, chan_mid)
-    second = second.transpose(1, 4, 2, 3, 0, 5)
-    low, high = second[0], second[1]
-    blocks = [low[0], low[1], low[2] + high[0], high[1], high[2]]
-    second = jnp.stack([block[0] for block in blocks] + [block[1] for block in blocks[1:]], 1)
-    second = second.reshape(3, 2, 3, per_group, chan_mid)
-    second = jnp.pad(second, ((0, 0), (1, 0), (0, 0), (0, 0), (0, 0)))
-    second_grad = second.reshape(27, per_group, chan_mid).transpose(0, 2, 1)
+    second_chunk = jnp.pad(second_chunk, ((0, 16 - 4 * pieces), (0, 0)))
+    both = jnp.concatenate([second_chunk, first_chunk], 0).astype(BF)
+    first_grad, second_grad = pl.pallas_call(
+        final_kernel,
+        out_shape=(
+            jax.ShapeDtypeStruct((27, chan_in, chan_mid), BF),
+            jax.ShapeDtypeStruct((27, per_group, chan_mid), BF),
+        ),
+        compiler_params=pltpu.CompilerParams(vmem_limit_bytes=8 << 20),
+        cost_estimate=pl.CostEstimate(
+            flops=40_000_000, bytes_accessed=1_200_000, transcendentals=0
+        ),
+    )(everywhere(both, "sample"))
+    second_grad = second_grad.transpose(0, 2, 1)
     return input_grad, first_grad, second_grad
 
 

time: 101 us -> 99.9 us (0.989)
  local copies, waits for them, and re-layouts: 6.02 us -> 4.27 us
  Pallas kernels: 6.54 us -> 7.66 us
    pallas_call x0 -> x1, Pallas kernels: none -> 1.13 us  [shards(): pl.pallas_call(final_kernel, out_shape=(jax.ShapeDtypeStruct((27, chan_in...]
where the time goes in v7:
time: 99.9 us; the launch traced here: 99.4 us
  waiting for transfers between devices  38.3 us (38%)
  starting transfers between devices  28.5 us (29%)
  blocking collectives  18.7 us (19%)
  Pallas kernels  7.66 us (8%)
  local copies, waits for them, and re-layouts  4.27 us (4%)
  other arithmetic  1.05 us (1%)
    all_to_all x2, waiting for transfers between devices, exchanged(): return lax.all_to_all(parts, axis, split_axis=0, concat_axis=0, tiled=True)  35.2 us
    all_to_all x1, blocking collectives, exchanged(): return lax.all_to_all(parts, axis, split_axis=0, concat_axis=0, tiled=True)  18.7 us
    all_to_all x2, starting transfers between devices, exchanged(): return lax.all_to_all(parts, axis, split_axis=0, concat_axis=0, tiled=True)  13.1 us
    ppermute x1, starting transfers between devices, shards(): lax.ppermute(own, 'space', [(i, (i - 1) % groups) for i in range(groups)])  6.89 us
    ppermute x1, starting transfers between devices, shards(): got = lax.ppermute(sent, 'space', [(i, i ^ 1) for i in range(groups)])  4.74 us
    pallas_call x1, Pallas kernels, shards(): pl.pallas_call(forward_kernel, out_shape=(jax.ShapeDtypeStruct((3, chan_m...  3.05 us
    pallas_call x1, Pallas kernels, shards(): pl.pallas_call(backward_kernel, out_shape=(jax.ShapeDtypeStruct((planes,...  2.3 us
    ppermute x1, waiting for transfers between devices, shards(): below = lax.ppermute(own, 'space', [(i, i + 1) for i in range(groups - 1)])  2.21 us
  transfers between devices with their start and end apart: 6, of which 4 were waited for; matrix products, arithmetic and copies ran while one was open for 2% of the time, Pallas kernels for 3%

profile of v7, /device:TPU:1, one launch (start us, length us, event | category | flops | bytes accessed | tf_op | source)
XLA Modules:
  0.0 99.4 jit_solution(9529068251279509688)
XLA Ops:
  0.6 0.0 copy-start.1
  0.6 1.1 %copy.33 = bf16[4,4,64,128]{3,2,1,0:T(8,128)(2,1)S(1)} copy(bf16[4,4,64,128]{3,1,0,2:T(4,128)(2,1)} %bitcast.36) | data formatting | bytes 524288 | tf_op jit(solution)/shard_map/transpose | solution.py:300
  1.8 0.7 pad_maximum_fusion.own
  2.5 6.9 %collective-permute-start.1 = (bf16[1088,128]{1,0:T(8,128)(2,1)S(1)}, bf16[1088,128]{1,0:T(8,128)(2,1)S(1)}, u32[]{:S(2)}, u32[]{:S(2)}) collective-permute-start(bf16[1088,128]{1,0:T(8,128)(2,1)S(1)} %pad_maximum_fusion.own), channel_id=1, source_target_pairs={{0,15},{1,0},{2,1},{3,2},{4,3},{5,4},{6,5},{7,6},{8,7},{9,8},{10,9... | collective-permute-start | bytes 835592 | tf_op jit(solution)/shard_map/ppermute | solution.py:303
  9.4 1.9 %collective-permute-start = (bf16[1088,128]{1,0:T(8,128)(2,1)S(1)}, bf16[1088,128]{1,0:T(8,128)(2,1)S(1)}, u32[]{:S(2)}, u32[]{:S(2)}) collective-permute-start(bf16[1088,128]{1,0:T(8,128)(2,1)S(1)} %pad_maximum_fusion.own), channel_id=1, source_target_pairs={{0,1},{1,2},{2,3},{3,4},{4,5},{5,6},{6,7},{7,8},{8,9},{9,10},{10,1... | collective-permute-start | bytes 835592 | tf_op jit(solution)/shard_map/ppermute | solution.py:304
  11.4 1.2 %copy.34 = bf16[1728,128]{0,1:T(8,128)(2,1)S(1)} copy(bf16[1728,128]{1,0:T(8,128)(2,1)} %bitcast.30) | data formatting | bytes 884736 | tf_op jit(solution)/shard_map/reshape | solution.py:305
  12.6 0.0 collective-permute-done.1.above
  12.6 2.2 %collective-permute-done.below = bf16[1088,128]{1,0:T(8,128)(2,1)S(1)} collective-permute-done((bf16[1088,128]{1,0:T(8,128)(2,1)S(1)}, bf16[1088,128]{1,0:T(8,128)(2,1)S(1)}, u32[]{:S(2)}, u32[]{:S(2)}) %collective-permute-start) | collective-permute-done | bytes 278560 | tf_op jit(solution)/shard_map/ppermute | solution.py:304
  14.8 0.0 copy-done.1
  14.8 0.0 copy-start
  14.9 3.1 %shard_map.67 = (f32[3,128,128]{2,1,0:T(8,128)S(1)}, bf16[256,64]{1,0:T(8,128)(2,1)S(1)}, bf16[64,896]{1,0:T(8,128)(2,1)S(1)}, bf16[64,896]{1,0:T(8,128)(2,1)S(1)}) custom-call(s32[3]{0:T(128)S(1)} %compare_select_fusion.1.scalars, bf16[1088,128]{1,0:T(8,128)(2,1)S(1)} %collective-permute-done.below, bf16[1088,128]{1,0:T(8,128)(2,1)S(1)} %pad_maximum_fusion.own, ...), custom_call_target="tpu_custom_call" | custom-call | flops 2000000000 | bytes 5000000 | tf_op jit(solution)/shard_map/pallas_call | solution.py:318
  17.9 1.9 %collective-permute-start.2 = (bf16[64,896]{1,0:T(8,128)(2,1)S(1)}, bf16[64,896]{1,0:T(8,128)(2,1)S(1)}, u32[]{:S(2)}, u32[]{:S(2)}) collective-permute-start(bf16[64,896]{1,0:T(8,128)(2,1)S(1)} %get-tuple-element.16), channel_id=1, source_target_pairs={{0,2},{1,3},{2,0},{3,1},{4,6},{5,7},{6,4},{7,5},{8,10},{9,11},{10,... | collective-permute-start | bytes 344072 | tf_op jit(solution)/shard_map/ppermute | solution.py:336
  19.8 0.0 copy-done
  19.9 2.3 %shard_map.68 = (bf16[4,4,64,128]{3,2,1,0:T(8,128)(2,1)S(1)}, bf16[32,28,128]{2,1,0:T(8,128)(2,1)S(1)}, bf16[32,28,128]{2,1,0:T(8,128)(2,1)S(1)}) custom-call(s32[3]{0:T(128)S(1)} %compare_select_fusion.1.scalars, bf16[1088,128]{1,0:T(8,128)(2,1)S(1)} %collective-permute-done.below, bf16[1088,128]{1,0:T(8,128)(2,1)S(1)} %pad_maximum_fusion.own, ...), custom_call_target="tpu_custom_call" | custom-call | flops 3000000000 | bytes 5000000 | tf_op jit(solution)/shard_map/pallas_call | solution.py:337
  22.2 4.7 %collective-permute-start.3 = (bf16[32,28,128]{2,1,0:T(8,128)(2,1)S(1)}, bf16[32,28,128]{2,1,0:T(8,128)(2,1)S(1)}, u32[]{:S(2)}, u32[]{:S(2)}) collective-permute-start(bf16[32,28,128]{2,1,0:T(8,128)(2,1)S(1)} %get-tuple-element.18), channel_id=1, source_target_pairs={{0,1},{1,0},{2,3},{3,2},{4,5},{5,4},{6,7},{7,6},{8,9},{9,8},{10,11... | collective-permute-start | bytes 688136 | tf_op jit(solution)/shard_map/ppermute | solution.py:349
  26.9 0.0 collective-permute-done.2.theirs
  26.9 0.3 shard_map.69.second
  27.2 0.8 collective-permute-done.3.got
  28.0 0.9 shard_map.70
  28.9 8.6 %all-to-all-start = ((bf16[32,68,128]{2,1,0:T(8,128)(2,1)}), bf16[32,68,128]{2,1,0:T(8,128)(2,1)S(1)}, u32[]{:S(2)}, u32[]{:S(2)}) async-start(bf16[32,68,128]{2,1,0:T(8,128)(2,1)} %shard_map.70), calls=%async_computation | async-start | bytes 1179648 | tf_op jit(solution)/shard_map/all_to_all | solution.py:286
  37.6 17.6 %all-to-all-done = bf16[32,68,128]{2,1,0:T(8,128)(2,1)S(1)} async-done(((bf16[32,68,128]{2,1,0:T(8,128)(2,1)}), bf16[32,68,128]{2,1,0:T(8,128)(2,1)S(1)}, u32[]{:S(2)}, u32[]{:S(2)}) %all-to-all-start) | async-done | bytes 557088 | tf_op jit(solution)/shard_map/all_to_all | solution.py:286
  55.2 0.1 convert_reduce_fusion
  55.4 18.7 %all_to_all.15 = bf16[16,32,128]{2,1,0:T(8,128)(2,1)S(1)} all-to-all(bf16[16,32,128]{2,1,0:T(8,128)(2,1)S(1)} %fusion.1), channel_id=1, replica_groups=mesh['sample'=32,'space'=16] {'space'}, dimensions={0} | all-to-all | bytes 262144 | tf_op jit(solution)/shard_map/all_to_all | solution.py:286
  74.2 0.1 reduce_sum.29
  74.4 0.9 broadcast_in_dim.45
  75.3 4.5 %all-to-all-start.2 = ((bf16[32,72,128]{2,1,0:T(8,128)(2,1)}), bf16[32,72,128]{2,1,0:T(8,128)(2,1)S(1)}, u32[]{:S(2)}, u32[]{:S(2)}) async-start(bf16[32,72,128]{2,1,0:T(8,128)(2,1)} %broadcast_in_dim.45), calls=%async_computation.2 | async-start | bytes 1179648 | tf_op jit(solution)/shard_map/all_to_all | solution.py:286
  79.8 0.9 copy.40
  80.7 17.6 %all-to-all-done.2.chunks = bf16[32,72,128]{2,1,0:T(8,128)(2,1)S(1)} async-done(((bf16[32,72,128]{2,1,0:T(8,128)(2,1)}), bf16[32,72,128]{2,1,0:T(8,128)(2,1)S(1)}, u32[]{:S(2)}, u32[]{:S(2)}) %all-to-all-start.2) | async-done | bytes 589856 | tf_op jit(solution)/shard_map/all_to_all | solution.py:286
  98.3 1.1 %shard_map.71 = (bf16[27,64,128]{2,1,0:T(8,128)(2,1)}, bf16[27,16,128]{2,1,0:T(8,128)(2,1)}) custom-call(bf16[32,72,128]{2,1,0:T(8,128)(2,1)S(1)} %all-to-all-done.2.chunks), custom_call_target="tpu_custom_call" | custom-call | flops 40000000 | bytes 1200000 | tf_op jit(solution)/shard_map/pallas_call | solution.py:391
  (17 shorter events, 0.2 us)
Async XLA Ops:
  0.6 14.2 %copy-start.1 = (bf16[27,128,256]{2,1,0:T(8,128)(2,1)S(1)}, bf16[27,128,256]{2,1,0:T(8,128)(2,1)}, u32[]{:S(2)}) copy-start(bf16[27,128,256]{2,1,0:T(8,128)(2,1)} %param.7) | copy-start | bytes 5308420
  2.5 10.1 %collective-permute-start.1 = (bf16[1088,128]{1,0:T(8,128)(2,1)S(1)}, bf16[1088,128]{1,0:T(8,128)(2,1)S(1)}, u32[]{:S(2)}, u32[]{:S(2)}) collective-permute-start(bf16[1088,128]{1,0:T(8,128)(2,1)S(1)} %pad_maximum_fusion.own), channel_id=1, source_target_pairs={{0,15},{1,0},{2,1},{3,2},{4,3},{5,4},{6,5},{7,6},{8,7},{9,8},{10,9... | collective-permute-start | bytes 835592 | tf_op jit(solution)/shard_map/ppermute | solution.py:303
  9.4 5.4 %collective-permute-start = (bf16[1088,128]{1,0:T(8,128)(2,1)S(1)}, bf16[1088,128]{1,0:T(8,128)(2,1)S(1)}, u32[]{:S(2)}, u32[]{:S(2)}) collective-permute-start(bf16[1088,128]{1,0:T(8,128)(2,1)S(1)} %pad_maximum_fusion.own), channel_id=1, source_target_pairs={{0,1},{1,2},{2,3},{3,4},{4,5},{5,6},{6,7},{7,8},{8,9},{9,10},{10,1... | collective-permute-start | bytes 835592 | tf_op jit(solution)/shard_map/ppermute | solution.py:304
  14.8 5.0 %copy-start = (bf16[27,64,128]{2,1,0:T(8,128)(2,1)S(1)}, bf16[27,64,128]{2,1,0:T(8,128)(2,1)}, u32[]{:S(2)}) copy-start(bf16[27,64,128]{2,1,0:T(8,128)(2,1)} %first_weight.1) | copy-start | bytes 1327108
  17.9 9.0 %collective-permute-start.2 = (bf16[64,896]{1,0:T(8,128)(2,1)S(1)}, bf16[64,896]{1,0:T(8,128)(2,1)S(1)}, u32[]{:S(2)}, u32[]{:S(2)}) collective-permute-start(bf16[64,896]{1,0:T(8,128)(2,1)S(1)} %get-tuple-element.16), channel_id=1, source_target_pairs={{0,2},{1,3},{2,0},{3,1},{4,6},{5,7},{6,4},{7,5},{8,10},{9,11},{10,... | collective-permute-start | bytes 344072 | tf_op jit(solution)/shard_map/ppermute | solution.py:336
  22.2 5.9 %collective-permute-start.3 = (bf16[32,28,128]{2,1,0:T(8,128)(2,1)S(1)}, bf16[32,28,128]{2,1,0:T(8,128)(2,1)S(1)}, u32[]{:S(2)}, u32[]{:S(2)}) collective-permute-start(bf16[32,28,128]{2,1,0:T(8,128)(2,1)S(1)} %get-tuple-element.18), channel_id=1, source_target_pairs={{0,1},{1,0},{2,3},{3,2},{4,5},{5,4},{6,7},{7,6},{8,9},{9,8},{10,11... | collective-permute-start | bytes 688136 | tf_op jit(solution)/shard_map/ppermute | solution.py:349
  28.9 26.2 %all-to-all-start = ((bf16[32,68,128]{2,1,0:T(8,128)(2,1)}), bf16[32,68,128]{2,1,0:T(8,128)(2,1)S(1)}, u32[]{:S(2)}, u32[]{:S(2)}) async-start(bf16[32,68,128]{2,1,0:T(8,128)(2,1)} %shard_map.70), calls=%async_computation | async-start | bytes 1179648 | tf_op jit(solution)/shard_map/all_to_all | solution.py:286
  75.3 23.0 %all-to-all-start.2 = ((bf16[32,72,128]{2,1,0:T(8,128)(2,1)}), bf16[32,72,128]{2,1,0:T(8,128)(2,1)S(1)}, u32[]{:S(2)}, u32[]{:S(2)}) async-start(bf16[32,72,128]{2,1,0:T(8,128)(2,1)} %broadcast_in_dim.45), calls=%async_computation.2 | async-start | bytes 1179648 | tf_op jit(solution)/shard_map/all_to_all | solution.py:286

commit v8 on v7

--- a/solution.py
+++ b/solution.py
@@ -83,10 +83,16 @@
             picked = picked.astype(BF)
             for p in range(planes):
                 for e in range(3):
-                    start = (first + p) * group + (3 * b + e) * chan_in
-                    blocks[start : start + chan_in, :] = picked[
-                        p * chan_in : (p + 1) * chan_in, e * 128 : (e + 1) * 128
-                    ]
+                    value = picked[p * chan_in : (p + 1) * chan_in, e * 128 : (e + 1) * 128]
+                    for a in range(3):
+                        h, odd = (first + p - a) // 2, (first + p - a) % 2
+                        if odd or not 0 <= h <= 4:
+                            continue
+                        placed = value
+                        if (a, h) == (0, 3):
+                            placed = jnp.where(inside, value.astype(F32), 0.0).astype(BF)
+                        start = a * group + (3 * b + e) * chan_in
+                        blocks[start : start + chan_in, h * 128 : (h + 1) * 128] = placed
         first += planes
     quarter = 32
     lines = 16 * chan_in
@@ -101,12 +107,9 @@
     )
     cotangent = jnp.concatenate([cotangent[:64], cotangent[64:]], 1)
     pres = []
+    wide = dot(flipped[...], blocks[...])
     for h in range(5):
-        if h == 3:
-            pre = jnp.where(inside, dot(flipped[:, :group], blocks[6 * group : 7 * group, :]), 0.0)
-            pre = pre + dot(flipped[:, group:], blocks[7 * group : 9 * group, :])
-        else:
-            pre = dot(flipped[...], blocks[2 * h * group : (2 * h + 3) * group, :])
+        pre = wide[:, h * 128 : (h + 1) * 128]
         pres.append(pre)
         hidden = (pre * jax.nn.sigmoid(pre)).astype(BF)
         chan = hidden.shape[0]
@@ -140,8 +143,8 @@
 
 
 def backward_kernel(
-    scalars, below, own, delta_ref, pre_ref, first_weight, second_weight,
-    volume_ref, kept_ref, sent_ref, grads,
+    scalars, below, own, delta_ref, pre_ref, second_weight,
+    stacks_ref, kept_ref, sent_ref, grads,
 ):
     parity = scalars[0]
     chan_in, cells = 64, 128
@@ -172,27 +175,8 @@
         for h in range(3)
     ]
 
-    def filters(a):
-        return [
-            jnp.concatenate([first_weight[9 * a + 3 * b + e] for e in range(3)], 1) for b in range(3)
-        ]
-
-    totals = {}
-    for h, chosen in enumerate(((1, 2), (0, 1, 2), (0,))):
-        left = jnp.concatenate(sum([filters(a) for a in chosen], []), 0)
-        result = dot(left, stacks[h])
-        for place, a in enumerate(chosen):
-            p = 2 * h + a - 1
-            for b in range(3):
-                for j in range(2):
-                    r = 2 * j + b - 1
-                    if r < 0:
-                        continue
-                    start = (3 * place + b) * chan_in
-                    term = result[start : start + chan_in, j * cells : (j + 1) * cells]
-                    totals[p, r] = totals[p, r] + term if (p, r) in totals else term
-    for (p, r), total in totals.items():
-        volume_ref[p, r] = total.astype(BF)
+    for h in range(3):
+        stacks_ref[h] = stacks[h]
 
     def plane(p, r):
         ref, start = (below, (12 + r) * chan_in) if p < 0 else (own, (4 * p + r) * chan_in)
@@ -224,8 +208,31 @@
         sent_ref[m] = jnp.where(parity == 0, upper, lower).astype(BF)
 
 
-def second_kernel(mine, theirs, second_ref):
+def middle_kernel(mine, theirs, stacks, first_weight, second_ref, volume_ref):
+    chan_in, cells = volume_ref.shape[2:]
     chan = second_ref.shape[2]
+    def filters(a):
+        return [
+            jnp.concatenate([first_weight[9 * a + 3 * b + e] for e in range(3)], 1) for b in range(3)
+        ]
+
+    totals = {}
+    for h, chosen in enumerate(((1, 2), (0, 1, 2), (0,))):
+        left = jnp.concatenate(sum([filters(a) for a in chosen], []), 0)
+        result = dot(left, stacks[h])
+        for place, a in enumerate(chosen):
+            p = 2 * h + a - 1
+            for b in range(3):
+                for j in range(2):
+                    r = 2 * j + b - 1
+                    if r < 0:
+                        continue
+                    start = (3 * place + b) * chan_in
+                    term = result[start : start + chan_in, j * cells : (j + 1) * cells]
+                    totals[p, r] = totals[p, r] + term if (p, r) in totals else term
+    for (p, r), total in totals.items():
+        volume_ref[p, r] = total.astype(BF)
+
     share = 5 * chan
     both = jnp.concatenate([mine[...], theirs[...]], 0)
     second = lax.dot_general(
@@ -325,7 +332,7 @@
         ),
         in_specs=[smem] + [vmem] * 5,
         scratch_shapes=[
-            pltpu.VMEM((11 * 9 * chan_in, rows * half), BF),
+            pltpu.VMEM((27 * chan_in, 5 * rows * half), BF),
             pltpu.VMEM((2 * quarter, 18 * chan_mid), BF),
         ],
         compiler_params=pltpu.CompilerParams(vmem_limit_bytes=16 << 20),
@@ -334,27 +341,28 @@
         ),
     )(scalars, below, own, above, flipped, flat_second)
     theirs = lax.ppermute(theirs, "space", [(i, i ^ 2) for i in range(groups)])
-    volume, kept, sent = pl.pallas_call(
+    stacks, kept, sent = pl.pallas_call(
         backward_kernel,
-        out_shape=(
-            jax.ShapeDtypeStruct((planes, height, chan_in, length), BF), halved, halved
-        ),
-        in_specs=[smem] + [vmem] * 6,
+        out_shape=(jax.ShapeDtypeStruct((3, 3 * chan_mid, 2 * length), BF), halved, halved),
+        in_specs=[smem] + [vmem] * 5,
         scratch_shapes=[pltpu.VMEM((28 * chan_in, chan_mid), F32)],
         compiler_params=pltpu.CompilerParams(vmem_limit_bytes=16 << 20),
         cost_estimate=pl.CostEstimate(
             flops=3_000_000_000, bytes_accessed=5_000_000, transcendentals=0
         ),
-    )(scalars, below, own, delta, pre, first_weight, flat_second)
+    )(scalars, below, own, delta, pre, flat_second)
     got = lax.ppermute(sent, "space", [(i, i ^ 1) for i in range(groups)])
-    second = pl.pallas_call(
-        second_kernel,
-        out_shape=jax.ShapeDtypeStruct((samples_n, per * 40, chan_mid), BF),
+    second, volume = pl.pallas_call(
+        middle_kernel,
+        out_shape=(
+            jax.ShapeDtypeStruct((samples_n, per * 40, chan_mid), BF),
+            jax.ShapeDtypeStruct((planes, height, chan_in, length), BF),
+        ),
         compiler_params=pltpu.CompilerParams(vmem_limit_bytes=8 << 20),
         cost_estimate=pl.CostEstimate(
             flops=2_000_000_000, bytes_accessed=2_000_000, transcendentals=0
         ),
-    )(mine, theirs)
+    )(mine, theirs, stacks, first_weight)
     payload = pl.pallas_call(
         pack_kernel,
         out_shape=jax.ShapeDtypeStruct((samples_n, per * 40 + size, chan_mid), BF),

time: 99.9 us -> 98.9 us (0.990)
  no operation moved by 1% of the time
where the time goes in v8:
time: 98.9 us; the launch traced here: 98.4 us
  waiting for transfers between devices  38 us (38%)
  starting transfers between devices  28.5 us (29%)
  blocking collectives  18.7 us (19%)
  Pallas kernels  6.93 us (7%)
  local copies, waits for them, and re-layouts  4.27 us (4%)
  other arithmetic  1.05 us (1%)
    all_to_all x2, waiting for transfers between devices, exchanged(): return lax.all_to_all(parts, axis, split_axis=0, concat_axis=0, tiled=True)  35.2 us
    all_to_all x1, blocking collectives, exchanged(): return lax.all_to_all(parts, axis, split_axis=0, concat_axis=0, tiled=True)  18.7 us
    all_to_all x2, starting transfers between devices, exchanged(): return lax.all_to_all(parts, axis, split_axis=0, concat_axis=0, tiled=True)  13.1 us
    ppermute x1, starting transfers between devices, shards(): lax.ppermute(own, 'space', [(i, (i - 1) % groups) for i in range(groups)])  6.89 us
    ppermute x1, starting transfers between devices, shards(): got = lax.ppermute(sent, 'space', [(i, i ^ 1) for i in range(groups)])  4.74 us
    pallas_call x1, Pallas kernels, shards(): pl.pallas_call(forward_kernel, out_shape=(jax.ShapeDtypeStruct((3, chan_m...  2.32 us
    ppermute x1, waiting for transfers between devices, shards(): below = lax.ppermute(own, 'space', [(i, i + 1) for i in range(groups - 1)])  2.21 us
    pallas_call x1, Pallas kernels, shards(): pl.pallas_call(backward_kernel, out_shape=(jax.ShapeDtypeStruct((3, 3 * c...  2.04 us
  transfers between devices with their start and end apart: 6, of which 4 were waited for; matrix products, arithmetic and copies ran while one was open for 2% of the time, Pallas kernels for 3%

profile of v8, /device:TPU:1, one launch (start us, length us, event | category | flops | bytes accessed | tf_op | source)
XLA Modules:
  0.0 98.4 jit_solution(7016045619578633784)
XLA Ops:
  0.6 0.0 copy-start.1
  0.6 1.1 %copy.33 = bf16[4,4,64,128]{3,2,1,0:T(8,128)(2,1)S(1)} copy(bf16[4,4,64,128]{3,1,0,2:T(4,128)(2,1)} %bitcast.36) | data formatting | bytes 524288 | tf_op jit(solution)/shard_map/transpose | solution.py:307
  1.8 0.7 pad_maximum_fusion.own
  2.5 6.9 %collective-permute-start.1 = (bf16[1088,128]{1,0:T(8,128)(2,1)S(1)}, bf16[1088,128]{1,0:T(8,128)(2,1)S(1)}, u32[]{:S(2)}, u32[]{:S(2)}) collective-permute-start(bf16[1088,128]{1,0:T(8,128)(2,1)S(1)} %pad_maximum_fusion.own), channel_id=1, source_target_pairs={{0,15},{1,0},{2,1},{3,2},{4,3},{5,4},{6,5},{7,6},{8,7},{9,8},{10,9... | collective-permute-start | bytes 835592 | tf_op jit(solution)/shard_map/ppermute | solution.py:310
  9.4 1.9 %collective-permute-start = (bf16[1088,128]{1,0:T(8,128)(2,1)S(1)}, bf16[1088,128]{1,0:T(8,128)(2,1)S(1)}, u32[]{:S(2)}, u32[]{:S(2)}) collective-permute-start(bf16[1088,128]{1,0:T(8,128)(2,1)S(1)} %pad_maximum_fusion.own), channel_id=1, source_target_pairs={{0,1},{1,2},{2,3},{3,4},{4,5},{5,6},{6,7},{7,8},{8,9},{9,10},{10,1... | collective-permute-start | bytes 835592 | tf_op jit(solution)/shard_map/ppermute | solution.py:311
  11.4 1.2 %copy.34 = bf16[1728,128]{0,1:T(8,128)(2,1)S(1)} copy(bf16[1728,128]{1,0:T(8,128)(2,1)} %bitcast.30) | data formatting | bytes 884736 | tf_op jit(solution)/shard_map/reshape | solution.py:312
  12.6 0.0 collective-permute-done.1.above
  12.6 2.2 %collective-permute-done.below = bf16[1088,128]{1,0:T(8,128)(2,1)S(1)} collective-permute-done((bf16[1088,128]{1,0:T(8,128)(2,1)S(1)}, bf16[1088,128]{1,0:T(8,128)(2,1)S(1)}, u32[]{:S(2)}, u32[]{:S(2)}) %collective-permute-start) | collective-permute-done | bytes 278560 | tf_op jit(solution)/shard_map/ppermute | solution.py:311
  14.8 0.0 copy-done.1
  14.8 2.3 %shard_map.67 = (f32[3,128,128]{2,1,0:T(8,128)S(1)}, bf16[256,64]{1,0:T(8,128)(2,1)S(1)}, bf16[64,896]{1,0:T(8,128)(2,1)S(1)}, bf16[64,896]{1,0:T(8,128)(2,1)S(1)}) custom-call(s32[3]{0:T(128)S(1)} %compare_select_fusion.1.scalars, bf16[1088,128]{1,0:T(8,128)(2,1)S(1)} %collective-permute-done.below, bf16[1088,128]{1,0:T(8,128)(2,1)S(1)} %pad_maximum_fusion.own, ...), custom_call_target="tpu_custom_call" | custom-call | flops 2000000000 | bytes 5000000 | tf_op jit(solution)/shard_map/pallas_call | solution.py:325
  17.2 1.9 %collective-permute-start.2 = (bf16[64,896]{1,0:T(8,128)(2,1)S(1)}, bf16[64,896]{1,0:T(8,128)(2,1)S(1)}, u32[]{:S(2)}, u32[]{:S(2)}) collective-permute-start(bf16[64,896]{1,0:T(8,128)(2,1)S(1)} %get-tuple-element.15), channel_id=1, source_target_pairs={{0,2},{1,3},{2,0},{3,1},{4,6},{5,7},{6,4},{7,5},{8,10},{9,11},{10,... | collective-permute-start | bytes 344072 | tf_op jit(solution)/shard_map/ppermute | solution.py:343
  19.1 0.0 copy-start
  19.1 2.0 %shard_map.68 = (bf16[3,384,256]{2,1,0:T(8,128)(2,1)S(1)}, bf16[32,28,128]{2,1,0:T(8,128)(2,1)S(1)}, bf16[32,28,128]{2,1,0:T(8,128)(2,1)S(1)}) custom-call(s32[3]{0:T(128)S(1)} %compare_select_fusion.1.scalars, bf16[1088,128]{1,0:T(8,128)(2,1)S(1)} %collective-permute-done.below, bf16[1088,128]{1,0:T(8,128)(2,1)S(1)} %pad_maximum_fusion.own, ...), custom_call_target="tpu_custom_call" | custom-call | flops 3000000000 | bytes 5000000 | tf_op jit(solution)/shard_map/pallas_call | solution.py:344
  21.2 4.7 %collective-permute-start.3 = (bf16[32,28,128]{2,1,0:T(8,128)(2,1)S(1)}, bf16[32,28,128]{2,1,0:T(8,128)(2,1)S(1)}, u32[]{:S(2)}, u32[]{:S(2)}) collective-permute-start(bf16[32,28,128]{2,1,0:T(8,128)(2,1)S(1)} %get-tuple-element.22), channel_id=1, source_target_pairs={{0,1},{1,0},{2,3},{3,2},{4,5},{5,4},{6,7},{7,6},{8,9},{9,8},{10,11... | collective-permute-start | bytes 688136 | tf_op jit(solution)/shard_map/ppermute | solution.py:354
  25.9 0.0 collective-permute-done.2.theirs
  25.9 0.0 copy-done
  25.9 0.5 shard_map.69
  26.5 0.6 collective-permute-done.3.got
  27.0 0.9 shard_map.70
  27.9 8.6 %all-to-all-start = ((bf16[32,68,128]{2,1,0:T(8,128)(2,1)}), bf16[32,68,128]{2,1,0:T(8,128)(2,1)S(1)}, u32[]{:S(2)}, u32[]{:S(2)}) async-start(bf16[32,68,128]{2,1,0:T(8,128)(2,1)} %shard_map.70), calls=%async_computation | async-start | bytes 1179648 | tf_op jit(solution)/shard_map/all_to_all | solution.py:293
  36.6 17.6 %all-to-all-done = bf16[32,68,128]{2,1,0:T(8,128)(2,1)S(1)} async-done(((bf16[32,68,128]{2,1,0:T(8,128)(2,1)}), bf16[32,68,128]{2,1,0:T(8,128)(2,1)S(1)}, u32[]{:S(2)}, u32[]{:S(2)}) %all-to-all-start) | async-done | bytes 557088 | tf_op jit(solution)/shard_map/all_to_all | solution.py:293
  54.2 0.1 convert_reduce_fusion
  54.4 18.7 %all_to_all.15 = bf16[16,32,128]{2,1,0:T(8,128)(2,1)S(1)} all-to-all(bf16[16,32,128]{2,1,0:T(8,128)(2,1)S(1)} %fusion.1), channel_id=1, replica_groups=mesh['sample'=32,'space'=16] {'space'}, dimensions={0} | all-to-all | bytes 262144 | tf_op jit(solution)/shard_map/all_to_all | solution.py:293
  73.2 0.1 reduce_sum.29
  73.4 0.9 broadcast_in_dim.45
  74.3 4.5 %all-to-all-start.2 = ((bf16[32,72,128]{2,1,0:T(8,128)(2,1)}), bf16[32,72,128]{2,1,0:T(8,128)(2,1)S(1)}, u32[]{:S(2)}, u32[]{:S(2)}) async-start(bf16[32,72,128]{2,1,0:T(8,128)(2,1)} %broadcast_in_dim.45), calls=%async_computation.2 | async-start | bytes 1179648 | tf_op jit(solution)/shard_map/all_to_all | solution.py:293
  78.8 0.9 copy.40
  79.7 17.6 %all-to-all-done.2.chunks = bf16[32,72,128]{2,1,0:T(8,128)(2,1)S(1)} async-done(((bf16[32,72,128]{2,1,0:T(8,128)(2,1)}), bf16[32,72,128]{2,1,0:T(8,128)(2,1)S(1)}, u32[]{:S(2)}, u32[]{:S(2)}) %all-to-all-start.2) | async-done | bytes 589856 | tf_op jit(solution)/shard_map/all_to_all | solution.py:293
  97.3 1.1 %shard_map.71 = (bf16[27,64,128]{2,1,0:T(8,128)(2,1)}, bf16[27,16,128]{2,1,0:T(8,128)(2,1)}) custom-call(bf16[32,72,128]{2,1,0:T(8,128)(2,1)S(1)} %all-to-all-done.2.chunks), custom_call_target="tpu_custom_call" | custom-call | flops 40000000 | bytes 1200000 | tf_op jit(solution)/shard_map/pallas_call | solution.py:399
  (17 shorter events, 0.2 us)
Async XLA Ops:
  0.6 14.2 %copy-start.1 = (bf16[27,128,256]{2,1,0:T(8,128)(2,1)S(1)}, bf16[27,128,256]{2,1,0:T(8,128)(2,1)}, u32[]{:S(2)}) copy-start(bf16[27,128,256]{2,1,0:T(8,128)(2,1)} %param.7) | copy-start | bytes 5308420
  2.5 10.1 %collective-permute-start.1 = (bf16[1088,128]{1,0:T(8,128)(2,1)S(1)}, bf16[1088,128]{1,0:T(8,128)(2,1)S(1)}, u32[]{:S(2)}, u32[]{:S(2)}) collective-permute-start(bf16[1088,128]{1,0:T(8,128)(2,1)S(1)} %pad_maximum_fusion.own), channel_id=1, source_target_pairs={{0,15},{1,0},{2,1},{3,2},{4,3},{5,4},{6,5},{7,6},{8,7},{9,8},{10,9... | collective-permute-start | bytes 835592 | tf_op jit(solution)/shard_map/ppermute | solution.py:310
  9.4 5.4 %collective-permute-start = (bf16[1088,128]{1,0:T(8,128)(2,1)S(1)}, bf16[1088,128]{1,0:T(8,128)(2,1)S(1)}, u32[]{:S(2)}, u32[]{:S(2)}) collective-permute-start(bf16[1088,128]{1,0:T(8,128)(2,1)S(1)} %pad_maximum_fusion.own), channel_id=1, source_target_pairs={{0,1},{1,2},{2,3},{3,4},{4,5},{5,6},{6,7},{7,8},{8,9},{9,10},{10,1... | collective-permute-start | bytes 835592 | tf_op jit(solution)/shard_map/ppermute | solution.py:311
  17.2 8.7 %collective-permute-start.2 = (bf16[64,896]{1,0:T(8,128)(2,1)S(1)}, bf16[64,896]{1,0:T(8,128)(2,1)S(1)}, u32[]{:S(2)}, u32[]{:S(2)}) collective-permute-start(bf16[64,896]{1,0:T(8,128)(2,1)S(1)} %get-tuple-element.15), channel_id=1, source_target_pairs={{0,2},{1,3},{2,0},{3,1},{4,6},{5,7},{6,4},{7,5},{8,10},{9,11},{10,... | collective-permute-start | bytes 344072 | tf_op jit(solution)/shard_map/ppermute | solution.py:343
  19.1 6.8 %copy-start = (bf16[27,64,128]{2,1,0:T(8,128)(2,1)S(1)}, bf16[27,64,128]{2,1,0:T(8,128)(2,1)}, u32[]{:S(2)}) copy-start(bf16[27,64,128]{2,1,0:T(8,128)(2,1)} %first_weight.1) | copy-start | bytes 1327108
  21.2 5.9 %collective-permute-start.3 = (bf16[32,28,128]{2,1,0:T(8,128)(2,1)S(1)}, bf16[32,28,128]{2,1,0:T(8,128)(2,1)S(1)}, u32[]{:S(2)}, u32[]{:S(2)}) collective-permute-start(bf16[32,28,128]{2,1,0:T(8,128)(2,1)S(1)} %get-tuple-element.22), channel_id=1, source_target_pairs={{0,1},{1,0},{2,3},{3,2},{4,5},{5,4},{6,7},{7,6},{8,9},{9,8},{10,11... | collective-permute-start | bytes 688136 | tf_op jit(solution)/shard_map/ppermute | solution.py:354
  27.9 26.2 %all-to-all-start = ((bf16[32,68,128]{2,1,0:T(8,128)(2,1)}), bf16[32,68,128]{2,1,0:T(8,128)(2,1)S(1)}, u32[]{:S(2)}, u32[]{:S(2)}) async-start(bf16[32,68,128]{2,1,0:T(8,128)(2,1)} %shard_map.70), calls=%async_computation | async-start | bytes 1179648 | tf_op jit(solution)/shard_map/all_to_all | solution.py:293
  74.3 23.0 %all-to-all-start.2 = ((bf16[32,72,128]{2,1,0:T(8,128)(2,1)}), bf16[32,72,128]{2,1,0:T(8,128)(2,1)S(1)}, u32[]{:S(2)}, u32[]{:S(2)}) async-start(bf16[32,72,128]{2,1,0:T(8,128)(2,1)} %broadcast_in_dim.45), calls=%async_computation.2 | async-start | bytes 1179648 | tf_op jit(solution)/shard_map/all_to_all | solution.py:293

commit v9 on v8

--- a/solution.py
+++ b/solution.py
@@ -261,14 +261,15 @@
 
 def final_kernel(chunks, first_ref, second_ref):
     taps, chan_in, chan = first_ref.shape
-    samples_n, rows = chunks.shape[0], chunks.shape[1] - 16
+    samples_n, rows = chunks.shape[0], chunks.shape[1] - 12
     for m in range(samples_n):
+        lines = chunks[m].astype(F32)[12:].astype(BF)
         at, stop = m * rows, min((m + 1) * rows, taps * chan_in)
         while at < stop:
             tap, channel = at // chan_in, at % chan_in
             count = min(stop - at, chan_in - channel)
-            begin = 16 + at - m * rows
-            first_ref[tap, channel : channel + count, :] = chunks[m, begin : begin + count, :]
+            begin = at - m * rows
+            first_ref[tap, channel : channel + count, :] = lines[begin : begin + count]
             at += count
     per_group = second_ref.shape[1]
 
@@ -394,7 +395,6 @@
     second_scale = 1.0 / math.sqrt(samples_n * groups * (planes // 4) * (height // 4) * quarter)
     first_chunk = first_chunk.reshape(2 * size, chan_mid) * first_scale
     second_chunk = second_chunk.reshape(4 * pieces, chan_mid) * second_scale
-    second_chunk = jnp.pad(second_chunk, ((0, 16 - 4 * pieces), (0, 0)))
     both = jnp.concatenate([second_chunk, first_chunk], 0).astype(BF)
     first_grad, second_grad = pl.pallas_call(
         final_kernel,

time: 98.9 us -> 99 us (level)
  no operation moved by 1% of the time
where the time goes in v9:
time: 99 us; the launch traced here: 98.5 us
  waiting for transfers between devices  38 us (38%)
  starting transfers between devices  28.5 us (29%)
  blocking collectives  18.7 us (19%)
  Pallas kernels  7.02 us (7%)
  local copies, waits for them, and re-layouts  4.27 us (4%)
  other arithmetic  1.06 us (1%)
    all_to_all x2, waiting for transfers between devices, exchanged(): return lax.all_to_all(parts, axis, split_axis=0, concat_axis=0, tiled=True)  35.2 us
    all_to_all x1, blocking collectives, exchanged(): return lax.all_to_all(parts, axis, split_axis=0, concat_axis=0, tiled=True)  18.7 us
    all_to_all x2, starting transfers between devices, exchanged(): return lax.all_to_all(parts, axis, split_axis=0, concat_axis=0, tiled=True)  13.1 us
    ppermute x1, starting transfers between devices, shards(): lax.ppermute(own, 'space', [(i, (i - 1) % groups) for i in range(groups)])  6.89 us
    ppermute x1, starting transfers between devices, shards(): got = lax.ppermute(sent, 'space', [(i, i ^ 1) for i in range(groups)])  4.74 us
    pallas_call x1, Pallas kernels, shards(): pl.pallas_call(forward_kernel, out_shape=(jax.ShapeDtypeStruct((3, chan_m...  2.32 us
    ppermute x1, waiting for transfers between devices, shards(): below = lax.ppermute(own, 'space', [(i, i + 1) for i in range(groups - 1)])  2.21 us
    pallas_call x1, Pallas kernels, shards(): pl.pallas_call(backward_kernel, out_shape=(jax.ShapeDtypeStruct((3, 3 * c...  2.04 us
  transfers between devices with their start and end apart: 6, of which 4 were waited for; matrix products, arithmetic and copies ran while one was open for 2% of the time, Pallas kernels for 3%

profile of v9, /device:TPU:1, one launch (start us, length us, event | category | flops | bytes accessed | tf_op | source)
XLA Modules:
  0.0 98.5 jit_solution(16698271568421338848)
XLA Ops:
  0.6 0.0 copy-start.1
  0.6 1.1 %copy.33 = bf16[4,4,64,128]{3,2,1,0:T(8,128)(2,1)S(1)} copy(bf16[4,4,64,128]{3,1,0,2:T(4,128)(2,1)} %bitcast.36) | data formatting | bytes 524288 | tf_op jit(solution)/shard_map/transpose | solution.py:308
  1.8 0.7 pad_maximum_fusion.own
  2.5 6.9 %collective-permute-start.1 = (bf16[1088,128]{1,0:T(8,128)(2,1)S(1)}, bf16[1088,128]{1,0:T(8,128)(2,1)S(1)}, u32[]{:S(2)}, u32[]{:S(2)}) collective-permute-start(bf16[1088,128]{1,0:T(8,128)(2,1)S(1)} %pad_maximum_fusion.own), channel_id=1, source_target_pairs={{0,15},{1,0},{2,1},{3,2},{4,3},{5,4},{6,5},{7,6},{8,7},{9,8},{10,9... | collective-permute-start | bytes 835592 | tf_op jit(solution)/shard_map/ppermute | solution.py:311
  9.4 1.9 %collective-permute-start = (bf16[1088,128]{1,0:T(8,128)(2,1)S(1)}, bf16[1088,128]{1,0:T(8,128)(2,1)S(1)}, u32[]{:S(2)}, u32[]{:S(2)}) collective-permute-start(bf16[1088,128]{1,0:T(8,128)(2,1)S(1)} %pad_maximum_fusion.own), channel_id=1, source_target_pairs={{0,1},{1,2},{2,3},{3,4},{4,5},{5,6},{6,7},{7,8},{8,9},{9,10},{10,1... | collective-permute-start | bytes 835592 | tf_op jit(solution)/shard_map/ppermute | solution.py:312
  11.4 1.2 %copy.34 = bf16[1728,128]{0,1:T(8,128)(2,1)S(1)} copy(bf16[1728,128]{1,0:T(8,128)(2,1)} %bitcast.30) | data formatting | bytes 884736 | tf_op jit(solution)/shard_map/reshape | solution.py:313
  12.6 0.0 collective-permute-done.1.above
  12.6 2.2 %collective-permute-done.below = bf16[1088,128]{1,0:T(8,128)(2,1)S(1)} collective-permute-done((bf16[1088,128]{1,0:T(8,128)(2,1)S(1)}, bf16[1088,128]{1,0:T(8,128)(2,1)S(1)}, u32[]{:S(2)}, u32[]{:S(2)}) %collective-permute-start) | collective-permute-done | bytes 278560 | tf_op jit(solution)/shard_map/ppermute | solution.py:312
  14.8 0.0 copy-done.1
  14.8 2.3 %shard_map.67 = (f32[3,128,128]{2,1,0:T(8,128)S(1)}, bf16[256,64]{1,0:T(8,128)(2,1)S(1)}, bf16[64,896]{1,0:T(8,128)(2,1)S(1)}, bf16[64,896]{1,0:T(8,128)(2,1)S(1)}) custom-call(s32[3]{0:T(128)S(1)} %compare_select_fusion.1.scalars, bf16[1088,128]{1,0:T(8,128)(2,1)S(1)} %collective-permute-done.below, bf16[1088,128]{1,0:T(8,128)(2,1)S(1)} %pad_maximum_fusion.own, ...), custom_call_target="tpu_custom_call" | custom-call | flops 2000000000 | bytes 5000000 | tf_op jit(solution)/shard_map/pallas_call | solution.py:326
  17.2 1.9 %collective-permute-start.2 = (bf16[64,896]{1,0:T(8,128)(2,1)S(1)}, bf16[64,896]{1,0:T(8,128)(2,1)S(1)}, u32[]{:S(2)}, u32[]{:S(2)}) collective-permute-start(bf16[64,896]{1,0:T(8,128)(2,1)S(1)} %get-tuple-element.15), channel_id=1, source_target_pairs={{0,2},{1,3},{2,0},{3,1},{4,6},{5,7},{6,4},{7,5},{8,10},{9,11},{10,... | collective-permute-start | bytes 344072 | tf_op jit(solution)/shard_map/ppermute | solution.py:344
  19.1 0.0 copy-start
  19.1 2.0 %shard_map.68 = (bf16[3,384,256]{2,1,0:T(8,128)(2,1)S(1)}, bf16[32,28,128]{2,1,0:T(8,128)(2,1)S(1)}, bf16[32,28,128]{2,1,0:T(8,128)(2,1)S(1)}) custom-call(s32[3]{0:T(128)S(1)} %compare_select_fusion.1.scalars, bf16[1088,128]{1,0:T(8,128)(2,1)S(1)} %collective-permute-done.below, bf16[1088,128]{1,0:T(8,128)(2,1)S(1)} %pad_maximum_fusion.own, ...), custom_call_target="tpu_custom_call" | custom-call | flops 3000000000 | bytes 5000000 | tf_op jit(solution)/shard_map/pallas_call | solution.py:345
  21.2 4.7 %collective-permute-start.3 = (bf16[32,28,128]{2,1,0:T(8,128)(2,1)S(1)}, bf16[32,28,128]{2,1,0:T(8,128)(2,1)S(1)}, u32[]{:S(2)}, u32[]{:S(2)}) collective-permute-start(bf16[32,28,128]{2,1,0:T(8,128)(2,1)S(1)} %get-tuple-element.22), channel_id=1, source_target_pairs={{0,1},{1,0},{2,3},{3,2},{4,5},{5,4},{6,7},{7,6},{8,9},{9,8},{10,11... | collective-permute-start | bytes 688136 | tf_op jit(solution)/shard_map/ppermute | solution.py:355
  25.9 0.0 collective-permute-done.2.theirs
  25.9 0.0 copy-done
  25.9 0.5 shard_map.69
  26.5 0.6 collective-permute-done.3.got
  27.0 0.9 shard_map.70
  27.9 8.6 %all-to-all-start = ((bf16[32,68,128]{2,1,0:T(8,128)(2,1)}), bf16[32,68,128]{2,1,0:T(8,128)(2,1)S(1)}, u32[]{:S(2)}, u32[]{:S(2)}) async-start(bf16[32,68,128]{2,1,0:T(8,128)(2,1)} %shard_map.70), calls=%async_computation | async-start | bytes 1179648 | tf_op jit(solution)/shard_map/all_to_all | solution.py:294
  36.6 17.6 %all-to-all-done = bf16[32,68,128]{2,1,0:T(8,128)(2,1)S(1)} async-done(((bf16[32,68,128]{2,1,0:T(8,128)(2,1)}), bf16[32,68,128]{2,1,0:T(8,128)(2,1)S(1)}, u32[]{:S(2)}, u32[]{:S(2)}) %all-to-all-start) | async-done | bytes 557088 | tf_op jit(solution)/shard_map/all_to_all | solution.py:294
  54.2 0.1 convert_reduce_fusion
  54.4 18.7 %all_to_all.15 = bf16[16,32,128]{2,1,0:T(8,128)(2,1)S(1)} all-to-all(bf16[16,32,128]{2,1,0:T(8,128)(2,1)S(1)} %fusion.1), channel_id=1, replica_groups=mesh['sample'=32,'space'=16] {'space'}, dimensions={0} | all-to-all | bytes 262144 | tf_op jit(solution)/shard_map/all_to_all | solution.py:294
  73.2 0.1 reduce_sum.29
  73.4 0.9 broadcast_in_dim.45
  74.3 4.5 %all-to-all-start.2 = ((bf16[32,68,128]{2,1,0:T(8,128)(2,1)}), bf16[32,68,128]{2,1,0:T(8,128)(2,1)S(1)}, u32[]{:S(2)}, u32[]{:S(2)}) async-start(bf16[32,68,128]{2,1,0:T(8,128)(2,1)} %broadcast_in_dim.45), calls=%async_computation.2 | async-start | bytes 1179648 | tf_op jit(solution)/shard_map/all_to_all | solution.py:294
  78.8 0.9 copy.40
  79.7 17.6 %all-to-all-done.2.chunks = bf16[32,68,128]{2,1,0:T(8,128)(2,1)S(1)} async-done(((bf16[32,68,128]{2,1,0:T(8,128)(2,1)}), bf16[32,68,128]{2,1,0:T(8,128)(2,1)S(1)}, u32[]{:S(2)}, u32[]{:S(2)}) %all-to-all-start.2) | async-done | bytes 557088 | tf_op jit(solution)/shard_map/all_to_all | solution.py:294
  97.3 1.2 %shard_map.71 = (bf16[27,64,128]{2,1,0:T(8,128)(2,1)}, bf16[27,16,128]{2,1,0:T(8,128)(2,1)}) custom-call(bf16[32,68,128]{2,1,0:T(8,128)(2,1)S(1)} %all-to-all-done.2.chunks), custom_call_target="tpu_custom_call" | custom-call | flops 40000000 | bytes 1200000 | tf_op jit(solution)/shard_map/pallas_call | solution.py:399
  (17 shorter events, 0.2 us)
Async XLA Ops:
  0.6 14.2 %copy-start.1 = (bf16[27,128,256]{2,1,0:T(8,128)(2,1)S(1)}, bf16[27,128,256]{2,1,0:T(8,128)(2,1)}, u32[]{:S(2)}) copy-start(bf16[27,128,256]{2,1,0:T(8,128)(2,1)} %param.7) | copy-start | bytes 5308420
  2.5 10.1 %collective-permute-start.1 = (bf16[1088,128]{1,0:T(8,128)(2,1)S(1)}, bf16[1088,128]{1,0:T(8,128)(2,1)S(1)}, u32[]{:S(2)}, u32[]{:S(2)}) collective-permute-start(bf16[1088,128]{1,0:T(8,128)(2,1)S(1)} %pad_maximum_fusion.own), channel_id=1, source_target_pairs={{0,15},{1,0},{2,1},{3,2},{4,3},{5,4},{6,5},{7,6},{8,7},{9,8},{10,9... | collective-permute-start | bytes 835592 | tf_op jit(solution)/shard_map/ppermute | solution.py:311
  9.4 5.4 %collective-permute-start = (bf16[1088,128]{1,0:T(8,128)(2,1)S(1)}, bf16[1088,128]{1,0:T(8,128)(2,1)S(1)}, u32[]{:S(2)}, u32[]{:S(2)}) collective-permute-start(bf16[1088,128]{1,0:T(8,128)(2,1)S(1)} %pad_maximum_fusion.own), channel_id=1, source_target_pairs={{0,1},{1,2},{2,3},{3,4},{4,5},{5,6},{6,7},{7,8},{8,9},{9,10},{10,1... | collective-permute-start | bytes 835592 | tf_op jit(solution)/shard_map/ppermute | solution.py:312
  17.2 8.7 %collective-permute-start.2 = (bf16[64,896]{1,0:T(8,128)(2,1)S(1)}, bf16[64,896]{1,0:T(8,128)(2,1)S(1)}, u32[]{:S(2)}, u32[]{:S(2)}) collective-permute-start(bf16[64,896]{1,0:T(8,128)(2,1)S(1)} %get-tuple-element.15), channel_id=1, source_target_pairs={{0,2},{1,3},{2,0},{3,1},{4,6},{5,7},{6,4},{7,5},{8,10},{9,11},{10,... | collective-permute-start | bytes 344072 | tf_op jit(solution)/shard_map/ppermute | solution.py:344
  19.1 6.8 %copy-start = (bf16[27,64,128]{2,1,0:T(8,128)(2,1)S(1)}, bf16[27,64,128]{2,1,0:T(8,128)(2,1)}, u32[]{:S(2)}) copy-start(bf16[27,64,128]{2,1,0:T(8,128)(2,1)} %first_weight.1) | copy-start | bytes 1327108
  21.2 5.9 %collective-permute-start.3 = (bf16[32,28,128]{2,1,0:T(8,128)(2,1)S(1)}, bf16[32,28,128]{2,1,0:T(8,128)(2,1)S(1)}, u32[]{:S(2)}, u32[]{:S(2)}) collective-permute-start(bf16[32,28,128]{2,1,0:T(8,128)(2,1)S(1)} %get-tuple-element.22), channel_id=1, source_target_pairs={{0,1},{1,0},{2,3},{3,2},{4,5},{5,4},{6,7},{7,6},{8,9},{9,8},{10,11... | collective-permute-start | bytes 688136 | tf_op jit(solution)/shard_map/ppermute | solution.py:355
  27.9 26.2 %all-to-all-start = ((bf16[32,68,128]{2,1,0:T(8,128)(2,1)}), bf16[32,68,128]{2,1,0:T(8,128)(2,1)S(1)}, u32[]{:S(2)}, u32[]{:S(2)}) async-start(bf16[32,68,128]{2,1,0:T(8,128)(2,1)} %shard_map.70), calls=%async_computation | async-start | bytes 1179648 | tf_op jit(solution)/shard_map/all_to_all | solution.py:294
  74.3 23.0 %all-to-all-start.2 = ((bf16[32,68,128]{2,1,0:T(8,128)(2,1)}), bf16[32,68,128]{2,1,0:T(8,128)(2,1)S(1)}, u32[]{:S(2)}, u32[]{:S(2)}) async-start(bf16[32,68,128]{2,1,0:T(8,128)(2,1)} %broadcast_in_dim.45), calls=%async_computation.2 | async-start | bytes 1179648 | tf_op jit(solution)/shard_map/all_to_all | solution.py:294

commit v10 on v9

--- a/solution.py
+++ b/solution.py
@@ -255,8 +255,7 @@
     rows = second.shape[1]
     for m in range(kept.shape[0]):
         payload_ref[m, :rows, :] = second[m]
-        total = kept[m].astype(F32) + got[m].astype(F32)
-        payload_ref[m, rows:, :] = total.astype(BF)
+        payload_ref[m, rows:, :] = kept[m] + got[m]
 
 
 def final_kernel(chunks, first_ref, second_ref):

time: 99 us -> 99 us (level)
  no operation moved by 1% of the time
where the time goes in v10:
time: 99 us; the launch traced here: 98.5 us
  waiting for transfers between devices  38 us (38%)
  starting transfers between devices  28.5 us (29%)
  blocking collectives  18.7 us (19%)
  Pallas kernels  7.03 us (7%)
  local copies, waits for them, and re-layouts  4.27 us (4%)
  other arithmetic  1.06 us (1%)
    all_to_all x2, waiting for transfers between devices, exchanged(): return lax.all_to_all(parts, axis, split_axis=0, concat_axis=0, tiled=True)  35.2 us
    all_to_all x1, blocking collectives, exchanged(): return lax.all_to_all(parts, axis, split_axis=0, concat_axis=0, tiled=True)  18.7 us
    all_to_all x2, starting transfers between devices, exchanged(): return lax.all_to_all(parts, axis, split_axis=0, concat_axis=0, tiled=True)  13.1 us
    ppermute x1, starting transfers between devices, shards(): lax.ppermute(own, 'space', [(i, (i - 1) % groups) for i in range(groups)])  6.89 us
    ppermute x1, starting transfers between devices, shards(): got = lax.ppermute(sent, 'space', [(i, i ^ 1) for i in range(groups)])  4.74 us
    pallas_call x1, Pallas kernels, shards(): pl.pallas_call(forward_kernel, out_shape=(jax.ShapeDtypeStruct((3, chan_m...  2.32 us
    ppermute x1, waiting for transfers between devices, shards(): below = lax.ppermute(own, 'space', [(i, i + 1) for i in range(groups - 1)])  2.21 us
    pallas_call x1, Pallas kernels, shards(): pl.pallas_call(backward_kernel, out_shape=(jax.ShapeDtypeStruct((3, 3 * c...  2.04 us
  transfers between devices with their start and end apart: 6, of which 4 were waited for; matrix products, arithmetic and copies ran while one was open for 2% of the time, Pallas kernels for 3%

profile of v10, /device:TPU:1, one launch (start us, length us, event | category | flops | bytes accessed | tf_op | source)
XLA Modules:
  0.0 98.5 jit_solution(8752377045994003147)
XLA Ops:
  0.6 0.0 copy-start.1
  0.6 1.1 %copy.33 = bf16[4,4,64,128]{3,2,1,0:T(8,128)(2,1)S(1)} copy(bf16[4,4,64,128]{3,1,0,2:T(4,128)(2,1)} %bitcast.36) | data formatting | bytes 524288 | tf_op jit(solution)/shard_map/transpose | solution.py:307
  1.8 0.7 pad_maximum_fusion.own
  2.5 6.9 %collective-permute-start.1 = (bf16[1088,128]{1,0:T(8,128)(2,1)S(1)}, bf16[1088,128]{1,0:T(8,128)(2,1)S(1)}, u32[]{:S(2)}, u32[]{:S(2)}) collective-permute-start(bf16[1088,128]{1,0:T(8,128)(2,1)S(1)} %pad_maximum_fusion.own), channel_id=1, source_target_pairs={{0,15},{1,0},{2,1},{3,2},{4,3},{5,4},{6,5},{7,6},{8,7},{9,8},{10,9... | collective-permute-start | bytes 835592 | tf_op jit(solution)/shard_map/ppermute | solution.py:310
  9.4 1.9 %collective-permute-start = (bf16[1088,128]{1,0:T(8,128)(2,1)S(1)}, bf16[1088,128]{1,0:T(8,128)(2,1)S(1)}, u32[]{:S(2)}, u32[]{:S(2)}) collective-permute-start(bf16[1088,128]{1,0:T(8,128)(2,1)S(1)} %pad_maximum_fusion.own), channel_id=1, source_target_pairs={{0,1},{1,2},{2,3},{3,4},{4,5},{5,6},{6,7},{7,8},{8,9},{9,10},{10,1... | collective-permute-start | bytes 835592 | tf_op jit(solution)/shard_map/ppermute | solution.py:311
  11.4 1.2 %copy.34 = bf16[1728,128]{0,1:T(8,128)(2,1)S(1)} copy(bf16[1728,128]{1,0:T(8,128)(2,1)} %bitcast.30) | data formatting | bytes 884736 | tf_op jit(solution)/shard_map/reshape | solution.py:312
  12.6 0.0 collective-permute-done.1.above
  12.6 2.2 %collective-permute-done.below = bf16[1088,128]{1,0:T(8,128)(2,1)S(1)} collective-permute-done((bf16[1088,128]{1,0:T(8,128)(2,1)S(1)}, bf16[1088,128]{1,0:T(8,128)(2,1)S(1)}, u32[]{:S(2)}, u32[]{:S(2)}) %collective-permute-start) | collective-permute-done | bytes 278560 | tf_op jit(solution)/shard_map/ppermute | solution.py:311
  14.8 0.0 copy-done.1
  14.8 2.3 %shard_map.67 = (f32[3,128,128]{2,1,0:T(8,128)S(1)}, bf16[256,64]{1,0:T(8,128)(2,1)S(1)}, bf16[64,896]{1,0:T(8,128)(2,1)S(1)}, bf16[64,896]{1,0:T(8,128)(2,1)S(1)}) custom-call(s32[3]{0:T(128)S(1)} %compare_select_fusion.1.scalars, bf16[1088,128]{1,0:T(8,128)(2,1)S(1)} %collective-permute-done.below, bf16[1088,128]{1,0:T(8,128)(2,1)S(1)} %pad_maximum_fusion.own, ...), custom_call_target="tpu_custom_call" | custom-call | flops 2000000000 | bytes 5000000 | tf_op jit(solution)/shard_map/pallas_call | solution.py:325
  17.2 1.9 %collective-permute-start.2 = (bf16[64,896]{1,0:T(8,128)(2,1)S(1)}, bf16[64,896]{1,0:T(8,128)(2,1)S(1)}, u32[]{:S(2)}, u32[]{:S(2)}) collective-permute-start(bf16[64,896]{1,0:T(8,128)(2,1)S(1)} %get-tuple-element.15), channel_id=1, source_target_pairs={{0,2},{1,3},{2,0},{3,1},{4,6},{5,7},{6,4},{7,5},{8,10},{9,11},{10,... | collective-permute-start | bytes 344072 | tf_op jit(solution)/shard_map/ppermute | solution.py:343
  19.1 0.0 copy-start
  19.1 2.0 %shard_map.68 = (bf16[3,384,256]{2,1,0:T(8,128)(2,1)S(1)}, bf16[32,28,128]{2,1,0:T(8,128)(2,1)S(1)}, bf16[32,28,128]{2,1,0:T(8,128)(2,1)S(1)}) custom-call(s32[3]{0:T(128)S(1)} %compare_select_fusion.1.scalars, bf16[1088,128]{1,0:T(8,128)(2,1)S(1)} %collective-permute-done.below, bf16[1088,128]{1,0:T(8,128)(2,1)S(1)} %pad_maximum_fusion.own, ...), custom_call_target="tpu_custom_call" | custom-call | flops 3000000000 | bytes 5000000 | tf_op jit(solution)/shard_map/pallas_call | solution.py:344
  21.2 4.7 %collective-permute-start.3 = (bf16[32,28,128]{2,1,0:T(8,128)(2,1)S(1)}, bf16[32,28,128]{2,1,0:T(8,128)(2,1)S(1)}, u32[]{:S(2)}, u32[]{:S(2)}) collective-permute-start(bf16[32,28,128]{2,1,0:T(8,128)(2,1)S(1)} %get-tuple-element.22), channel_id=1, source_target_pairs={{0,1},{1,0},{2,3},{3,2},{4,5},{5,4},{6,7},{7,6},{8,9},{9,8},{10,11... | collective-permute-start | bytes 688136 | tf_op jit(solution)/shard_map/ppermute | solution.py:354
  25.9 0.0 collective-permute-done.2.theirs
  25.9 0.0 copy-done
  25.9 0.5 shard_map.69
  26.5 0.6 collective-permute-done.3.got
  27.0 0.9 shard_map.70
  28.0 8.6 %all-to-all-start = ((bf16[32,68,128]{2,1,0:T(8,128)(2,1)}), bf16[32,68,128]{2,1,0:T(8,128)(2,1)S(1)}, u32[]{:S(2)}, u32[]{:S(2)}) async-start(bf16[32,68,128]{2,1,0:T(8,128)(2,1)} %shard_map.70), calls=%async_computation | async-start | bytes 1179648 | tf_op jit(solution)/shard_map/all_to_all | solution.py:293
  36.6 17.6 %all-to-all-done = bf16[32,68,128]{2,1,0:T(8,128)(2,1)S(1)} async-done(((bf16[32,68,128]{2,1,0:T(8,128)(2,1)}), bf16[32,68,128]{2,1,0:T(8,128)(2,1)S(1)}, u32[]{:S(2)}, u32[]{:S(2)}) %all-to-all-start) | async-done | bytes 557088 | tf_op jit(solution)/shard_map/all_to_all | solution.py:293
  54.2 0.1 convert_reduce_fusion
  54.4 18.7 %all_to_all.15 = bf16[16,32,128]{2,1,0:T(8,128)(2,1)S(1)} all-to-all(bf16[16,32,128]{2,1,0:T(8,128)(2,1)S(1)} %fusion.1), channel_id=1, replica_groups=mesh['sample'=32,'space'=16] {'space'}, dimensions={0} | all-to-all | bytes 262144 | tf_op jit(solution)/shard_map/all_to_all | solution.py:293
  73.2 0.1 reduce_sum.29
  73.4 0.9 broadcast_in_dim.45
  74.3 4.5 %all-to-all-start.2 = ((bf16[32,68,128]{2,1,0:T(8,128)(2,1)}), bf16[32,68,128]{2,1,0:T(8,128)(2,1)S(1)}, u32[]{:S(2)}, u32[]{:S(2)}) async-start(bf16[32,68,128]{2,1,0:T(8,128)(2,1)} %broadcast_in_dim.45), calls=%async_computation.2 | async-start | bytes 1179648 | tf_op jit(solution)/shard_map/all_to_all | solution.py:293
  78.8 0.9 copy.40
  79.7 17.6 %all-to-all-done.2.chunks = bf16[32,68,128]{2,1,0:T(8,128)(2,1)S(1)} async-done(((bf16[32,68,128]{2,1,0:T(8,128)(2,1)}), bf16[32,68,128]{2,1,0:T(8,128)(2,1)S(1)}, u32[]{:S(2)}, u32[]{:S(2)}) %all-to-all-start.2) | async-done | bytes 557088 | tf_op jit(solution)/shard_map/all_to_all | solution.py:293
  97.3 1.2 %shard_map.71 = (bf16[27,64,128]{2,1,0:T(8,128)(2,1)}, bf16[27,16,128]{2,1,0:T(8,128)(2,1)}) custom-call(bf16[32,68,128]{2,1,0:T(8,128)(2,1)S(1)} %all-to-all-done.2.chunks), custom_call_target="tpu_custom_call" | custom-call | flops 40000000 | bytes 1200000 | tf_op jit(solution)/shard_map/pallas_call | solution.py:398
  (17 shorter events, 0.2 us)
Async XLA Ops:
  0.6 14.2 %copy-start.1 = (bf16[27,128,256]{2,1,0:T(8,128)(2,1)S(1)}, bf16[27,128,256]{2,1,0:T(8,128)(2,1)}, u32[]{:S(2)}) copy-start(bf16[27,128,256]{2,1,0:T(8,128)(2,1)} %param.7) | copy-start | bytes 5308420
  2.5 10.1 %collective-permute-start.1 = (bf16[1088,128]{1,0:T(8,128)(2,1)S(1)}, bf16[1088,128]{1,0:T(8,128)(2,1)S(1)}, u32[]{:S(2)}, u32[]{:S(2)}) collective-permute-start(bf16[1088,128]{1,0:T(8,128)(2,1)S(1)} %pad_maximum_fusion.own), channel_id=1, source_target_pairs={{0,15},{1,0},{2,1},{3,2},{4,3},{5,4},{6,5},{7,6},{8,7},{9,8},{10,9... | collective-permute-start | bytes 835592 | tf_op jit(solution)/shard_map/ppermute | solution.py:310
  9.4 5.4 %collective-permute-start = (bf16[1088,128]{1,0:T(8,128)(2,1)S(1)}, bf16[1088,128]{1,0:T(8,128)(2,1)S(1)}, u32[]{:S(2)}, u32[]{:S(2)}) collective-permute-start(bf16[1088,128]{1,0:T(8,128)(2,1)S(1)} %pad_maximum_fusion.own), channel_id=1, source_target_pairs={{0,1},{1,2},{2,3},{3,4},{4,5},{5,6},{6,7},{7,8},{8,9},{9,10},{10,1... | collective-permute-start | bytes 835592 | tf_op jit(solution)/shard_map/ppermute | solution.py:311
  17.2 8.7 %collective-permute-start.2 = (bf16[64,896]{1,0:T(8,128)(2,1)S(1)}, bf16[64,896]{1,0:T(8,128)(2,1)S(1)}, u32[]{:S(2)}, u32[]{:S(2)}) collective-permute-start(bf16[64,896]{1,0:T(8,128)(2,1)S(1)} %get-tuple-element.15), channel_id=1, source_target_pairs={{0,2},{1,3},{2,0},{3,1},{4,6},{5,7},{6,4},{7,5},{8,10},{9,11},{10,... | collective-permute-start | bytes 344072 | tf_op jit(solution)/shard_map/ppermute | solution.py:343
  19.1 6.8 %copy-start = (bf16[27,64,128]{2,1,0:T(8,128)(2,1)S(1)}, bf16[27,64,128]{2,1,0:T(8,128)(2,1)}, u32[]{:S(2)}) copy-start(bf16[27,64,128]{2,1,0:T(8,128)(2,1)} %first_weight.1) | copy-start | bytes 1327108
  21.2 5.9 %collective-permute-start.3 = (bf16[32,28,128]{2,1,0:T(8,128)(2,1)S(1)}, bf16[32,28,128]{2,1,0:T(8,128)(2,1)S(1)}, u32[]{:S(2)}, u32[]{:S(2)}) collective-permute-start(bf16[32,28,128]{2,1,0:T(8,128)(2,1)S(1)} %get-tuple-element.22), channel_id=1, source_target_pairs={{0,1},{1,0},{2,3},{3,2},{4,5},{5,4},{6,7},{7,6},{8,9},{9,8},{10,11... | collective-permute-start | bytes 688136 | tf_op jit(solution)/shard_map/ppermute | solution.py:354
  28.0 26.2 %all-to-all-start = ((bf16[32,68,128]{2,1,0:T(8,128)(2,1)}), bf16[32,68,128]{2,1,0:T(8,128)(2,1)S(1)}, u32[]{:S(2)}, u32[]{:S(2)}) async-start(bf16[32,68,128]{2,1,0:T(8,128)(2,1)} %shard_map.70), calls=%async_computation | async-start | bytes 1179648 | tf_op jit(solution)/shard_map/all_to_all | solution.py:293
  74.3 23.0 %all-to-all-start.2 = ((bf16[32,68,128]{2,1,0:T(8,128)(2,1)}), bf16[32,68,128]{2,1,0:T(8,128)(2,1)S(1)}, u32[]{:S(2)}, u32[]{:S(2)}) async-start(bf16[32,68,128]{2,1,0:T(8,128)(2,1)} %broadcast_in_dim.45), calls=%async_computation.2 | async-start | bytes 1179648 | tf_op jit(solution)/shard_map/all_to_all | solution.py:293
